TPU v7x, 256 devices: a whole 4x4x8 slice. The times are simulated.
256 devices in a mesh: member: 8 (over y, x_hi), space: 32 (over z, x_lo, core).
Axes of the slice: x: 4 (x_hi: 2, x_lo: 2; x = x_hi * 2 + x_lo), y: 4, z: 8, core: 2. Of those that a mesh axis runs over, the one named last changes fastest.
Arguments:
- zonal_wind: bfloat16 [48, 256, 256, 128], P('member', 'space'), may hold values from -6 to 6
- meridional_wind: bfloat16 [48, 256, 256, 128], P('member', 'space'), may hold values from -6 to 6
- heat_anomaly: bfloat16 [48, 256, 256, 128], P('member', 'space'), may hold values from -6 to 6
- moisture_anomaly: bfloat16 [48, 256, 256, 128], P('member', 'space'), may hold values from -6 to 6
- projection_scale: float32 [256, 256], P('space'), may hold values from 0.5 to 2
- balance_multiplier: float32 [256, 256], P('space'), may hold values from -4 to 4
- heat_on_curl_slope: float32 [128], replicated, may hold values from 0.3 to 1.5
- moisture_on_heat_slope: float32 [128], replicated, may hold values from 0.3 to 1.5
Outputs:
- covariance: float32 [32, 512, 512], P('space', 'member')
All inputs are finite; a program needn't handle non-finite values.
Results may differ from a plain program's by a relative error of at most 0.0009.
Values may be sent and summed in bfloat16 or wider, within the bound.
No kernel may reach another device: no remote copies, remote signals or barrier semaphores. Data moves between devices by JAX's collectives and lax.ppermute only.
A program may use at most 128 MiB of HBM per device.

v0:
```python
import jax
import jax.numpy as jnp
from jax import lax
from jax.sharding import PartitionSpec as P


def extended(block, sides, width):
    for axis, dim in sides:
        count = lax.axis_size(axis)
        forward = [(i, i + 1) for i in range(count - 1)]
        backward = [(target, source) for source, target in forward]
        low = lax.ppermute(
            lax.slice_in_dim(block, block.shape[dim] - width, None, axis=dim), axis, forward
        )
        high = lax.ppermute(lax.slice_in_dim(block, 0, width, axis=dim), axis, backward)
        block = jnp.concatenate([low, block, high], axis=dim)
    return block


def lat_diff(padded):
    return (-padded[:, 4:] + 8.0 * padded[:, 3:-1] - 8.0 * padded[:, 1:-3] + padded[:, :-4]) / 12.0


def lon_diff(field):
    return (jnp.roll(field, -1, 2) - jnp.roll(field, 1, 2)) / 2.0


def gram_rows(left, right, precision):
    return lax.dot_general(
        left,
        right,
        (((0,), (0,)), ((), ())),
        preferred_element_type=jnp.float32,
        precision=precision,
    )


def on_device(
    zonal_wind,
    meridional_wind,
    heat_anomaly,
    moisture_anomaly,
    projection_scale,
    balance_multiplier,
    heat_on_curl_slope,
    moisture_on_heat_slope,
):
    winds = jnp.stack([zonal_wind, meridional_wind])
    padded = extended(winds, (("space", 2),), 2)
    u_full = padded[0].astype(jnp.float32)
    v_full = padded[1].astype(jnp.float32)
    u_mid = u_full[:, 2:-2]
    v_mid = v_full[:, 2:-2]
    factor = projection_scale[None, :, :, None]
    wind_curl = factor * (lon_diff(v_mid) - lat_diff(u_full))
    wind_spreading = factor * (lon_diff(u_mid) + lat_diff(v_full))
    heat_residual = (
        heat_anomaly.astype(jnp.float32)
        - heat_on_curl_slope * balance_multiplier[None, :, :, None] * wind_curl
    )
    moisture_residual = (
        moisture_anomaly.astype(jnp.float32) - moisture_on_heat_slope * heat_residual
    )
    sample_vector = jnp.concatenate(
        [wind_curl, wind_spreading, heat_residual, moisture_residual], axis=3
    ).astype(jnp.bfloat16)
    width = sample_vector.shape[3]
    groups = lax.axis_size("member")
    members_all = float(sample_vector.shape[0] * groups)
    rows = width // groups
    scale = 1.0 / (
        (sample_vector.shape[0] * groups - 1) * sample_vector.shape[1] * sample_vector.shape[2]
    )
    local_sum = jnp.sum(sample_vector.astype(jnp.float32), axis=0)
    highest = lax.Precision.HIGHEST
    totals = lax.psum(local_sum.astype(jnp.bfloat16), "member").astype(jnp.float32)
    ens_mean = totals / members_all
    anomaly = (sample_vector.astype(jnp.float32) - ens_mean[None]).reshape(-1, width)
    summed = lax.psum(gram_rows(anomaly, anomaly, highest), "member")
    mine = lax.dynamic_slice_in_dim(summed, lax.axis_index("member") * rows, rows, 0)
    return (mine * scale)[None]


def solution(mesh):
    placed = (
        P("member", "space", None, None),
        P("member", "space", None, None),
        P("member", "space", None, None),
        P("member", "space", None, None),
        P("space", None),
        P("space", None),
        P(),
        P(),
    )
    return jax.shard_map(
        on_device, mesh=mesh, in_specs=placed, out_specs=P("space", "member", None), check_vma=False
    )
```

profile of v0, /device:TPU:2, one launch (start us, length us, event | category | flops | bytes accessed | tf_op | source)
XLA Modules:
  0.0 396.8 jit_solution(15187263086016481652)
XLA Ops:
  6.5 2.3 pad_maximum_fusion.4
  8.8 2.1 collective-permute-start
  10.9 3.6 collective-permute-start.1
  14.6 1.3 broadcast_multiply_fusion
  15.9 31.6 %collective-permute-done = bf16[2,6,2,256,128]{4,3,2,1,0:T(8,128)(2,1)S(1)} collective-permute-done((bf16[2,6,2,256,128]{4,3,2,1,0:T(8,128)(2,1)S(1)}, bf16[2,6,2,256,128]{4,3,2,1,0:T(8,128)(2,1)S(1)}, u32[]{:S(2)}, u32[]{:S(2)}) %collective-permute-start) | collective-permute-done | bytes 1572896 | tf_op jit(solution)/shard_map/ppermute | solution.py:12
  47.5 0.0 collective-permute-done.1
  47.6 4.4 %pad_maximum_fusion.1 = bf16[2,6,12,256,128]{4,3,2,1,0:T(8,128)(2,1)} fusion(bf16[2,6,2,256,128]{4,3,2,1,0:T(8,128)(2,1)S(1)} %collective-permute-done.1, bf16[1,6,8,256,128]{4,3,2,1,0:T(8,128)(2,1)S(1)} %bitcast.21, bf16[1,6,8,256,128]{4,3,2,1,0:T(8,128)(2,1)S(1)} %bitcast.23, bf16[2,6,2,256,128]{4,3,2,1,0:T(8,128)(2,1)S(1)} %collective-permute-done), kind=kLoop, calls=%fused_computation.5 | loop fusion | flops 14155776 | bytes 18874368 | tf_op jit(solution)/shard_map/concatenate | solution.py:16
  52.0 12.8 %fusion.18 = (f32[6,12,256,128]{3,2,1,0:T(8,128)}, f32[6,12,256,128]{3,2,1,0:T(8,128)}) fusion(bf16[2,6,12,256,128]{4,3,2,1,0:T(8,128)(2,1)} %pad_maximum_fusion.1), kind=kLoop, calls=%fused_computation.34 | loop fusion | flops 4718592 | bytes 28311552 | tf_op jit(solution)/shard_map/convert_element_type | solution.py:51
  64.8 1.3 fusion.27
  66.1 0.0 copy-start.8
  66.1 15.6 %fusion.28 = (f32[6,8,255,128]{3,2,1,0:T(8,128)S(1)}, f32[6,8,255,128]{3,2,1,0:T(8,128)}, f32[6,8,255,128]{3,2,1,0:T(8,128)}, f32[6,8,255,128]{3,2,1,0:T(8,128)}) fusion(f32[6,12,256,128]{3,2,1,0:T(8,128)} %get-tuple-element.18, f32[6,12,256,128]{3,2,1,0:T(8,128)} %get-tuple-element.17), kind=kLoop, calls=%fused_computation.46 | loop fusion | bytes 50135040 | tf_op jit(solution)/shard_map/jit(_roll_static)/slice | solution.py:25
  81.8 27.2 %fusion.25 = (bf16[6,8,256,128]{3,2,1,0:T(8,128)(2,1)S(1)}, f32[6,8,256,128]{3,2,1,0:T(8,128)}, bf16[6,8,256,128]{3,2,1,0:T(8,128)(2,1)}) fusion(f32[6,12,256,128]{3,2,1,0:T(8,128)} %get-tuple-element.18, f32[6,8,255,128]{3,2,1,0:T(8,128)} %get-tuple-element.24, f32[6,8,1,128]{3,2,1,0:T(1,128)S(1)} %get-tuple-element.22, ...), kind=kLoop, calls=%fused_computation.44 | loop fusion | flops 44040192 | bytes 88088576 | tf_op jit(solution)/shard_map/convert.3
  109.0 9.8 %fusion.19 = (bf16[6,8,256,128]{3,2,1,0:T(8,128)(2,1)S(1)}, bf16[6,8,256,128]{3,2,1,0:T(8,128)(2,1)}) fusion(f32[6,8,256,128]{3,2,1,0:T(8,128)} %get-tuple-element.6, bf16[6,8,256,128]{3,2,1,0:T(8,128)(2,1)} %param.10, f32[8,256,128]{2,1,0:T(8,128)} %broadcast_multiply_fusion, f32[128]{0:T(128)S(1)} %copy-done.10, bf16[6,8,256,128]{3,2,1,0:T(8,128)(2,1)} %param.11), kind=kLoop, calls=%fused_computation.36 | loop fusion | flops 12582912 | bytes 19923456 | tf_op jit(solution)/shard_map/convert.5
  118.8 1.7 copy-done.6
  120.5 8.1 %fusion.20 = bf16[8,256,512]{2,1,0:T(8,128)(2,1)} fusion(bf16[6,8,256,128]{3,2,1,0:T(8,128)(2,1)} %get-tuple-element.8, bf16[6,8,256,128]{3,2,1,0:T(8,128)(2,1)S(1)} %get-tuple-element.7, bf16[6,8,256,128]{3,2,1,0:T(8,128)(2,1)S(1)} %copy-done.2, bf16[6,8,256,128]{3,2,1,0:T(8,128)(2,1)S(1)} %get-tuple-element.5), kind=kLoop, calls=%fused_computation.37 | loop fusion | flops 55574528 | bytes 14680064 | tf_op jit(solution)/shard_map/reduce_sum | solution.py:74
  128.5 0.0 all-reduce.3.cloned.1.call-update
  128.6 0.2 all-reduce.5.cloned.1.call-start
  128.8 115.3 %all-reduce.3.cloned.1.call-done = bf16[8,256,512]{2,1,0:T(8,128)(2,1)} async-done(((bf16[8,256,512]{2,1,0:T(8,128)(2,1)}), bf16[8,256,512]{2,1,0:T(8,128)(2,1)}) %all-reduce.3.cloned.1.call-update) | async-done | bytes 2097168 | tf_op jit(solution)/shard_map/psum | solution.py:76
  244.1 2.4 convert_multiply_fusion
  246.5 0.1 copy-done.3
  246.7 47.7 %fusion.21 = f32[512,512]{1,0:T(8,128)} fusion(f32[8,256,512]{2,1,0:T(8,128)S(1)} %convert_multiply_fusion, bf16[6,8,256,128]{3,2,1,0:T(8,128)(2,1)} %get-tuple-element.8, bf16[6,8,256,128]{3,2,1,0:T(8,128)(2,1)} %copy-done.6, bf16[6,8,256,128]{3,2,1,0:T(8,128)(2,1)S(1)} %copy-done.3, bf16[6,8,256,128]{3,2,1,0:T(8,128)(2,1)S(1)} %copy-done.1), kind=kOutput, calls=%fused_computation.40 | convolution fusion | flops 38711328768 | bytes 17825792 | tf_op jit(solution)/shard_map/dot_general | solution.py:29
  294.3 0.0 all-reduce.5.cloned.1.call-update
  294.4 94.0 %all-reduce.5.cloned.1.call-done = f32[512,512]{1,0:T(8,128)} async-done(((f32[512,512]{1,0:T(8,128)}), f32[512,512]{1,0:T(8,128)}) %all-reduce.5.cloned.1.call-update) | async-done | bytes 1048592 | tf_op jit(solution)/shard_map/psum | solution.py:79
  388.4 1.6 multiply_bitcast_fusion
  (20 shorter events, 0.0 us)
Async XLA Ops:
  6.5 41.0 %copy-start.4 = (bf16[6,8,256,128]{3,2,1,0:T(8,128)(2,1)S(1)}, bf16[6,8,256,128]{3,2,1,0:T(8,128)(2,1)}, u32[]{:S(2)}) copy-start(bf16[6,8,256,128]{3,2,1,0:T(8,128)(2,1)} %param.9) | copy-start | bytes 9437188
  6.5 8.0 %copy-start.7 = (f32[8,256]{1,0:T(8,128)S(1)}, f32[8,256]{1,0:T(8,128)}, u32[]{:S(2)}) copy-start(f32[8,256]{1,0:T(8,128)} %param.13) | copy-start | bytes 24580
  6.5 8.0 %copy-start.9 = (f32[128]{0:T(128)S(1)}, f32[128]{0:T(128)}, u32[]{:S(2)}) copy-start(f32[128]{0:T(128)} %param.14) | copy-start | bytes 1540
  6.5 237.6 %all-reduce.3.cloned.1.call-start = ((), (), s32[]{:S(2)}) async-start(), calls=%async_computation | async-start | bytes 4194304 | tf_op jit(solution)/shard_map/psum | solution.py:76
  6.5 41.0 %copy-start.5 = (bf16[6,8,256,128]{3,2,1,0:T(8,128)(2,1)S(1)}, bf16[6,8,256,128]{3,2,1,0:T(8,128)(2,1)}, u32[]{:S(2)}) copy-start(bf16[6,8,256,128]{3,2,1,0:T(8,128)(2,1)} %param.8) | copy-start | bytes 9437188
  8.8 38.7 %collective-permute-start = (bf16[2,6,2,256,128]{4,3,2,1,0:T(8,128)(2,1)S(1)}, bf16[2,6,2,256,128]{4,3,2,1,0:T(8,128)(2,1)S(1)}, u32[]{:S(2)}, u32[]{:S(2)}) collective-permute-start(bf16[2,6,2,256,128]{4,3,2,1,0:T(8,128)(2,1)S(1)} %get-tuple-element.19), channel_id=1, source_target_pairs={{0,1},{1,2},{2,3},{3,4},{4,5},{5,6},{6,7},{7,8},{8,9},{9,10},{10,1... | collective-permute-start | bytes 4718600 | tf_op jit(solution)/shard_map/ppermute | solution.py:12
  10.9 36.7 %collective-permute-start.1 = (bf16[2,6,2,256,128]{4,3,2,1,0:T(8,128)(2,1)S(1)}, bf16[2,6,2,256,128]{4,3,2,1,0:T(8,128)(2,1)S(1)}, u32[]{:S(2)}, u32[]{:S(2)}) collective-permute-start(bf16[2,6,2,256,128]{4,3,2,1,0:T(8,128)(2,1)S(1)} %get-tuple-element.20), channel_id=1, source_target_pairs={{1,0},{2,1},{3,2},{4,3},{5,4},{6,5},{7,6},{8,7},{9,8},{10,9},{11,1... | collective-permute-start | bytes 4718600 | tf_op jit(solution)/shard_map/ppermute | solution.py:15
  66.1 15.7 %copy-start.8 = (f32[8,256]{1,0:T(8,128)S(1)}, f32[8,256]{1,0:T(8,128)}, u32[]{:S(2)}) copy-start(f32[8,256]{1,0:T(8,128)} %param.12) | copy-start | bytes 24580
  81.8 27.2 %copy-start.10 = (f32[128]{0:T(128)S(1)}, f32[128]{0:T(128)}, u32[]{:S(2)}) copy-start(f32[128]{0:T(128)} %param.15) | copy-start | bytes 1540
  109.0 9.8 %copy-start = (bf16[6,8,256,128]{3,2,1,0:T(8,128)(2,1)}, bf16[6,8,256,128]{3,2,1,0:T(8,128)(2,1)S(1)}, u32[]{:S(2)}) copy-start(bf16[6,8,256,128]{3,2,1,0:T(8,128)(2,1)S(1)} %get-tuple-element.5) | copy-start | bytes 9437188
  109.0 11.5 %copy-start.2 = (bf16[6,8,256,128]{3,2,1,0:T(8,128)(2,1)S(1)}, bf16[6,8,256,128]{3,2,1,0:T(8,128)(2,1)}, u32[]{:S(2)}) copy-start(bf16[6,8,256,128]{3,2,1,0:T(8,128)(2,1)} %get-tuple-element.21) | copy-start | bytes 9437188
  118.8 1.7 copy-start.6
  128.5 118.0 %copy-start.1 = (bf16[6,8,256,128]{3,2,1,0:T(8,128)(2,1)S(1)}, bf16[6,8,256,128]{3,2,1,0:T(8,128)(2,1)}, u32[]{:S(2)}) copy-start(bf16[6,8,256,128]{3,2,1,0:T(8,128)(2,1)} %copy-done) | copy-start | bytes 9437188
  128.6 259.8 %all-reduce.5.cloned.1.call-start = ((), (), s32[]{:S(2)}) async-start(), calls=%async_computation.1 | async-start | bytes 2097152 | tf_op jit(solution)/shard_map/psum | solution.py:79
  244.1 2.5 copy-start.3
Sparse Core Ops, SparseCore 0:
  128.7 115.4 all-reduce.2
  294.5 93.8 all-reduce.4
where the time goes:
time: 398 us; the launch traced here: 397 us
  waiting for transfers between devices  241 us (61%)
  other arithmetic  69.8 us (18%)
  matrix products  47.7 us (12%)
  local copies, waits for them, and re-layouts  18.8 us (5%)
  between operations  13.5 us (3%)
  starting transfers between devices  5.92 us (1%)
    psum x1, waiting for transfers between devices, on_device(): lax.psum(local_sum.astype(jnp.bfloat16), 'member').astype(jnp.float32)  115 us
    psum x1, waiting for transfers between devices, on_device(): summed = lax.psum(gram_rows(anomaly, anomaly, highest), 'member')  94 us
    dot_general x1, matrix products, gram_rows(): lax.dot_general(left, right, (((0,), (0,)), ((), ())), preferred_element_...  47.7 us
    another operation x2, other arithmetic  37 us
    ppermute x1, waiting for transfers between devices, extended(): lax.ppermute(lax.slice_in_dim(block, block.shape[dim] - width, None, axis...  31.6 us
    slice x2, local copies, waits for them, and re-layouts, lon_diff(): return (jnp.roll(field, -1, 2) - jnp.roll(field, 1, 2)) / 2.0  17 us
    convert_element_type x1, other arithmetic, on_device(): v_full = padded[1].astype(jnp.float32)  12.8 us
    reduce_sum x1, other arithmetic, on_device(): local_sum = jnp.sum(sample_vector.astype(jnp.float32), axis=0)  8.08 us
  transfers between devices with their start and end apart: 4, of which 3 were waited for; matrix products, arithmetic and copies ran while one was open for 0% of the time, Pallas kernels for 0%

commit v1 on v0

v1 whole, which is shorter than its diff:
```python
import functools

import jax
import jax.numpy as jnp
from jax import lax
from jax.experimental import pallas as pl
from jax.experimental.pallas import tpu as pltpu
from jax.sharding import PartitionSpec as P

CHUNK = 32


def gram(a):
    return lax.dot_general(a, a, (((0,), (0,)), ((), ())), preferred_element_type=jnp.float32)


def rows_kernel(
    dims,
    late,
    u_hbm,
    v_hbm,
    h_hbm,
    q_hbm,
    halo_hbm,
    psi_ref,
    bal_ref,
    slopes_ref,
    g_ref,
    m_ref,
    u_ext,
    v_ext,
    h_buf,
    q_buf,
    d_buf,
    psi_b,
    sb_b,
    s_buf,
    sems,
):
    members, parallels, meridians, levels = dims
    core = lax.axis_index("space") % 2
    if late:
        n, own, own_from, own_to, halo_to, row_from = 2, 4, 4 * core, 2 * (1 - core), 4 * core, 6 * core
    else:
        n, own, own_from, own_to = parallels - 2, parallels, 0, 2 * core
        halo_to, row_from = parallels * (1 - core), 2 * (1 - core)

    copies = [
        pltpu.make_async_copy(halo_hbm.at[0], u_ext.at[:, pl.ds(halo_to, 2)], sems.at[0]),
        pltpu.make_async_copy(halo_hbm.at[1], v_ext.at[:, pl.ds(halo_to, 2)], sems.at[1]),
        pltpu.make_async_copy(u_hbm.at[:, pl.ds(own_from, own)], u_ext.at[:, pl.ds(own_to, own)], sems.at[2]),
        pltpu.make_async_copy(v_hbm.at[:, pl.ds(own_from, own)], v_ext.at[:, pl.ds(own_to, own)], sems.at[3]),
        pltpu.make_async_copy(h_hbm.at[:, pl.ds(row_from, n)], h_buf, sems.at[4]),
        pltpu.make_async_copy(q_hbm.at[:, pl.ds(row_from, n)], q_buf, sems.at[5]),
    ]
    for copy in copies:
        copy.start()

    row = lax.broadcasted_iota(jnp.int32, (meridians, meridians), 0)
    col = lax.broadcasted_iota(jnp.int32, (meridians, meridians), 1)
    east = (row + 1) % meridians == col
    west = (row + meridians - 1) % meridians == col
    stencil = jnp.where(east, 6.0, jnp.where(west, -6.0, 0.0)).astype(jnp.bfloat16)
    g_ref[...] = jnp.zeros_like(g_ref)
    slope_t = slopes_ref[0:1, :]
    slope_q = slopes_ref[1:2, :]

    for copy in copies:
        copy.wait()

    @pl.loop(0, n)
    def _(k):
        i = row_from + k
        psi_row = psi_ref[pl.ds(i, 1), :] * (1.0 / 12.0)
        bal_row = bal_ref[pl.ds(i, 1), :]
        psi_b[...] = jnp.transpose(jnp.broadcast_to(psi_row, (levels, meridians)))
        sb_b[...] = jnp.transpose(jnp.broadcast_to(bal_row, (levels, meridians))) * slope_t

        for m in range(members):
            winds = jnp.concatenate([v_ext[m, k + 2], u_ext[m, k + 2]], axis=1)
            d_buf[m] = jnp.dot(stencil, winds, preferred_element_type=jnp.float32)

        @pl.loop(0, meridians // CHUNK)
        def _(c):
            j = pl.multiple_of(c * CHUNK, CHUNK)
            at = pl.ds(j, CHUNK)
            psi = psi_b[at, :]
            sb = sb_b[at, :]
            total = [jnp.zeros((CHUNK, levels), jnp.float32) for _ in range(4)]
            for m in range(members):
                u = [u_ext[m, k + e, at, :].astype(jnp.float32) for e in (0, 1, 3, 4)]
                v = [v_ext[m, k + e, at, :].astype(jnp.float32) for e in (0, 1, 3, 4)]
                du = (u[2] - u[1]) * 8.0 - (u[3] - u[0])
                dv = (v[2] - v[1]) * 8.0 - (v[3] - v[0])
                curl = psi * (d_buf[m, at, 0:levels] - du)
                spread = psi * (d_buf[m, at, levels : 2 * levels] + dv)
                heat = h_buf[m, k, at, :].astype(jnp.float32) - sb * curl
                moist = q_buf[m, k, at, :].astype(jnp.float32) - slope_q * heat
                for f, x in enumerate((curl, spread, heat, moist)):
                    x = x.astype(jnp.bfloat16)
                    s_buf[m, at, f * levels : (f + 1) * levels] = x
                    total[f] = total[f] + x.astype(jnp.float32)
            for f in range(4):
                cut = slice(f * levels, (f + 1) * levels)
                mean = total[f] * (1.0 / members)
                m_ref[c, k, :, cut] = mean.astype(jnp.bfloat16)
                for m in range(members):
                    s_buf[m, at, cut] = (s_buf[m, at, cut].astype(jnp.float32) - mean).astype(jnp.bfloat16)

        g_ref[...] += gram(s_buf[...].reshape(members * meridians, 4 * levels))


def rows_call(dims, late, u, v, h, q, halo, psi, bal, slopes, peers):
    members, parallels, meridians, levels = dims
    n = 2 if late else parallels - 2
    width = 4 * levels
    any_spec = pl.BlockSpec(memory_space=pl.ANY)
    vmem_spec = pl.BlockSpec(memory_space=pltpu.VMEM)
    flops = 2 * n * members * meridians * (width * width + 2 * meridians * levels)
    return pl.pallas_call(
        functools.partial(rows_kernel, dims, late),
        name="late_rows" if late else "early_rows",
        out_shape=(
            jax.ShapeDtypeStruct((width, width), jnp.float32),
            jax.ShapeDtypeStruct((peers, n, CHUNK, width), jnp.bfloat16),
        ),
        in_specs=[any_spec] * 5 + [vmem_spec] * 3,
        out_specs=(vmem_spec, vmem_spec),
        scratch_shapes=[
            pltpu.VMEM((members, n + 4, meridians, levels), jnp.bfloat16),
            pltpu.VMEM((members, n + 4, meridians, levels), jnp.bfloat16),
            pltpu.VMEM((members, n, meridians, levels), jnp.bfloat16),
            pltpu.VMEM((members, n, meridians, levels), jnp.bfloat16),
            pltpu.VMEM((members, meridians, 2 * levels), jnp.float32),
            pltpu.VMEM((meridians, levels), jnp.float32),
            pltpu.VMEM((meridians, levels), jnp.float32),
            pltpu.VMEM((members, meridians, width), jnp.bfloat16),
            pltpu.SemaphoreType.DMA((6,)),
        ],
        compiler_params=pltpu.CompilerParams(vmem_limit_bytes=40 << 20),
        cost_estimate=pl.CostEstimate(flops=flops, bytes_accessed=16 << 20, transcendentals=0),
    )(u, v, h, q, halo, psi, bal, slopes)


def between_kernel(members, early_ref, late_ref, ge_ref, gl_ref, out_ref):
    total = ge_ref[...] + gl_ref[...]
    for part in (early_ref, late_ref):
        means = part[...].astype(jnp.float32)
        peers, n, chunk, width = means.shape
        overall = jnp.sum(means, axis=0, keepdims=True) * (1.0 / peers)
        apart = (means - overall).astype(jnp.bfloat16)
        total = total + gram(apart.reshape(peers * n * chunk, width)) * float(members)
    out_ref[...] = total


def between_call(members, early, late, ge, gl):
    vmem_spec = pl.BlockSpec(memory_space=pltpu.VMEM)
    return pl.pallas_call(
        functools.partial(between_kernel, members),
        name="between",
        out_shape=jax.ShapeDtypeStruct(ge.shape, jnp.float32),
        in_specs=[vmem_spec] * 4,
        out_specs=vmem_spec,
        compiler_params=pltpu.CompilerParams(vmem_limit_bytes=40 << 20),
        cost_estimate=pl.CostEstimate(flops=1 << 30, bytes_accessed=5 << 20, transcendentals=0),
    )(early, late, ge, gl)


def on_device(u, v, h, q, psi, bal, slope_t, slope_q):
    dims = u.shape
    members, parallels = dims[0], dims[1]
    count = lax.axis_size("space")
    peers = lax.axis_size("member")
    core = lax.axis_index("space") % 2
    slopes = jnp.stack([slope_t, slope_q])

    across = [(i, i + 1) for i in range(1, count - 1, 2)]
    across = across + [(b, a) for a, b in across]
    within = [(i, i + 1) for i in range(0, count, 2)]
    within = within + [(b, a) for a, b in within]

    def edge(start):
        return jnp.stack([lax.dynamic_slice_in_dim(x, start, 2, axis=1) for x in (u, v)])

    far = lax.ppermute(edge((parallels - 2) * core), "space", across)
    near = lax.ppermute(edge((parallels - 2) * (1 - core)), "space", within)

    ge, me = rows_call(dims, False, u, v, h, q, near, psi, bal, slopes, peers)
    me = lax.all_to_all(me, "member", 0, 0, tiled=True)
    gl, ml = rows_call(dims, True, u, v, h, q, far, psi, bal, slopes, peers)
    ml = lax.all_to_all(ml, "member", 0, 0, tiled=True)
    total = between_call(members, me, ml, ge, gl)
    width = total.shape[0]
    parts = lax.all_to_all(total.reshape(peers, width // peers, width), "member", 0, 0, tiled=True)
    scale = 1.0 / ((members * peers - 1) * parallels * dims[2])
    return (jnp.sum(parts, axis=0) * scale)[None]


def solution(mesh):
    placed = (P("member", "space", None, None),) * 4 + (P("space", None),) * 2 + (P(), P())
    return jax.shard_map(
        on_device, mesh=mesh, in_specs=placed, out_specs=P("space", "member", None), check_vma=False
    )
```

time: 398 us -> 131 us (0.33)
  waiting for transfers between devices: 241 us -> 36.1 us
  other arithmetic: 69.8 us -> 2.22 us
  matrix products: 47.7 us -> 0 us
  blocking collectives: 0 us -> 43.3 us
  Pallas kernels: 0 us -> 28.9 us
  between operations: 13.5 us -> 0.15 us
  local copies, waits for them, and re-layouts: 18.8 us -> 10.1 us
  starting transfers between devices: 5.92 us -> 10.1 us
    psum x2 -> x0, waiting for transfers between devices: 209 us -> none  [the longest x1 115 us: on_device(): lax.psum(local_sum.astype(jnp.bfloat16), 'member').astype(jnp.float32)]
    dot_general x1 -> x0, matrix products: 47.7 us -> none  [gram_rows(): lax.dot_general(left, right, (((0,), (0,)), ((), ())), preferred_element_...]
    all_to_all x0 -> x2, blocking collectives: none -> 43.3 us  [the longest x1 27.8 us: on_device(): me = lax.all_to_all(me, 'member', 0, 0, tiled=True)]
    another operation x2 -> x3, other arithmetic: 37 us -> 1.47 us  [the longest x2 1.46 us: edge(): jnp.stack([lax.dynamic_slice_in_dim(x, start, 2, axis=1) for x in (u, v)])]
    pallas_call x0 -> x3, Pallas kernels: none -> 28.9 us  [the longest x2 26.3 us: rows_call(): pl.pallas_call(functools.partial(rows_kernel, dims, late), name='late_row...]
    slice x2 -> x0, local copies, waits for them, and re-layouts: 17 us -> none  [lon_diff(): return (jnp.roll(field, -1, 2) - jnp.roll(field, 1, 2)) / 2.0]
    convert_element_type x1 -> x0, other arithmetic: 12.8 us -> none  [on_device(): v_full = padded[1].astype(jnp.float32)]
    reduce_sum x1, other arithmetic: 8.08 us -> 0.08 us  [on_device(): return (jnp.sum(parts, axis=0) * scale)[None]]
  transfers between devices with their start and end apart: 4 -> 3, of which waited for: 3 -> 1; matrix products, arithmetic and copies ran while one was open for 0% -> 1% of each run, Pallas kernels for 0% -> 20%
where the time goes in v1:
time: 131 us
  blocking collectives  43.3 us (33%)
  waiting for transfers between devices  36.1 us (28%)
  Pallas kernels  28.9 us (22%)
  local copies, waits for them, and re-layouts  10.1 us (8%)
  starting transfers between devices  10.1 us (8%)
  other arithmetic  2.22 us (2%)
    ppermute x1, waiting for transfers between devices, on_device(): far = lax.ppermute(edge((parallels - 2) * core), 'space', across)  36.1 us
    all_to_all x1, blocking collectives, on_device(): me = lax.all_to_all(me, 'member', 0, 0, tiled=True)  27.8 us
    pallas_call x2, Pallas kernels, rows_call(): pl.pallas_call(functools.partial(rows_kernel, dims, late), name='late_row...  26.3 us
    all_to_all x1, blocking collectives, on_device(): lax.all_to_all(total.reshape(peers, width // peers, width), 'member', 0,...  15.5 us
    unnamed x30, local copies, waits for them, and re-layouts  7.77 us
    all_to_all x1, starting transfers between devices, on_device(): ml = lax.all_to_all(ml, 'member', 0, 0, tiled=True)  6.04 us
  transfers between devices with their start and end apart: 3, of which 1 were waited for; matrix products, arithmetic and copies ran while one was open for 1% of the time, Pallas kernels for 20%

profile of v1, /device:TPU:2, one launch (start us, length us, event | category | flops | bytes accessed | tf_op | source)
XLA Modules:
  0.0 131.0 jit_solution(8586333302557687524)
XLA Ops:
  0.0 2.3 %dynamic-slice_bitcast_fusion = (bf16[1,6,2,256,128]{4,3,2,1,0:T(8,128)(2,1)S(1)}, bf16[1,6,2,256,128]{4,3,2,1,0:T(8,128)(2,1)S(1)}, bf16[1,6,2,256,128]{4,3,2,1,0:T(8,128)(2,1)S(1)}, bf16[1,6,2,256,128]{4,3,2,1,0:T(8,128)(2,1)S(1)}) fusion(bf16[6,8,256,128]{3,2,1,0:T(8,128)(2,1)} %v_hbm.3, s32[]{:T(128)S(6)} %select_n.17, s32[]{:T(128)S(6)} %select_n.16, ...), kind=kLoop, calls=%fused_computation.2 | loop fusion | bytes 6291464 | tf_op jit(solution)/shard_map/stack | solution.py:183
  2.4 0.0 copy-start.13
  2.4 0.0 copy-start.11
  2.4 0.1 pad_maximum_fusion.1
  2.6 2.1 %collective-permute-start.1 = (bf16[2,6,2,256,128]{4,3,2,1,0:T(8,128)(2,1)S(1)}, bf16[2,6,2,256,128]{4,3,2,1,0:T(8,128)(2,1)S(1)}, u32[]{:S(2)}, u32[]{:S(2)}) collective-permute-start(bf16[2,6,2,256,128]{4,3,2,1,0:T(8,128)(2,1)S(1)} %pad_maximum_fusion.1), channel_id=1, source_target_pairs={{1,2},{3,4},{5,6},{7,8},{9,10},{11,12},{13,14},{15,16},{17,18},{19... | collective-permute-start | bytes 4718600 | tf_op jit(solution)/shard_map/ppermute | solution.py:185
  4.6 0.0 copy-start
  4.6 1.3 %pad_maximum_fusion = bf16[2,6,2,256,128]{4,3,2,1,0:T(8,128)(2,1)} fusion(bf16[1,6,2,256,128]{4,3,2,1,0:T(8,128)(2,1)S(1)} %get-tuple-element.16, bf16[1,6,2,256,128]{4,3,2,1,0:T(8,128)(2,1)S(1)} %get-tuple-element.17), kind=kLoop, calls=%fused_computation | loop fusion | flops 786432 | bytes 3145728 | tf_op jit(solution)/shard_map/stack | solution.py:183
  5.9 2.0 %collective-permute-start = (bf16[2,6,2,256,128]{4,3,2,1,0:T(8,128)(2,1)}, bf16[2,6,2,256,128]{4,3,2,1,0:T(8,128)(2,1)}, u32[]{:S(2)}, u32[]{:S(2)}) collective-permute-start(bf16[2,6,2,256,128]{4,3,2,1,0:T(8,128)(2,1)} %pad_maximum_fusion), channel_id=1, source_target_pairs={{0,1},{2,3},{4,5},{6,7},{8,9},{10,11},{12,13},{14,15},{16,17},{18,... | collective-permute-start | bytes 4718600 | tf_op jit(solution)/shard_map/ppermute | solution.py:186
  8.0 36.1 %collective-permute-done.1.halo_hbm = bf16[2,6,2,256,128]{4,3,2,1,0:T(8,128)(2,1)S(1)} collective-permute-done((bf16[2,6,2,256,128]{4,3,2,1,0:T(8,128)(2,1)S(1)}, bf16[2,6,2,256,128]{4,3,2,1,0:T(8,128)(2,1)S(1)}, u32[]{:S(2)}, u32[]{:S(2)}) %collective-permute-start.1) | collective-permute-done | bytes 1572896 | tf_op jit(solution)/shard_map/ppermute | solution.py:185
  44.1 7.3 %late_rows.1 = (f32[512,512]{1,0:T(8,128)S(1)}, bf16[8,2,32,512]{3,2,1,0:T(8,128)(2,1)S(1)}) custom-call(bf16[6,8,256,128]{3,2,1,0:T(8,128)(2,1)S(1)} %copy-done, bf16[6,8,256,128]{3,2,1,0:T(8,128)(2,1)S(1)} %copy-done.1, bf16[6,8,256,128]{3,2,1,0:T(8,128)(2,1)S(1)} %copy-done.3, bf16[6,8,256,128]{3,2,1,0:T(8,128)(2,1)} %q_hbm.3, ...), custom_call_target="tpu_custom_call" | custom-call | flops 2013265920 | bytes 16777216 | tf_op jit(solution)/shard_map/late_rows/pallas_call | solution.py:120
  51.4 1.0 copy-done.6
  52.4 0.8 copy-done.10
  53.2 6.0 %all-to-all-start.1 = ((bf16[8,2,32,512]{3,2,1,0:T(8,128)(2,1)}), bf16[8,2,32,512]{3,2,1,0:T(8,128)(2,1)}, u32[]{:S(2)}, u32[]{:S(2)}) async-start(bf16[8,2,32,512]{3,2,1,0:T(8,128)(2,1)} %copy-done.10), calls=%async_computation.1 | async-start | bytes 1048576 | tf_op jit(solution)/shard_map/all_to_all | solution.py:191
  59.2 0.0 copy-start.2
  59.2 1.9 %copy-done.2 = bf16[6,8,256,128]{3,2,1,0:T(8,128)(2,1)S(1)} copy-done((bf16[6,8,256,128]{3,2,1,0:T(8,128)(2,1)S(1)}, bf16[6,8,256,128]{3,2,1,0:T(8,128)(2,1)}, u32[]{:S(2)}) %copy-start.2) | copy-done | bytes 3145752
  61.1 1.9 %copy-done.4 = bf16[6,8,256,128]{3,2,1,0:T(8,128)(2,1)S(1)} copy-done((bf16[6,8,256,128]{3,2,1,0:T(8,128)(2,1)S(1)}, bf16[6,8,256,128]{3,2,1,0:T(8,128)(2,1)}, u32[]{:S(2)}) %copy-start.4) | copy-done | bytes 3145752
  63.0 19.1 %early_rows.1 = (f32[512,512]{1,0:T(8,128)S(1)}, bf16[8,6,32,512]{3,2,1,0:T(8,128)(2,1)S(1)}) custom-call(bf16[6,8,256,128]{3,2,1,0:T(8,128)(2,1)S(1)} %copy-done, bf16[6,8,256,128]{3,2,1,0:T(8,128)(2,1)S(1)} %copy-done.2, bf16[6,8,256,128]{3,2,1,0:T(8,128)(2,1)S(1)} %copy-done.4, bf16[6,8,256,128]{3,2,1,0:T(8,128)(2,1)} %q_hbm.3, ...), custom_call_target="tpu_custom_call" | custom-call | flops 6039797760 | bytes 16777216 | tf_op jit(solution)/shard_map/early_rows/pallas_call | solution.py:120
  82.1 1.2 copy-done.5
  83.3 1.0 copy-done.8
  84.3 27.8 %all_to_all.15.early_ref = bf16[8,6,32,512]{3,2,1,0:T(8,128)(2,1)S(1)} all-to-all(bf16[8,6,32,512]{3,2,1,0:T(8,128)(2,1)} %copy-done.5), channel_id=1, replica_groups=mesh['member'=8,'space'=32] {'member'}, dimensions={0} | all-to-all | bytes 3145728 | tf_op jit(solution)/shard_map/all_to_all | solution.py:189
  112.1 2.6 %between.1 = f32[512,512]{1,0:T(8,128)S(1)} custom-call(bf16[8,6,32,512]{3,2,1,0:T(8,128)(2,1)S(1)} %all_to_all.15.early_ref, bf16[8,2,32,512]{3,2,1,0:T(8,128)(2,1)} %all-to-all-done.1.late_ref, f32[512,512]{1,0:T(8,128)S(1)} %copy-done.9, f32[512,512]{1,0:T(8,128)S(1)} %copy-done.7), custom_call_target="tpu_custom_call" | custom-call | flops 1073741824 | bytes 5242880 | tf_op jit(solution)/shard_map/between/pallas_call | solution.py:158
  114.7 15.5 %all_to_all.16 = f32[8,64,512]{2,1,0:T(8,128)S(1)} all-to-all(f32[8,64,512]{2,1,0:T(8,128)S(1)} %bitcast.13), channel_id=1, replica_groups=mesh['member'=8,'space'=32] {'member'}, dimensions={0} | all-to-all | bytes 2097152 | tf_op jit(solution)/shard_map/all_to_all | solution.py:194
  130.2 0.1 reduce_sum.9
  130.3 0.7 multiply_bitcast_fusion
  (23 shorter events, 0.1 us)
Async XLA Ops:
  0.0 44.1 %copy-start.3 = (bf16[6,8,256,128]{3,2,1,0:T(8,128)(2,1)S(1)}, bf16[6,8,256,128]{3,2,1,0:T(8,128)(2,1)}, u32[]{:S(2)}) copy-start(bf16[6,8,256,128]{3,2,1,0:T(8,128)(2,1)} %h_hbm.3) | copy-start | bytes 9437188
  0.0 44.1 %copy-start.12 = (f32[8,256]{1,0:T(8,128)S(1)}, f32[8,256]{1,0:T(8,128)}, u32[]{:S(2)}) copy-start(f32[8,256]{1,0:T(8,128)} %bal_ref.3) | copy-start | bytes 24580
  2.4 5.6 %copy-start.13 = (f32[128]{0:T(128)S(1)}, f32[128]{0:T(128)}, u32[]{:S(2)}) copy-start(f32[128]{0:T(128)} %param.15) | copy-start | bytes 1540
  2.4 5.6 %copy-start.14 = (f32[128]{0:T(128)S(1)}, f32[128]{0:T(128)}, u32[]{:S(2)}) copy-start(f32[128]{0:T(128)} %param.14) | copy-start | bytes 1540
  2.4 41.7 %copy-start.1 = (bf16[6,8,256,128]{3,2,1,0:T(8,128)(2,1)S(1)}, bf16[6,8,256,128]{3,2,1,0:T(8,128)(2,1)}, u32[]{:S(2)}) copy-start(bf16[6,8,256,128]{3,2,1,0:T(8,128)(2,1)} %v_hbm.3) | copy-start | bytes 9437188
  2.4 41.7 %copy-start.11 = (f32[8,256]{1,0:T(8,128)S(1)}, f32[8,256]{1,0:T(8,128)}, u32[]{:S(2)}) copy-start(f32[8,256]{1,0:T(8,128)} %psi_ref.3) | copy-start | bytes 24580
  2.6 41.5 %collective-permute-start.1 = (bf16[2,6,2,256,128]{4,3,2,1,0:T(8,128)(2,1)S(1)}, bf16[2,6,2,256,128]{4,3,2,1,0:T(8,128)(2,1)S(1)}, u32[]{:S(2)}, u32[]{:S(2)}) collective-permute-start(bf16[2,6,2,256,128]{4,3,2,1,0:T(8,128)(2,1)S(1)} %pad_maximum_fusion.1), channel_id=1, source_target_pairs={{1,2},{3,4},{5,6},{7,8},{9,10},{11,12},{13,14},{15,16},{17,18},{19... | collective-permute-start | bytes 4718600 | tf_op jit(solution)/shard_map/ppermute | solution.py:185
  4.6 39.5 %copy-start = (bf16[6,8,256,128]{3,2,1,0:T(8,128)(2,1)S(1)}, bf16[6,8,256,128]{3,2,1,0:T(8,128)(2,1)}, u32[]{:S(2)}) copy-start(bf16[6,8,256,128]{3,2,1,0:T(8,128)(2,1)} %u_hbm.3) | copy-start | bytes 9437188
  5.9 53.3 %collective-permute-start = (bf16[2,6,2,256,128]{4,3,2,1,0:T(8,128)(2,1)}, bf16[2,6,2,256,128]{4,3,2,1,0:T(8,128)(2,1)}, u32[]{:S(2)}, u32[]{:S(2)}) collective-permute-start(bf16[2,6,2,256,128]{4,3,2,1,0:T(8,128)(2,1)} %pad_maximum_fusion), channel_id=1, source_target_pairs={{0,1},{2,3},{4,5},{6,7},{8,9},{10,11},{12,13},{14,15},{16,17},{18,... | collective-permute-start | bytes 4718600 | tf_op jit(solution)/shard_map/ppermute | solution.py:186
  51.4 1.0 copy-start.6
  52.4 0.8 copy-start.10
  53.2 31.1 %all-to-all-start.1 = ((bf16[8,2,32,512]{3,2,1,0:T(8,128)(2,1)}), bf16[8,2,32,512]{3,2,1,0:T(8,128)(2,1)}, u32[]{:S(2)}, u32[]{:S(2)}) async-start(bf16[8,2,32,512]{3,2,1,0:T(8,128)(2,1)} %copy-done.10), calls=%async_computation.1 | async-start | bytes 1048576 | tf_op jit(solution)/shard_map/all_to_all | solution.py:191
  59.2 1.9 %copy-start.2 = (bf16[6,8,256,128]{3,2,1,0:T(8,128)(2,1)S(1)}, bf16[6,8,256,128]{3,2,1,0:T(8,128)(2,1)}, u32[]{:S(2)}) copy-start(bf16[6,8,256,128]{3,2,1,0:T(8,128)(2,1)} %v_hbm.3) | copy-start | bytes 9437188
  61.1 1.9 %copy-start.4 = (bf16[6,8,256,128]{3,2,1,0:T(8,128)(2,1)S(1)}, bf16[6,8,256,128]{3,2,1,0:T(8,128)(2,1)}, u32[]{:S(2)}) copy-start(bf16[6,8,256,128]{3,2,1,0:T(8,128)(2,1)} %h_hbm.3) | copy-start | bytes 9437188
  82.1 1.2 copy-start.5
  83.3 1.0 copy-start.8
  84.3 27.8 %copy-start.7 = (f32[512,512]{1,0:T(8,128)S(1)}, f32[512,512]{1,0:T(8,128)}, u32[]{:S(2)}) copy-start(f32[512,512]{1,0:T(8,128)} %copy-done.6) | copy-start | bytes 3145732
  84.3 27.8 %copy-start.9 = (f32[512,512]{1,0:T(8,128)S(1)}, f32[512,512]{1,0:T(8,128)}, u32[]{:S(2)}) copy-start(f32[512,512]{1,0:T(8,128)} %copy-done.8) | copy-start | bytes 3145732

commit v2 on v0

v2 whole, which is shorter than its diff:
```python
import functools

import jax
import jax.numpy as jnp
from jax import lax
from jax.experimental import pallas as pl
from jax.experimental.pallas import tpu as pltpu
from jax.sharding import PartitionSpec as P

ANY = pl.BlockSpec(memory_space=pl.ANY)
VMEM = pl.BlockSpec(memory_space=pltpu.VMEM)
HBM = pl.BlockSpec(memory_space=pltpu.HBM)
SIDE = 2
EDGE = 2


def params(mebibytes):
    return pltpu.CompilerParams(vmem_limit_bytes=mebibytes << 20)


def cost(flops, moved):
    return pl.CostEstimate(flops=flops, bytes_accessed=moved, transcendentals=0)


def gram(a):
    return lax.dot_general(a, a, (((0,), (0,)), ((), ())), preferred_element_type=jnp.float32)


def core_index():
    return lax.axis_index("space") % 2


def run(copies):
    for copy in copies:
        copy.start()


def finish(copies):
    for copy in copies:
        copy.wait()


def edges_kernel(parallels, u_hbm, v_hbm, far_ref, near_ref, sums_ref, sems):
    core = core_index()
    far_at = pl.ds((parallels - EDGE) * core, EDGE)
    near_at = pl.ds((parallels - EDGE) * (1 - core), EDGE)
    far = [pltpu.make_async_copy(x.at[:, far_at], far_ref.at[f], sems.at[f]) for f, x in enumerate((u_hbm, v_hbm))]
    near = [pltpu.make_async_copy(x.at[:, near_at], near_ref.at[f], sems.at[2 + f]) for f, x in enumerate((u_hbm, v_hbm))]
    run(far + near)
    for f in range(2):
        far[f].wait()
        for r in range(EDGE):
            total = far_ref[f, 0, r].astype(jnp.float32)
            for m in range(1, far_ref.shape[1]):
                total = total + far_ref[f, m, r].astype(jnp.float32)
            sums_ref[f, r] = total.astype(jnp.bfloat16)
    finish(near)


def edges_call(u, v):
    members, parallels, meridians, levels = u.shape
    edge = jax.ShapeDtypeStruct((2, members, EDGE, meridians, levels), u.dtype)
    return pl.pallas_call(
        functools.partial(edges_kernel, parallels),
        name="edges",
        out_shape=(edge, edge, jax.ShapeDtypeStruct((2, EDGE, meridians, levels), u.dtype)),
        in_specs=[HBM, HBM],
        out_specs=(VMEM, VMEM, VMEM),
        scratch_shapes=[pltpu.SemaphoreType.DMA((4,))],
        compiler_params=params(8),
        cost_estimate=cost(1 << 20, 6 << 20),
    )(u, v)


def spread_over(ref, rows_at, psi_b, sb_b, psi_ref, bal_ref, slope_t):
    meridians, levels = psi_b.shape
    psi_row = psi_ref[pl.ds(rows_at, 1), :] * (1.0 / 12.0)
    bal_row = bal_ref[pl.ds(rows_at, 1), :]
    psi_b[...] = jnp.transpose(jnp.broadcast_to(psi_row, (levels, meridians)))
    sb_b[...] = jnp.transpose(jnp.broadcast_to(bal_row, (levels, meridians))) * slope_t


def lat_diff(rows):
    return (rows[2] - rows[1]) * 8.0 - (rows[3] - rows[0])


def compute_rows(n, row_from, u_ext, v_ext, h_buf, q_buf, psi_ref, bal_ref, slopes_ref, d_buf, psi_b, sb_b, s_buf, g_ref, m_scr, mean_ref, chunk):
    members, _, meridians, levels = u_ext.shape
    row = lax.broadcasted_iota(jnp.int32, (meridians, meridians), 0)
    col = lax.broadcasted_iota(jnp.int32, (meridians, meridians), 1)
    east = (row + 1) % meridians == col
    west = (row + meridians - 1) % meridians == col
    stencil = jnp.where(east, 6.0, jnp.where(west, -6.0, 0.0)).astype(jnp.bfloat16)
    slope_t = slopes_ref[0:1, :]
    slope_q = slopes_ref[1:2, :]

    @pl.loop(0, n)
    def _(k):
        spread_over(None, row_from + k, psi_b, sb_b, psi_ref, bal_ref, slope_t)
        for m in range(members):
            winds = jnp.concatenate([v_ext[m, k + 2], u_ext[m, k + 2]], axis=1)
            d_buf[m] = jnp.dot(stencil, winds, preferred_element_type=jnp.float32)

        @pl.loop(0, meridians // chunk)
        def _(c):
            at = pl.ds(pl.multiple_of(c * chunk, chunk), chunk)
            psi = psi_b[at, :]
            sb = sb_b[at, :]
            total = [jnp.zeros((chunk, levels), jnp.float32) for _ in range(4)]
            for m in range(members):
                du = lat_diff([u_ext[m, k + e, at, :].astype(jnp.float32) for e in (0, 1, 3, 4)])
                dv = lat_diff([v_ext[m, k + e, at, :].astype(jnp.float32) for e in (0, 1, 3, 4)])
                curl = psi * (d_buf[m, at, 0:levels] - du)
                spread = psi * (d_buf[m, at, levels : 2 * levels] + dv)
                heat = h_buf[m, k, at, :].astype(jnp.float32) - sb * curl
                moist = q_buf[m, k, at, :].astype(jnp.float32) - slope_q * heat
                for f, x in enumerate((curl, spread, heat, moist)):
                    cut = slice(f * levels, (f + 1) * levels)
                    x = x.astype(jnp.bfloat16)
                    if mean_ref is None:
                        s_buf[m, at, cut] = x
                        total[f] = total[f] + x.astype(jnp.float32)
                    else:
                        mean = mean_ref[c, k, :, cut].astype(jnp.float32)
                        s_buf[m, at, cut] = (x.astype(jnp.float32) - mean).astype(jnp.bfloat16)
            if mean_ref is None:
                for f in range(4):
                    cut = slice(f * levels, (f + 1) * levels)
                    mean = total[f] * (1.0 / members)
                    m_scr[c, k, :, cut] = mean.astype(jnp.bfloat16)
                    for m in range(members):
                        s_buf[m, at, cut] = (s_buf[m, at, cut].astype(jnp.float32) - mean).astype(jnp.bfloat16)

        g_ref[...] += gram(s_buf[...].reshape(members * meridians, 4 * levels))


def scatter_means(m_scr, outs, first, sem, groups):
    y = lax.axis_index("member") // SIDE
    n = m_scr.shape[1]
    return [
        pltpu.make_async_copy(
            m_scr.at[pl.ds(SIDE * lax.rem(y + r, groups), SIDE)], out.at[:, pl.ds(first, n)], sem.at[r]
        )
        for r, out in enumerate(outs)
    ]


def inner_kernel(chunk, u_hbm, v_hbm, h_hbm, q_hbm, psi_ref, bal_ref, slopes_ref, g_ref, *rest):
    outs, (u_ext, v_ext, h_buf, q_buf, d_buf, psi_b, sb_b, s_buf, m_scr, sems, out_sems) = rest[:-11], rest[-11:]
    n = h_buf.shape[1]
    copies = [
        pltpu.make_async_copy(u_hbm, u_ext, sems.at[0]),
        pltpu.make_async_copy(v_hbm, v_ext, sems.at[1]),
        pltpu.make_async_copy(h_hbm.at[:, pl.ds(EDGE, n)], h_buf, sems.at[2]),
        pltpu.make_async_copy(q_hbm.at[:, pl.ds(EDGE, n)], q_buf, sems.at[3]),
    ]
    run(copies)
    g_ref[...] = jnp.zeros_like(g_ref)
    finish(copies)
    compute_rows(n, EDGE, u_ext, v_ext, h_buf, q_buf, psi_ref, bal_ref, slopes_ref, d_buf, psi_b, sb_b, s_buf, g_ref, m_scr, None, chunk)
    sends = scatter_means(m_scr, outs, 0, out_sems, len(outs))
    run(sends)
    finish(sends)


def edge_copies(side, u_hbm, v_hbm, h_hbm, q_hbm, halo, u_ext, v_ext, h_buf, q_buf, sems):
    parallels = u_hbm.shape[1]
    own = u_ext.shape[1] - EDGE
    own_from = pl.ds((parallels - own) * side, own)
    own_to = pl.ds(EDGE * (1 - side), own)
    halo_to = pl.ds(own * side, EDGE)
    row_from = pl.ds((parallels - EDGE) * side, EDGE)
    copies = [
        pltpu.make_async_copy(u_hbm.at[:, own_from], u_ext.at[:, own_to], sems.at[0]),
        pltpu.make_async_copy(v_hbm.at[:, own_from], v_ext.at[:, own_to], sems.at[1]),
        pltpu.make_async_copy(h_hbm.at[:, row_from], h_buf, sems.at[2]),
        pltpu.make_async_copy(q_hbm.at[:, row_from], q_buf, sems.at[3]),
    ]
    if halo is not None:
        copies.append(pltpu.make_async_copy(halo.at[0], u_ext.at[:, halo_to], sems.at[4]))
        copies.append(pltpu.make_async_copy(halo.at[1], v_ext.at[:, halo_to], sems.at[5]))
    return copies


def near_kernel(chunk, u_hbm, v_hbm, h_hbm, q_hbm, near_hbm, far_sums_ref, psi_ref, bal_ref, slopes_ref, g_in_ref, g_ref, late_ref, *rest):
    outs, scratch = rest[:-14], rest[-14:]
    u_ext, v_ext, h_buf, q_buf, d_buf, psi_b, sb_b, s_buf, m_scr, u_sum, v_sum, sems, late_sems, out_sems = scratch
    members, parallels, meridians, levels = u_hbm.shape
    core = core_index()
    side = 1 - core
    copies = edge_copies(side, u_hbm, v_hbm, h_hbm, q_hbm, near_hbm, u_ext, v_ext, h_buf, q_buf, sems)
    run(copies)
    g_ref[...] = g_in_ref[...]
    finish(copies)
    compute_rows(EDGE, (parallels - EDGE) * side, u_ext, v_ext, h_buf, q_buf, psi_ref, bal_ref, slopes_ref, d_buf, psi_b, sb_b, s_buf, g_ref, m_scr, None, chunk)
    near_sends = scatter_means(m_scr, outs, 0, out_sems, len(outs))
    run(near_sends)

    copies = edge_copies(core, u_hbm, v_hbm, h_hbm, q_hbm, None, u_ext, v_ext, h_buf, q_buf, late_sems)
    run(copies)
    own = u_ext.shape[1] - EDGE
    finish(copies)
    for f, (ext, total) in enumerate(((u_ext, u_sum), (v_ext, v_sum))):
        for r in range(EDGE):
            total[own * core + r] = far_sums_ref[f, r].astype(jnp.float32)
        for r in range(own):
            e = EDGE * (1 - core) + r
            total[e] = sum(ext[m, e].astype(jnp.float32) for m in range(members))
    for k in range(EDGE):
        spread_over(None, (parallels - EDGE) * core + k, psi_b, sb_b, psi_ref, bal_ref, slopes_ref[0:1, :])
        du = lat_diff([u_sum[k + e] for e in (0, 1, 3, 4)])
        dv = lat_diff([v_sum[k + e] for e in (0, 1, 3, 4)])
        east = [(pltpu.roll(x[k + 2], meridians - 1, 0) - pltpu.roll(x[k + 2], 1, 0)) * 6.0 for x in (v_sum, u_sum)]
        curl = psi_b[...] * (east[0] - du)
        spread = psi_b[...] * (east[1] + dv)
        heat = sum(h_buf[m, k].astype(jnp.float32) for m in range(members)) - sb_b[...] * curl
        moist = sum(q_buf[m, k].astype(jnp.float32) for m in range(members)) - slopes_ref[1:2, :] * heat
        for f, x in enumerate((curl, spread, heat, moist)):
            mean = (x * (1.0 / members)).astype(jnp.bfloat16)
            late_ref[:, k, :, f * levels : (f + 1) * levels] = mean.reshape(meridians // chunk, chunk, levels)
    late_sends = scatter_means(late_ref, outs, EDGE, late_sems, len(outs))
    run(late_sends)
    finish(near_sends + late_sends)


def far_kernel(chunk, u_hbm, v_hbm, h_hbm, q_hbm, far_hbm, late_ref, psi_ref, bal_ref, slopes_ref, g_in_ref, mine_ref, theirs_ref, g_ref, u_ext, v_ext, h_buf, q_buf, d_buf, psi_b, sb_b, s_buf, sems):
    members, parallels, meridians, levels = u_hbm.shape
    core = core_index()
    copies = edge_copies(core, u_hbm, v_hbm, h_hbm, q_hbm, far_hbm, u_ext, v_ext, h_buf, q_buf, sems)
    run(copies)
    groups = lax.axis_size("member") // SIDE
    apart = (mine_ref[...].astype(jnp.float32) - theirs_ref[...].astype(jnp.float32)).astype(jnp.bfloat16)
    apart = apart.reshape(-1, 4 * levels)
    g_ref[...] = g_in_ref[...] + gram(apart) * (members * groups / 2.0)
    finish(copies)
    compute_rows(EDGE, (parallels - EDGE) * core, u_ext, v_ext, h_buf, q_buf, psi_ref, bal_ref, slopes_ref, d_buf, psi_b, sb_b, s_buf, g_ref, None, late_ref, chunk)


def row_scratch(dims, n, ext):
    members, _, meridians, levels = dims
    return [
        pltpu.VMEM((members, ext, meridians, levels), jnp.bfloat16),
        pltpu.VMEM((members, ext, meridians, levels), jnp.bfloat16),
        pltpu.VMEM((members, n, meridians, levels), jnp.bfloat16),
        pltpu.VMEM((members, n, meridians, levels), jnp.bfloat16),
        pltpu.VMEM((members, meridians, 2 * levels), jnp.float32),
        pltpu.VMEM((meridians, levels), jnp.float32),
        pltpu.VMEM((meridians, levels), jnp.float32),
        pltpu.VMEM((members, meridians, 4 * levels), jnp.bfloat16),
    ]


def row_cost(dims, n):
    members, _, meridians, levels = dims
    return cost(4 * n * members * meridians * 16 * levels * levels, 8 << 20)


def between_kernel(members, g_in_ref, *rest):
    parts, (g_ref, mine_ref, theirs_ref) = rest[:-3], rest[-3:]
    side = lax.axis_index("member") % SIDE
    groups = len(parts) // 2
    total = g_in_ref[...]
    first = 0
    for part in (parts[:groups], parts[groups:]):
        _, n, chunk, width = part[0].shape
        overall = sum(p[...].astype(jnp.float32) for p in part) * (1.0 / groups)
        apart = [(p[...].astype(jnp.float32) - overall).astype(jnp.bfloat16).reshape(-1, width) for p in part]
        total = total + gram(jnp.concatenate(apart, axis=0)) * float(members)
        overall = overall.astype(jnp.bfloat16)
        low = side == 0
        mine_ref[first : first + n] = jnp.where(low, overall[0], overall[1])
        theirs_ref[first : first + n] = jnp.where(low, overall[1], overall[0])
        first += n
    g_ref[...] = total


def on_device(u, v, h, q, psi, bal, slope_t, slope_q):
    dims = members, parallels, meridians, levels = u.shape
    width = 4 * levels
    count = lax.axis_size("space")
    peers = lax.axis_size("member")
    groups = peers // SIDE
    chunk = meridians // peers
    inner = parallels - 2 * EDGE
    slopes = jnp.stack([slope_t, slope_q])

    across = [(i, i + 1) for i in range(1, count - 1, 2)]
    across = across + [(b, a) for a, b in across]
    within = [(i, i + 1) for i in range(0, count, 2)]
    within = within + [(b, a) for a, b in within]

    def along_y(r):
        return [(y * SIDE + x, (y + r) % groups * SIDE + x) for y in range(groups) for x in range(SIDE)]

    along_x = [(y * SIDE + x, y * SIDE + 1 - x) for y in range(groups) for x in range(SIDE)]

    far_edge, near_edge, far_sums = edges_call(u, v)
    far_sums = lax.ppermute(far_sums, "space", across)
    far = lax.ppermute(far_edge, "space", across)
    near = lax.ppermute(near_edge, "space", within)

    g_shape = jax.ShapeDtypeStruct((width, width), jnp.float32)
    handed = lambda n: (jax.ShapeDtypeStruct((SIDE, n, chunk, width), jnp.bfloat16),) * groups

    g, *inner_means = pl.pallas_call(
        functools.partial(inner_kernel, chunk),
        name="inner_rows",
        out_shape=(g_shape,) + handed(inner),
        in_specs=[HBM] * 4 + [VMEM] * 3,
        out_specs=(VMEM,) + (ANY,) * groups,
        scratch_shapes=row_scratch(dims, inner, parallels)
        + [pltpu.VMEM((peers, inner, chunk, width), jnp.bfloat16), pltpu.SemaphoreType.DMA((4,)), pltpu.SemaphoreType.DMA((groups,))],
        compiler_params=params(20),
        cost_estimate=row_cost(dims, inner),
    )(u, v, h, q, psi, bal, slopes)
    inner_means = [x if r == 0 else lax.ppermute(x, "member", along_y(r)) for r, x in enumerate(inner_means)]

    sum_shape = (2 * EDGE + EDGE, meridians, levels)
    g, late, *edge_means = pl.pallas_call(
        functools.partial(near_kernel, chunk),
        name="near_rows",
        out_shape=(g_shape, jax.ShapeDtypeStruct((peers, EDGE, chunk, width), jnp.bfloat16)) + handed(2 * EDGE),
        in_specs=[HBM] * 4 + [ANY] + [VMEM] * 5,
        out_specs=(VMEM, VMEM) + (ANY,) * groups,
        scratch_shapes=row_scratch(dims, EDGE, 3 * EDGE)
        + [pltpu.VMEM((peers, EDGE, chunk, width), jnp.bfloat16), pltpu.VMEM(sum_shape, jnp.float32), pltpu.VMEM(sum_shape, jnp.float32)]
        + [pltpu.SemaphoreType.DMA((6,)), pltpu.SemaphoreType.DMA((4,)), pltpu.SemaphoreType.DMA((groups,))],
        compiler_params=params(18),
        cost_estimate=row_cost(dims, EDGE),
    )(u, v, h, q, near, far_sums, psi, bal, slopes, g)
    edge_means = [x if r == 0 else lax.ppermute(x, "member", along_y(r)) for r, x in enumerate(edge_means)]

    half = jax.ShapeDtypeStruct((parallels, chunk, width), jnp.bfloat16)
    g, mine, theirs = pl.pallas_call(
        functools.partial(between_kernel, members),
        name="between",
        out_shape=(g_shape, half, half),
        in_specs=[VMEM] * (1 + 2 * groups),
        out_specs=(VMEM, VMEM, VMEM),
        compiler_params=params(16),
        cost_estimate=cost(1 << 30, 5 << 20),
    )(g, *inner_means, *edge_means)
    theirs = lax.ppermute(theirs, "member", along_x)

    g = pl.pallas_call(
        functools.partial(far_kernel, chunk),
        name="far_rows",
        out_shape=g_shape,
        in_specs=[ANY] * 5 + [VMEM] * 7,
        out_specs=VMEM,
        scratch_shapes=row_scratch(dims, EDGE, 3 * EDGE) + [pltpu.SemaphoreType.DMA((6,))],
        compiler_params=params(18),
        cost_estimate=row_cost(dims, EDGE),
    )(u, v, h, q, far, late, psi, bal, slopes, g, mine, theirs)

    parts = lax.all_to_all(g.reshape(peers, width // peers, width), "member", 0, 0, tiled=True)
    scale = 1.0 / ((members * peers - 1) * parallels * meridians)
    return (jnp.sum(parts, axis=0) * scale)[None]


def solution(mesh):
    placed = (P("member", "space", None, None),) * 4 + (P("space", None),) * 2 + (P(), P())
    return jax.shard_map(
        on_device, mesh=mesh, in_specs=placed, out_specs=P("space", "member", None), check_vma=False
    )
```

time: 398 us -> 101 us (0.25)
  the two profiles are of different devices: /device:TPU:2 before, /device:TPU:64 now
where the time goes in v2:
time: 101 us; the launch traced here: 100 us
  Pallas kernels  28.9 us (29%)
  blocking collectives  22.9 us (23%)
  waiting for transfers between devices  19.9 us (20%)
  starting transfers between devices  19.4 us (19%)
  local copies, waits for them, and re-layouts  8.28 us (8%)
    all_to_all x1, blocking collectives, on_device(): lax.all_to_all(g.reshape(peers, width // peers, width), 'member', 0, 0, t...  22.9 us
    ppermute x6, waiting for transfers between devices, on_device(): lax.ppermute(x, 'member', along_y(r))  12.9 us
    pallas_call x1, Pallas kernels, on_device(): pl.pallas_call(functools.partial(inner_kernel, chunk), name='inner_rows',...  12 us
    ppermute x6, starting transfers between devices, on_device(): lax.ppermute(x, 'member', along_y(r))  9.45 us
    pallas_call x1, Pallas kernels, on_device(): pl.pallas_call(functools.partial(near_kernel, chunk), name='near_rows', o...  8.69 us
    unnamed x24, local copies, waits for them, and re-layouts  8.28 us
    ppermute x1, waiting for transfers between devices, on_device(): theirs = lax.ppermute(theirs, 'member', along_x)  7.03 us
    pallas_call x1, Pallas kernels, on_device(): pl.pallas_call(functools.partial(far_kernel, chunk), name='far_rows', out...  6.06 us
  transfers between devices with their start and end apart: 10, of which 3 were waited for; matrix products, arithmetic and copies ran while one was open for 0% of the time, Pallas kernels for 22%

profile of v2, /device:TPU:64, one launch (start us, length us, event | category | flops | bytes accessed | tf_op | source)
XLA Modules:
  0.0 100.3 jit_solution(15038787327983820754)
XLA Ops:
  0.0 1.9 %copy-done = bf16[6,8,256,128]{3,2,1,0:T(8,128)(2,1)S(1)} copy-done((bf16[6,8,256,128]{3,2,1,0:T(8,128)(2,1)S(1)}, bf16[6,8,256,128]{3,2,1,0:T(8,128)(2,1)}, u32[]{:S(2)}) %copy-start) | copy-done | bytes 3145752
  1.9 1.9 %copy-done.2 = bf16[6,8,256,128]{3,2,1,0:T(8,128)(2,1)S(1)} copy-done((bf16[6,8,256,128]{3,2,1,0:T(8,128)(2,1)S(1)}, bf16[6,8,256,128]{3,2,1,0:T(8,128)(2,1)}, u32[]{:S(2)}) %copy-start.2) | copy-done | bytes 3145752
  3.8 0.6 edges.1
  4.5 3.2 %collective-permute-start.2 = (bf16[2,2,256,128]{3,2,1,0:T(8,128)(2,1)S(1)}, bf16[2,2,256,128]{3,2,1,0:T(8,128)(2,1)S(1)}, u32[]{:S(2)}, u32[]{:S(2)}) collective-permute-start(bf16[2,2,256,128]{3,2,1,0:T(8,128)(2,1)S(1)} %get-tuple-element.24), channel_id=1, source_target_pairs={{1,2},{3,4},{5,6},{7,8},{9,10},{11,12},{13,14},{15,16},{17,18},{19... | collective-permute-start | bytes 786440 | tf_op jit(solution)/shard_map/ppermute | solution.py:298
  7.7 3.6 %collective-permute-start = (bf16[2,6,2,256,128]{4,3,2,1,0:T(8,128)(2,1)S(1)}, bf16[2,6,2,256,128]{4,3,2,1,0:T(8,128)(2,1)S(1)}, u32[]{:S(2)}, u32[]{:S(2)}) collective-permute-start(bf16[2,6,2,256,128]{4,3,2,1,0:T(8,128)(2,1)S(1)} %get-tuple-element.22), channel_id=1, source_target_pairs={{1,2},{3,4},{5,6},{7,8},{9,10},{11,12},{13,14},{15,16},{17,18},{19... | collective-permute-start | bytes 4718600 | tf_op jit(solution)/shard_map/ppermute | solution.py:299
  11.3 1.9 %copy-done.4 = bf16[6,8,256,128]{3,2,1,0:T(8,128)(2,1)S(1)} copy-done((bf16[6,8,256,128]{3,2,1,0:T(8,128)(2,1)S(1)}, bf16[6,8,256,128]{3,2,1,0:T(8,128)(2,1)}, u32[]{:S(2)}) %copy-start.4) | copy-done | bytes 3145752
  13.2 1.9 %copy-done.6 = bf16[6,8,256,128]{3,2,1,0:T(8,128)(2,1)S(1)} copy-done((bf16[6,8,256,128]{3,2,1,0:T(8,128)(2,1)S(1)}, bf16[6,8,256,128]{3,2,1,0:T(8,128)(2,1)}, u32[]{:S(2)}) %copy-start.6) | copy-done | bytes 3145752
  15.1 0.7 copy-done.9
  15.8 12.0 %inner_rows.1 = (f32[512,512]{1,0:T(8,128)S(1)}, bf16[2,4,32,512]{3,2,1,0:T(8,128)(2,1)S(1)}, bf16[2,4,32,512]{3,2,1,0:T(8,128)(2,1)S(1)}, bf16[2,4,32,512]{3,2,...) custom-call(bf16[6,8,256,128]{3,2,1,0:T(8,128)(2,1)S(1)} %copy-done.1, bf16[6,8,256,128]{3,2,1,0:T(8,128)(2,1)S(1)} %copy-done.3, ...), custom_call_target="tpu_custom_call" | custom-call | flops 6442450944 | bytes 8388608 | tf_op jit(solution)/shard_map/inner_rows/pallas_call | solution.py:305
  27.8 1.7 %collective-permute-start.3 = (bf16[2,4,32,512]{3,2,1,0:T(8,128)(2,1)S(1)}, bf16[2,4,32,512]{3,2,1,0:T(8,128)(2,1)S(1)}, u32[]{:S(2)}, u32[]{:S(2)}) collective-permute-start(bf16[2,4,32,512]{3,2,1,0:T(8,128)(2,1)S(1)} %get-tuple-element.29), channel_id=1, source_target_pairs={{0,64},{32,96},{64,128},{96,160},{128,192},{160,224},{192,0},{224,... | collective-permute-start | bytes 786440 | tf_op jit(solution)/shard_map/ppermute | solution.py:316
  29.5 2.9 %collective-permute-start.4 = (bf16[2,4,32,512]{3,2,1,0:T(8,128)(2,1)S(1)}, bf16[2,4,32,512]{3,2,1,0:T(8,128)(2,1)S(1)}, u32[]{:S(2)}, u32[]{:S(2)}) collective-permute-start(bf16[2,4,32,512]{3,2,1,0:T(8,128)(2,1)S(1)} %get-tuple-element.30), channel_id=1, source_target_pairs={{0,128},{32,160},{64,192},{96,224},{128,0},{160,32},{192,64},{224,... | collective-permute-start | bytes 786440 | tf_op jit(solution)/shard_map/ppermute | solution.py:316
  32.4 1.3 %collective-permute-start.5 = (bf16[2,4,32,512]{3,2,1,0:T(8,128)(2,1)S(1)}, bf16[2,4,32,512]{3,2,1,0:T(8,128)(2,1)S(1)}, u32[]{:S(2)}, u32[]{:S(2)}) collective-permute-start(bf16[2,4,32,512]{3,2,1,0:T(8,128)(2,1)S(1)} %get-tuple-element.31), channel_id=1, source_target_pairs={{0,192},{32,224},{64,0},{96,32},{128,64},{160,96},{192,128},{224,1... | collective-permute-start | bytes 786440 | tf_op jit(solution)/shard_map/ppermute | solution.py:316
  33.7 8.7 %near_rows.1 = (f32[512,512]{1,0:T(8,128)S(1)}, bf16[8,2,32,512]{3,2,1,0:T(8,128)(2,1)S(1)}, bf16[2,4,32,512]{3,2,1,0:T(8,128)(2,1)S(1)}, bf16[2,4,32,512]{3,2,1...) custom-call(bf16[6,8,256,128]{3,2,1,0:T(8,128)(2,1)S(1)} %copy-done.1, ...), custom_call_target="tpu_custom_call" | custom-call | flops 3221225472 | bytes 8388608 | tf_op jit(solution)/shard_map/near_rows/pallas_call | solution.py:319
  42.4 0.8 collective-permute-start.6
  43.2 1.2 %collective-permute-start.7 = (bf16[2,4,32,512]{3,2,1,0:T(8,128)(2,1)S(1)}, bf16[2,4,32,512]{3,2,1,0:T(8,128)(2,1)S(1)}, u32[]{:S(2)}, u32[]{:S(2)}) collective-permute-start(bf16[2,4,32,512]{3,2,1,0:T(8,128)(2,1)S(1)} %get-tuple-element.34), channel_id=1, source_target_pairs={{0,128},{32,160},{64,192},{96,224},{128,0},{160,32},{192,64},{224,... | collective-permute-start | bytes 786440 | tf_op jit(solution)/shard_map/ppermute | solution.py:331
  44.4 1.6 %collective-permute-start.8 = (bf16[2,4,32,512]{3,2,1,0:T(8,128)(2,1)S(1)}, bf16[2,4,32,512]{3,2,1,0:T(8,128)(2,1)S(1)}, u32[]{:S(2)}, u32[]{:S(2)}) collective-permute-start(bf16[2,4,32,512]{3,2,1,0:T(8,128)(2,1)S(1)} %get-tuple-element.35), channel_id=1, source_target_pairs={{0,192},{32,224},{64,0},{96,32},{128,64},{160,96},{192,128},{224,1... | collective-permute-start | bytes 786440 | tf_op jit(solution)/shard_map/ppermute | solution.py:331
  46.0 11.7 %collective-permute-done.6.rest_5_ = bf16[2,4,32,512]{3,2,1,0:T(8,128)(2,1)S(1)} collective-permute-done((bf16[2,4,32,512]{3,2,1,0:T(8,128)(2,1)S(1)}, bf16[2,4,32,512]{3,2,1,0:T(8,128)(2,1)S(1)}, u32[]{:S(2)}, u32[]{:S(2)}) %collective-permute-start.6) | collective-permute-done | bytes 262176 | tf_op jit(solution)/shard_map/ppermute | solution.py:331
  57.7 1.2 %collective-permute-done.8.rest_7_ = bf16[2,4,32,512]{3,2,1,0:T(8,128)(2,1)S(1)} collective-permute-done((bf16[2,4,32,512]{3,2,1,0:T(8,128)(2,1)S(1)}, bf16[2,4,32,512]{3,2,1,0:T(8,128)(2,1)S(1)}, u32[]{:S(2)}, u32[]{:S(2)}) %collective-permute-start.8) | collective-permute-done | bytes 262176 | tf_op jit(solution)/shard_map/ppermute | solution.py:331
  58.9 1.5 %between.1 = (f32[512,512]{1,0:T(8,128)S(1)}, bf16[8,32,512]{2,1,0:T(8,128)(2,1)S(1)}, bf16[8,32,512]{2,1,0:T(8,128)(2,1)S(1)}) custom-call(f32[512,512]{1,0:T(8,128)S(1)} %get-tuple-element.27.g_in_ref, bf16[2,4,32,512]{3,2,1,0:T(8,128)(2,1)S(1)} %get-tuple-element.28.rest_0_, bf16[2,4,32,512]{3,2,1,0:T(8,128)(2,1)S(1)} %collective-permute-done.3.rest_1_, ...), custom_call_target="tpu_custom_call" | custom-call | flops 1073741824 | bytes 5242880 | tf_op jit(solution)/shard_map/between/pallas_call | solution.py:334
  60.4 3.1 %collective-permute-start.9 = (bf16[8,32,512]{2,1,0:T(8,128)(2,1)S(1)}, bf16[8,32,512]{2,1,0:T(8,128)(2,1)S(1)}, u32[]{:S(2)}, u32[]{:S(2)}) collective-permute-start(bf16[8,32,512]{2,1,0:T(8,128)(2,1)S(1)} %get-tuple-element.38), channel_id=1, source_target_pairs={{0,32},{32,0},{64,96},{96,64},{128,160},{160,128},{192,224},{224,1... | collective-permute-start | bytes 786440 | tf_op jit(solution)/shard_map/ppermute | solution.py:343
  63.6 7.0 %collective-permute-done.9.theirs_ref = bf16[8,32,512]{2,1,0:T(8,128)(2,1)S(1)} collective-permute-done((bf16[8,32,512]{2,1,0:T(8,128)(2,1)S(1)}, bf16[8,32,512]{2,1,0:T(8,128)(2,1)S(1)}, u32[]{:S(2)}, u32[]{:S(2)}) %collective-permute-start.9) | collective-permute-done | bytes 262176 | tf_op jit(solution)/shard_map/ppermute | solution.py:343
  70.6 6.1 %far_rows.1 = f32[512,512]{1,0:T(8,128)S(1)} custom-call(bf16[6,8,256,128]{3,2,1,0:T(8,128)(2,1)S(1)} %copy-done.1, bf16[6,8,256,128]{3,2,1,0:T(8,128)(2,1)S(1)} %copy-done.3, bf16[6,8,256,128]{3,2,1,0:T(8,128)(2,1)S(1)} %copy-done.5, bf16[6,8,256,128]{3,2,1,0:T(8,128)(2,1)S(1)} %copy-done.7, bf16[2,6,2,256,128]{4,3,2,1,0:T(8,128)(2,1)S(1)} %collective-permute-done.far_hbm, ...), custom_call_target="tpu_custom_call" | custom-call | flops 3221225472 | bytes 8388608 | tf_op jit(solution)/shard_map/far_rows/pallas_call | solution.py:345
  76.7 22.9 %all_to_all.5 = f32[8,64,512]{2,1,0:T(8,128)S(1)} all-to-all(f32[8,64,512]{2,1,0:T(8,128)S(1)} %bitcast.5), channel_id=1, replica_groups=mesh['member'=8,'space'=32] {'member'}, dimensions={0} | all-to-all | bytes 2097152 | tf_op jit(solution)/shard_map/all_to_all | solution.py:356
  99.6 0.7 multiply_bitcast_fusion
  (29 shorter events, 0.2 us)
Async XLA Ops:
  0.0 1.9 %copy-start = (bf16[6,8,256,128]{3,2,1,0:T(8,128)(2,1)S(1)}, bf16[6,8,256,128]{3,2,1,0:T(8,128)(2,1)}, u32[]{:S(2)}) copy-start(bf16[6,8,256,128]{3,2,1,0:T(8,128)(2,1)} %u_hbm.7) | copy-start | bytes 9437188
  1.9 1.9 %copy-start.2 = (bf16[6,8,256,128]{3,2,1,0:T(8,128)(2,1)S(1)}, bf16[6,8,256,128]{3,2,1,0:T(8,128)(2,1)}, u32[]{:S(2)}) copy-start(bf16[6,8,256,128]{3,2,1,0:T(8,128)(2,1)} %v_hbm.7) | copy-start | bytes 9437188
  3.8 7.5 %copy-start.10 = (f32[128]{0:T(128)S(1)}, f32[128]{0:T(128)}, u32[]{:S(2)}) copy-start(f32[128]{0:T(128)} %param.15) | copy-start | bytes 1540
  3.8 7.5 %copy-start.11 = (f32[128]{0:T(128)S(1)}, f32[128]{0:T(128)}, u32[]{:S(2)}) copy-start(f32[128]{0:T(128)} %param.14) | copy-start | bytes 1540
  3.8 7.5 %copy-start.1 = (bf16[6,8,256,128]{3,2,1,0:T(8,128)(2,1)S(1)}, bf16[6,8,256,128]{3,2,1,0:T(8,128)(2,1)}, u32[]{:S(2)}) copy-start(bf16[6,8,256,128]{3,2,1,0:T(8,128)(2,1)} %u_hbm.7) | copy-start | bytes 9437188
  3.8 7.5 %copy-start.3 = (bf16[6,8,256,128]{3,2,1,0:T(8,128)(2,1)S(1)}, bf16[6,8,256,128]{3,2,1,0:T(8,128)(2,1)}, u32[]{:S(2)}) copy-start(bf16[6,8,256,128]{3,2,1,0:T(8,128)(2,1)} %v_hbm.7) | copy-start | bytes 9437188
  3.8 7.5 %copy-start.8 = (f32[8,256]{1,0:T(8,128)S(1)}, f32[8,256]{1,0:T(8,128)}, u32[]{:S(2)}) copy-start(f32[8,256]{1,0:T(8,128)} %psi_ref.5) | copy-start | bytes 24580
  4.4 29.3 %collective-permute-start.1 = (bf16[2,6,2,256,128]{4,3,2,1,0:T(8,128)(2,1)S(1)}, bf16[2,6,2,256,128]{4,3,2,1,0:T(8,128)(2,1)S(1)}, u32[]{:S(2)}, u32[]{:S(2)}) collective-permute-start(bf16[2,6,2,256,128]{4,3,2,1,0:T(8,128)(2,1)S(1)} %get-tuple-element.23), channel_id=1, source_target_pairs={{0,1},{2,3},{4,5},{6,7},{8,9},{10,11},{12,13},{14,15},{16,17},{18,... | collective-permute-start | bytes 4718600 | tf_op jit(solution)/shard_map/ppermute | solution.py:300
  4.5 27.9 %collective-permute-start.2 = (bf16[2,2,256,128]{3,2,1,0:T(8,128)(2,1)S(1)}, bf16[2,2,256,128]{3,2,1,0:T(8,128)(2,1)S(1)}, u32[]{:S(2)}, u32[]{:S(2)}) collective-permute-start(bf16[2,2,256,128]{3,2,1,0:T(8,128)(2,1)S(1)} %get-tuple-element.24), channel_id=1, source_target_pairs={{1,2},{3,4},{5,6},{7,8},{9,10},{11,12},{13,14},{15,16},{17,18},{19... | collective-permute-start | bytes 786440 | tf_op jit(solution)/shard_map/ppermute | solution.py:298
  7.7 55.9 %collective-permute-start = (bf16[2,6,2,256,128]{4,3,2,1,0:T(8,128)(2,1)S(1)}, bf16[2,6,2,256,128]{4,3,2,1,0:T(8,128)(2,1)S(1)}, u32[]{:S(2)}, u32[]{:S(2)}) collective-permute-start(bf16[2,6,2,256,128]{4,3,2,1,0:T(8,128)(2,1)S(1)} %get-tuple-element.22), channel_id=1, source_target_pairs={{1,2},{3,4},{5,6},{7,8},{9,10},{11,12},{13,14},{15,16},{17,18},{19... | collective-permute-start | bytes 4718600 | tf_op jit(solution)/shard_map/ppermute | solution.py:299
  11.3 1.9 %copy-start.4 = (bf16[6,8,256,128]{3,2,1,0:T(8,128)(2,1)S(1)}, bf16[6,8,256,128]{3,2,1,0:T(8,128)(2,1)}, u32[]{:S(2)}) copy-start(bf16[6,8,256,128]{3,2,1,0:T(8,128)(2,1)} %h_hbm.5) | copy-start | bytes 9437188
  13.2 1.9 %copy-start.6 = (bf16[6,8,256,128]{3,2,1,0:T(8,128)(2,1)S(1)}, bf16[6,8,256,128]{3,2,1,0:T(8,128)(2,1)}, u32[]{:S(2)}) copy-start(bf16[6,8,256,128]{3,2,1,0:T(8,128)(2,1)} %q_hbm.5) | copy-start | bytes 9437188
  15.1 0.7 copy-start.9
  27.8 15.4 %collective-permute-start.3 = (bf16[2,4,32,512]{3,2,1,0:T(8,128)(2,1)S(1)}, bf16[2,4,32,512]{3,2,1,0:T(8,128)(2,1)S(1)}, u32[]{:S(2)}, u32[]{:S(2)}) collective-permute-start(bf16[2,4,32,512]{3,2,1,0:T(8,128)(2,1)S(1)} %get-tuple-element.29), channel_id=1, source_target_pairs={{0,64},{32,96},{64,128},{96,160},{128,192},{160,224},{192,0},{224,... | collective-permute-start | bytes 786440 | tf_op jit(solution)/shard_map/ppermute | solution.py:316
  29.5 14.9 %collective-permute-start.4 = (bf16[2,4,32,512]{3,2,1,0:T(8,128)(2,1)S(1)}, bf16[2,4,32,512]{3,2,1,0:T(8,128)(2,1)S(1)}, u32[]{:S(2)}, u32[]{:S(2)}) collective-permute-start(bf16[2,4,32,512]{3,2,1,0:T(8,128)(2,1)S(1)} %get-tuple-element.30), channel_id=1, source_target_pairs={{0,128},{32,160},{64,192},{96,224},{128,0},{160,32},{192,64},{224,... | collective-permute-start | bytes 786440 | tf_op jit(solution)/shard_map/ppermute | solution.py:316
  32.4 13.6 %collective-permute-start.5 = (bf16[2,4,32,512]{3,2,1,0:T(8,128)(2,1)S(1)}, bf16[2,4,32,512]{3,2,1,0:T(8,128)(2,1)S(1)}, u32[]{:S(2)}, u32[]{:S(2)}) collective-permute-start(bf16[2,4,32,512]{3,2,1,0:T(8,128)(2,1)S(1)} %get-tuple-element.31), channel_id=1, source_target_pairs={{0,192},{32,224},{64,0},{96,32},{128,64},{160,96},{192,128},{224,1... | collective-permute-start | bytes 786440 | tf_op jit(solution)/shard_map/ppermute | solution.py:316
  33.7 36.9 %copy-start.7 = (bf16[6,8,256,128]{3,2,1,0:T(8,128)(2,1)S(1)}, bf16[6,8,256,128]{3,2,1,0:T(8,128)(2,1)}, u32[]{:S(2)}) copy-start(bf16[6,8,256,128]{3,2,1,0:T(8,128)(2,1)} %q_hbm.5) | copy-start | bytes 9437188
  42.4 28.2 %copy-start.5 = (bf16[6,8,256,128]{3,2,1,0:T(8,128)(2,1)S(1)}, bf16[6,8,256,128]{3,2,1,0:T(8,128)(2,1)}, u32[]{:S(2)}) copy-start(bf16[6,8,256,128]{3,2,1,0:T(8,128)(2,1)} %h_hbm.5) | copy-start | bytes 9437188
  42.4 15.2 %collective-permute-start.6 = (bf16[2,4,32,512]{3,2,1,0:T(8,128)(2,1)S(1)}, bf16[2,4,32,512]{3,2,1,0:T(8,128)(2,1)S(1)}, u32[]{:S(2)}, u32[]{:S(2)}) collective-permute-start(bf16[2,4,32,512]{3,2,1,0:T(8,128)(2,1)S(1)} %get-tuple-element.33), channel_id=1, source_target_pairs={{0,64},{32,96},{64,128},{96,160},{128,192},{160,224},{192,0},{224,... | collective-permute-start | bytes 786440 | tf_op jit(solution)/shard_map/ppermute | solution.py:331
  43.2 14.5 %collective-permute-start.7 = (bf16[2,4,32,512]{3,2,1,0:T(8,128)(2,1)S(1)}, bf16[2,4,32,512]{3,2,1,0:T(8,128)(2,1)S(1)}, u32[]{:S(2)}, u32[]{:S(2)}) collective-permute-start(bf16[2,4,32,512]{3,2,1,0:T(8,128)(2,1)S(1)} %get-tuple-element.34), channel_id=1, source_target_pairs={{0,128},{32,160},{64,192},{96,224},{128,0},{160,32},{192,64},{224,... | collective-permute-start | bytes 786440 | tf_op jit(solution)/shard_map/ppermute | solution.py:331
  44.4 14.5 %collective-permute-start.8 = (bf16[2,4,32,512]{3,2,1,0:T(8,128)(2,1)S(1)}, bf16[2,4,32,512]{3,2,1,0:T(8,128)(2,1)S(1)}, u32[]{:S(2)}, u32[]{:S(2)}) collective-permute-start(bf16[2,4,32,512]{3,2,1,0:T(8,128)(2,1)S(1)} %get-tuple-element.35), channel_id=1, source_target_pairs={{0,192},{32,224},{64,0},{96,32},{128,64},{160,96},{192,128},{224,1... | collective-permute-start | bytes 786440 | tf_op jit(solution)/shard_map/ppermute | solution.py:331
  60.4 10.2 %collective-permute-start.9 = (bf16[8,32,512]{2,1,0:T(8,128)(2,1)S(1)}, bf16[8,32,512]{2,1,0:T(8,128)(2,1)S(1)}, u32[]{:S(2)}, u32[]{:S(2)}) collective-permute-start(bf16[8,32,512]{2,1,0:T(8,128)(2,1)S(1)} %get-tuple-element.38), channel_id=1, source_target_pairs={{0,32},{32,0},{64,96},{96,64},{128,160},{160,128},{192,224},{224,1... | collective-permute-start | bytes 786440 | tf_op jit(solution)/shard_map/ppermute | solution.py:343

commit v3 on v2

v3 whole, which is shorter than its diff:
```python
import functools

import jax
import jax.numpy as jnp
from jax import lax
from jax.experimental import pallas as pl
from jax.experimental.pallas import tpu as pltpu
from jax.sharding import PartitionSpec as P

ANY = pl.BlockSpec(memory_space=pl.ANY)
VMEM = pl.BlockSpec(memory_space=pltpu.VMEM)
SIDE = 2
EDGE = 2


def params(mebibytes):
    return pltpu.CompilerParams(vmem_limit_bytes=mebibytes << 20)


def in_hbm(x):
    return pltpu.with_memory_space_constraint(x, pltpu.HBM)


def cost(flops, moved):
    return pl.CostEstimate(flops=flops, bytes_accessed=moved, transcendentals=0)


def gram(a, b):
    return lax.dot_general(a, b, (((0,), (0,)), ((), ())), preferred_element_type=jnp.float32)


def core_index():
    return lax.axis_index("space") % 2


def run(copies):
    for copy in copies:
        copy.start()


def finish(copies):
    for copy in copies:
        copy.wait()


def edges_kernel(parallels, u_hbm, v_hbm, far_ref, near_ref, sums_ref, sems):
    core = core_index()
    far_at = pl.ds((parallels - EDGE) * core, EDGE)
    near_at = pl.ds((parallels - EDGE) * (1 - core), EDGE)
    far = [pltpu.make_async_copy(x.at[:, far_at], far_ref.at[f], sems.at[f]) for f, x in enumerate((u_hbm, v_hbm))]
    near = [pltpu.make_async_copy(x.at[:, near_at], near_ref.at[f], sems.at[2 + f]) for f, x in enumerate((u_hbm, v_hbm))]
    run(far + near)
    for f in range(2):
        far[f].wait()
        for r in range(EDGE):
            total = far_ref[f, 0, r].astype(jnp.float32)
            for m in range(1, far_ref.shape[1]):
                total = total + far_ref[f, m, r].astype(jnp.float32)
            sums_ref[f, r] = total.astype(jnp.bfloat16)
    finish(near)


def edges_call(u, v):
    members, parallels, meridians, levels = u.shape
    edge = jax.ShapeDtypeStruct((2, members, EDGE, meridians, levels), u.dtype)
    return pl.pallas_call(
        functools.partial(edges_kernel, parallels),
        name="edges",
        out_shape=(edge, edge, jax.ShapeDtypeStruct((2, EDGE, meridians, levels), u.dtype)),
        in_specs=[ANY, ANY],
        out_specs=(VMEM, VMEM, VMEM),
        scratch_shapes=[pltpu.SemaphoreType.DMA((4,))],
        compiler_params=params(50),
        cost_estimate=cost(1 << 20, 6 << 20),
    )(u, v)


def spread_over(at, psi_ref, bal_ref, slope_t, levels):
    shape = (levels, psi_ref.shape[1])
    psi = jnp.transpose(jnp.broadcast_to(psi_ref[pl.ds(at, 1), :] * (1.0 / 12.0), shape))
    balance = jnp.transpose(jnp.broadcast_to(bal_ref[pl.ds(at, 1), :], shape))
    return psi, balance * slope_t


def lat_diff(rows):
    return (rows[2] - rows[1]) * 8.0 - (rows[3] - rows[0])


def add_gram(g_ref, a):
    half = a.shape[1] // 2
    g_ref[0:half] += gram(a[:, :half], a)
    g_ref[half:, half:] += gram(a[:, half:], a[:, half:])


def compute_rows(n, row_from, winds, scalars, psi_ref, bal_ref, slopes_ref, work, g_ref, m_ref, known, chunk, ready=lambda: None):
    u_ext, v_ext = winds
    h_buf, q_buf = scalars
    d_bufs, psi_bs, sb_bs, s_bufs = work[0:2], work[2:4], work[4:6], work[6:8]
    members, _, meridians, levels = u_ext.shape
    row = lax.broadcasted_iota(jnp.int32, (meridians, meridians), 0)
    col = lax.broadcasted_iota(jnp.int32, (meridians, meridians), 1)
    east = (row + 1) % meridians == col
    west = (row + meridians - 1) % meridians == col
    stencil = jnp.where(east, 6.0, jnp.where(west, -6.0, 0.0)).astype(jnp.bfloat16)
    slope_t = slopes_ref[0:1, :]
    slope_q = slopes_ref[1:2, :]
    half = meridians // 2
    cuts = [slice(f * levels, (f + 1) * levels) for f in range(4)]

    def prepare(k):
        b = k % 2
        psi_bs[b][...], sb_bs[b][...] = spread_over(row_from + k, psi_ref, bal_ref, slope_t, levels)
        for m in range(members):
            both = jnp.concatenate([v_ext[m, k + EDGE], u_ext[m, k + EDGE]], axis=1)
            d_bufs[b][m] = jnp.dot(stencil, both, preferred_element_type=jnp.float32)

    def derive(k, part):
        b = k % 2
        s_buf = s_bufs[part]
        for start in range(0, half, chunk):
            c = (part * half + start) // chunk
            at = slice(c * chunk, (c + 1) * chunk)
            to = slice(start, start + chunk)
            psi = psi_bs[b][at, :]
            sb = sb_bs[b][at, :]
            total = [None] * 4
            for m in range(members):
                du = lat_diff([u_ext[m, k + e, at, :].astype(jnp.float32) for e in (0, 1, 3, 4)])
                dv = lat_diff([v_ext[m, k + e, at, :].astype(jnp.float32) for e in (0, 1, 3, 4)])
                curl = psi * (d_bufs[b][m, at, 0:levels] - du)
                spread = psi * (d_bufs[b][m, at, levels : 2 * levels] + dv)
                heat = h_buf[m, k, at, :].astype(jnp.float32) - sb * curl
                moist = q_buf[m, k, at, :].astype(jnp.float32) - slope_q * heat
                for f, x in enumerate((curl, spread, heat, moist)):
                    x = x.astype(jnp.bfloat16)
                    if known:
                        mean = m_ref[c, k, :, cuts[f]].astype(jnp.float32)
                        s_buf[m, to, cuts[f]] = (x.astype(jnp.float32) - mean).astype(jnp.bfloat16)
                    else:
                        s_buf[m, to, cuts[f]] = x
                        x = x.astype(jnp.float32)
                        total[f] = x if m == 0 else total[f] + x
            if not known:
                for f, cut in enumerate(cuts):
                    mean = total[f] * (1.0 / members)
                    m_ref[c, k, :, cut] = mean.astype(jnp.bfloat16)
                    for m in range(members):
                        s_buf[m, to, cut] = (s_buf[m, to, cut].astype(jnp.float32) - mean).astype(jnp.bfloat16)

    def take(part):
        s_buf = s_bufs[part]
        add_gram(g_ref, s_buf[...].reshape(-1, s_buf.shape[2]))

    prepare(0)
    ready()
    for k in range(n):
        derive(k, 0)
        if k > 0:
            take(1)
        if k + 1 < n:
            prepare(k + 1)
        derive(k, 1)
        take(0)
    take(1)


def scatter_means(m_scr, outs, first, sem, groups):
    y = lax.axis_index("member") // SIDE
    n = m_scr.shape[1]
    return [
        pltpu.make_async_copy(
            m_scr.at[pl.ds(SIDE * lax.rem(y + r, groups), SIDE)], out.at[:, pl.ds(first, n)], sem.at[r]
        )
        for r, out in enumerate(outs)
    ]


def inner_kernel(chunk, u_hbm, v_hbm, h_hbm, q_hbm, psi_ref, bal_ref, slopes_ref, g_ref, *rest):
    outs, scratch = rest[:-15], rest[-15:]
    u_ext, v_ext, h_buf, q_buf = scratch[:4]
    work = scratch[4:12]
    m_scr, sems, out_sems = scratch[12:]
    n = m_scr.shape[1]
    inner = pl.ds(EDGE, n)
    pairs = ((u_hbm, u_ext), (v_hbm, v_ext), (h_hbm.at[:, inner], h_buf), (q_hbm.at[:, inner], q_buf))
    copies = [pltpu.make_async_copy(x, y, sems.at[i]) for i, (x, y) in enumerate(pairs)]
    run(copies)
    g_ref[...] = jnp.zeros_like(g_ref)
    finish(copies[:2])
    compute_rows(n, EDGE, (u_ext, v_ext), (h_buf, q_buf), psi_ref, bal_ref, slopes_ref, work, g_ref, m_scr, False, chunk, lambda: finish(copies[2:]))
    sends = scatter_means(m_scr, outs, 0, out_sems, len(outs))
    run(sends)
    finish(sends)


def edge_copies(side, u_hbm, v_hbm, h_hbm, q_hbm, halo, u_ext, v_ext, h_buf, q_buf, sems):
    parallels = u_hbm.shape[1]
    own = u_ext.shape[1] - EDGE
    own_from = pl.ds((parallels - own) * side, own)
    own_to = pl.ds(EDGE * (1 - side), own)
    halo_to = pl.ds(own * side, EDGE)
    row_from = pl.ds((parallels - EDGE) * side, EDGE)
    copies = [
        pltpu.make_async_copy(u_hbm.at[:, own_from], u_ext.at[:, own_to], sems.at[0]),
        pltpu.make_async_copy(v_hbm.at[:, own_from], v_ext.at[:, own_to], sems.at[1]),
        pltpu.make_async_copy(h_hbm.at[:, row_from], h_buf, sems.at[2]),
        pltpu.make_async_copy(q_hbm.at[:, row_from], q_buf, sems.at[3]),
    ]
    if halo is not None:
        copies.append(pltpu.make_async_copy(halo.at[0], u_ext.at[:, halo_to], sems.at[4]))
        copies.append(pltpu.make_async_copy(halo.at[1], v_ext.at[:, halo_to], sems.at[5]))
    return copies


def near_kernel(chunk, u_hbm, v_hbm, h_hbm, q_hbm, near_hbm, far_sums_ref, psi_ref, bal_ref, slopes_ref, g_in_ref, g_ref, late_ref, *rest):
    outs, scratch = rest[:-22], rest[-22:]
    u_ext, v_ext, h_buf, q_buf = scratch[:4]
    work = scratch[4:12]
    m_scr, u_sum, v_sum, sems, out_sems, late_sems = scratch[12:18]
    members, parallels, meridians, levels = u_hbm.shape
    side = 1 - core_index()
    copies = edge_copies(side, u_hbm, v_hbm, h_hbm, q_hbm, near_hbm, u_ext, v_ext, h_buf, q_buf, sems)
    run(copies)
    copies_far = edge_copies(1 - side, u_hbm, v_hbm, h_hbm, q_hbm, None, *scratch[18:22], late_sems)
    run(copies_far)
    g_ref[...] = g_in_ref[...]
    finish(copies)
    compute_rows(EDGE, (parallels - EDGE) * side, (u_ext, v_ext), (h_buf, q_buf), psi_ref, bal_ref, slopes_ref, work, g_ref, m_scr, False, chunk)
    sends = scatter_means(m_scr, outs, 0, out_sems, len(outs))
    run(sends)

    finish(copies_far)
    u_ext, v_ext, h_buf, q_buf = scratch[18:22]
    core = core_index()
    own = 2 * EDGE
    row_from = (parallels - EDGE) * core
    for f, (ext, total) in enumerate(((u_ext, u_sum), (v_ext, v_sum))):
        for r in range(EDGE):
            total[own * core + r] = far_sums_ref[f, r].astype(jnp.float32)
        for r in range(own):
            total[EDGE * (1 - core) + r] = sum(ext[m, EDGE * (1 - core) + r].astype(jnp.float32) for m in range(members))
    for k in range(EDGE):
        work[2][...], work[4][...] = spread_over(row_from + k, psi_ref, bal_ref, slopes_ref[0:1, :], levels)
        for c in range(meridians // chunk):
            at = slice(c * chunk, (c + 1) * chunk)
            du = lat_diff([u_sum[k + e, at] for e in (0, 1, 3, 4)])
            dv = lat_diff([v_sum[k + e, at] for e in (0, 1, 3, 4)])
            work[0][0, at, 0:levels] = du
            work[0][0, at, levels : 2 * levels] = dv
        east = [(pltpu.roll(x[k + EDGE], meridians - 1, 0) - pltpu.roll(x[k + EDGE], 1, 0)) * 6.0 for x in (v_sum, u_sum)]
        work[1][0, :, 0:levels] = east[0]
        work[1][0, :, levels : 2 * levels] = east[1]
        for c in range(meridians // chunk):
            at = slice(c * chunk, (c + 1) * chunk)
            psi = work[2][at]
            curl = psi * (work[1][0, at, 0:levels] - work[0][0, at, 0:levels])
            spread = psi * (work[1][0, at, levels : 2 * levels] + work[0][0, at, levels : 2 * levels])
            heat = sum(h_buf[m, k, at].astype(jnp.float32) for m in range(members)) - work[4][at] * curl
            moist = sum(q_buf[m, k, at].astype(jnp.float32) for m in range(members)) - slopes_ref[1:2, :] * heat
            for f, x in enumerate((curl, spread, heat, moist)):
                late_ref[c, k, :, f * levels : (f + 1) * levels] = (x * (1.0 / members)).astype(jnp.bfloat16)
    late_sends = scatter_means(late_ref, outs, EDGE, late_sems, len(outs))
    run(late_sends)
    finish(sends + late_sends)


def far_kernel(chunk, u_hbm, v_hbm, h_hbm, q_hbm, far_hbm, late_ref, psi_ref, bal_ref, slopes_ref, g_in_ref, g_ref, *scratch):
    u_ext, v_ext, h_buf, q_buf = scratch[:4]
    work = scratch[4:12]
    sems = scratch[12]
    core = core_index()
    copies = edge_copies(core, u_hbm, v_hbm, h_hbm, q_hbm, far_hbm, u_ext, v_ext, h_buf, q_buf, sems)
    run(copies)
    g_ref[...] = g_in_ref[...]
    finish(copies)
    row_from = (u_hbm.shape[1] - EDGE) * core
    compute_rows(EDGE, row_from, (u_ext, v_ext), (h_buf, q_buf), psi_ref, bal_ref, slopes_ref, work, g_ref, late_ref, True, chunk)


def halves_kernel(weight, g_in_ref, mine_ref, theirs_ref, g_ref):
    apart = (mine_ref[...].astype(jnp.float32) - theirs_ref[...].astype(jnp.float32)).astype(jnp.bfloat16)
    apart = apart.reshape(-1, apart.shape[2])
    half = g_ref.shape[0] // 2
    top = g_in_ref[0:half] + gram(apart[:, :half], apart) * weight
    g_ref[0:half] = top
    g_ref[half:, 0:half] = jnp.transpose(top[:, half:])
    g_ref[half:, half:] = g_in_ref[half:, half:] + gram(apart[:, half:], apart[:, half:]) * weight


def row_scratch(dims, n, ext):
    members, _, meridians, levels = dims
    return (
        [pltpu.VMEM((members, ext, meridians, levels), jnp.bfloat16)] * 2
        + [pltpu.VMEM((members, n, meridians, levels), jnp.bfloat16)] * 2
        + [pltpu.VMEM((members, meridians, 2 * levels), jnp.float32)] * 2
        + [pltpu.VMEM((meridians, levels), jnp.float32)] * 4
        + [pltpu.VMEM((members, meridians // 2, 4 * levels), jnp.bfloat16)] * 2
    )


def row_cost(dims, n):
    members, _, meridians, levels = dims
    return cost(4 * n * members * meridians * 16 * levels * levels, 8 << 20)


def between_kernel(members, g_in_ref, *rest):
    parts, (g_ref, mine_ref, theirs_ref) = rest[:-3], rest[-3:]
    side = lax.axis_index("member") % SIDE
    groups = len(parts) // 2
    g_ref[...] = g_in_ref[...]
    first = 0
    for part in (parts[:groups], parts[groups:]):
        _, n, chunk, width = part[0].shape
        overall = sum(p[...].astype(jnp.float32) for p in part) * (1.0 / groups)
        apart = [(p[...].astype(jnp.float32) - overall).astype(jnp.bfloat16).reshape(-1, width) for p in part]
        apart = jnp.concatenate(apart, axis=0)
        half = width // 2
        g_ref[0:half] += gram(apart[:, :half], apart) * float(members)
        g_ref[half:, half:] += gram(apart[:, half:], apart[:, half:]) * float(members)
        overall = overall.astype(jnp.bfloat16)
        low = side == 0
        mine_ref[first : first + n] = jnp.where(low, overall[0], overall[1])
        theirs_ref[first : first + n] = jnp.where(low, overall[1], overall[0])
        first += n


def on_device(u, v, h, q, psi, bal, slope_t, slope_q):
    dims = members, parallels, meridians, levels = u.shape
    width = 4 * levels
    count = lax.axis_size("space")
    peers = lax.axis_size("member")
    groups = peers // SIDE
    chunk = meridians // peers
    inner = parallels - 2 * EDGE
    slopes = jnp.stack([slope_t, slope_q])

    across = [(i, i + 1) for i in range(1, count - 1, 2)]
    across = across + [(b, a) for a, b in across]
    within = [(i, i + 1) for i in range(0, count, 2)]
    within = within + [(b, a) for a, b in within]

    def along_y(r):
        return [(y * SIDE + x, (y + r) % groups * SIDE + x) for y in range(groups) for x in range(SIDE)]

    along_x = [(y * SIDE + x, y * SIDE + 1 - x) for y in range(groups) for x in range(SIDE)]

    far_edge, near_edge, far_sums = edges_call(u, v)
    far_sums = lax.ppermute(far_sums, "space", across)
    far = lax.ppermute(far_edge, "space", across)
    near = lax.ppermute(near_edge, "space", within)

    g_shape = jax.ShapeDtypeStruct((width, width), jnp.float32)
    handed = lambda n: (jax.ShapeDtypeStruct((SIDE, n, chunk, width), jnp.bfloat16),) * groups

    dma = pltpu.SemaphoreType.DMA
    sum_shape = (3 * EDGE, meridians, levels)
    late_shape = jax.ShapeDtypeStruct((peers, EDGE, chunk, width), jnp.bfloat16)
    g, *means = pl.pallas_call(
        functools.partial(inner_kernel, chunk),
        name="inner_rows",
        out_shape=(g_shape,) + handed(inner),
        in_specs=[ANY] * 4 + [VMEM] * 3,
        out_specs=(VMEM,) + (ANY,) * groups,
        scratch_shapes=row_scratch(dims, inner, parallels)
        + [pltpu.VMEM((peers, inner, chunk, width), jnp.bfloat16), dma((4,)), dma((groups,))],
        compiler_params=params(22),
        cost_estimate=row_cost(dims, inner),
    )(u, v, in_hbm(h), in_hbm(q), psi, bal, slopes)
    means = [x if r == 0 else lax.ppermute(x, "member", along_y(r)) for r, x in enumerate(means)]

    g, late, *edge_means = pl.pallas_call(
        functools.partial(near_kernel, chunk),
        name="near_rows",
        out_shape=(g_shape, late_shape) + handed(2 * EDGE),
        in_specs=[ANY] * 5 + [VMEM] * 5,
        out_specs=(VMEM, VMEM) + (ANY,) * groups,
        scratch_shapes=row_scratch(dims, EDGE, 3 * EDGE)
        + [pltpu.VMEM((peers, EDGE, chunk, width), jnp.bfloat16)]
        + [pltpu.VMEM(sum_shape, jnp.float32)] * 2
        + [dma((6,)), dma((groups,)), dma((4,))]
        + row_scratch(dims, EDGE, 3 * EDGE)[:4],
        compiler_params=params(24),
        cost_estimate=row_cost(dims, EDGE),
    )(u, v, h, q, near, far_sums, psi, bal, slopes, g)
    edge_means = [x if r == 0 else lax.ppermute(x, "member", along_y(r)) for r, x in enumerate(edge_means)]

    half = jax.ShapeDtypeStruct((parallels, chunk, width), jnp.bfloat16)
    g, mine, theirs = pl.pallas_call(
        functools.partial(between_kernel, members),
        name="between",
        out_shape=(g_shape, half, half),
        in_specs=[VMEM] * (1 + 2 * groups),
        out_specs=(VMEM, VMEM, VMEM),
        compiler_params=params(16),
        cost_estimate=cost(1 << 30, 5 << 20),
    )(g, *means, *edge_means)
    theirs = lax.ppermute(theirs, "member", along_x)

    g = pl.pallas_call(
        functools.partial(far_kernel, chunk),
        name="far_rows",
        out_shape=g_shape,
        in_specs=[ANY] * 5 + [VMEM] * 5,
        out_specs=VMEM,
        scratch_shapes=row_scratch(dims, EDGE, 3 * EDGE) + [dma((6,))],
        compiler_params=params(16),
        cost_estimate=row_cost(dims, EDGE),
    )(u, v, h, q, far, late, psi, bal, slopes, g)

    g = pl.pallas_call(
        functools.partial(halves_kernel, members * groups / 2.0),
        name="halves",
        out_shape=g_shape,
        in_specs=[VMEM] * 3,
        out_specs=VMEM,
        compiler_params=params(8),
        cost_estimate=cost(1 << 28, 3 << 20),
    )(g, mine, theirs)

    parts = lax.all_to_all(g.reshape(peers, width // peers, width), "member", 0, 0, tiled=True)
    scale = 1.0 / ((members * peers - 1) * parallels * meridians)
    return (jnp.sum(parts, axis=0) * scale)[None]


def solution(mesh):
    placed = (P("member", "space", None, None),) * 4 + (P("space", None),) * 2 + (P(), P())
    return jax.shard_map(
        on_device, mesh=mesh, in_specs=placed, out_specs=P("space", "member", None), check_vma=False
    )
```

time: 101 us -> 105 us (1.040)
  the two profiles are of different devices: /device:TPU:64 before, /device:TPU:2 now
where the time goes in v3:
time: 105 us
  waiting for transfers between devices  35.2 us (34%)
  Pallas kernels  26.2 us (25%)
  starting transfers between devices  22.3 us (21%)
  blocking collectives  19.6 us (19%)
    ppermute x1, waiting for transfers between devices, on_device(): far_sums = lax.ppermute(far_sums, 'space', across)  22.8 us
    all_to_all x1, blocking collectives, on_device(): lax.all_to_all(g.reshape(peers, width // peers, width), 'member', 0, 0, t...  19.6 us
    ppermute x6, waiting for transfers between devices, on_device(): lax.ppermute(x, 'member', along_y(r))  12.2 us
    ppermute x6, starting transfers between devices, on_device(): lax.ppermute(x, 'member', along_y(r))  11.4 us
    pallas_call x1, Pallas kernels, on_device(): pl.pallas_call(functools.partial(inner_kernel, chunk), name='inner_rows',...  11 us
    pallas_call x1, Pallas kernels, on_device(): pl.pallas_call(functools.partial(near_kernel, chunk), name='near_rows', o...  7.32 us
    ppermute x1, starting transfers between devices, on_device(): theirs = lax.ppermute(theirs, 'member', along_x)  4.63 us
    ppermute x1, starting transfers between devices, on_device(): far = lax.ppermute(far_edge, 'space', across)  4.25 us
  transfers between devices with their start and end apart: 10, of which 5 were waited for; matrix products, arithmetic and copies ran while one was open for 0% of the time, Pallas kernels for 23%

profile of v3, /device:TPU:2, one launch (start us, length us, event | category | flops | bytes accessed | tf_op | source)
XLA Modules:
  0.0 104.9 jit_solution(485920605939372440)
XLA Ops:
  0.0 2.0 %edges.1 = (bf16[2,6,2,256,128]{4,3,2,1,0:T(8,128)(2,1)S(1)}, bf16[2,6,2,256,128]{4,3,2,1,0:T(8,128)(2,1)S(1)}, bf16[2,2,256,128]{3,2,1,0:T(8,128)(2,1)S(1)}) custom-call(bf16[6,8,256,128]{3,2,1,0:T(8,128)(2,1)} %u_hbm.7, bf16[6,8,256,128]{3,2,1,0:T(8,128)(2,1)} %v_hbm.7), custom_call_target="tpu_custom_call" | custom-call | flops 1048576 | bytes 6291456 | tf_op jit(solution)/shard_map/edges/pallas_call | solution.py:66
  2.1 0.1 collective-permute-start.1
  2.2 4.3 %collective-permute-start = (bf16[2,6,2,256,128]{4,3,2,1,0:T(8,128)(2,1)S(1)}, bf16[2,6,2,256,128]{4,3,2,1,0:T(8,128)(2,1)S(1)}, u32[]{:S(2)}, u32[]{:S(2)}) collective-permute-start(bf16[2,6,2,256,128]{4,3,2,1,0:T(8,128)(2,1)S(1)} %get-tuple-element.22), channel_id=1, source_target_pairs={{1,2},{3,4},{5,6},{7,8},{9,10},{11,12},{13,14},{15,16},{17,18},{19... | collective-permute-start | bytes 4718600 | tf_op jit(solution)/shard_map/ppermute | solution.py:349
  6.4 1.9 %collective-permute-start.2 = (bf16[2,2,256,128]{3,2,1,0:T(8,128)(2,1)S(1)}, bf16[2,2,256,128]{3,2,1,0:T(8,128)(2,1)S(1)}, u32[]{:S(2)}, u32[]{:S(2)}) collective-permute-start(bf16[2,2,256,128]{3,2,1,0:T(8,128)(2,1)S(1)} %get-tuple-element.24), channel_id=1, source_target_pairs={{1,2},{3,4},{5,6},{7,8},{9,10},{11,12},{13,14},{15,16},{17,18},{19... | collective-permute-start | bytes 786440 | tf_op jit(solution)/shard_map/ppermute | solution.py:348
  8.4 0.7 copy-done.5
  9.1 11.0 %inner_rows.1 = (f32[512,512]{1,0:T(8,128)S(1)}, bf16[2,4,32,512]{3,2,1,0:T(8,128)(2,1)S(1)}, bf16[2,4,32,512]{3,2,1,0:T(8,128)(2,1)S(1)}, bf16[2,4,32,512]{3,2,...) custom-call(bf16[6,8,256,128]{3,2,1,0:T(8,128)(2,1)S(1)} %copy-done, bf16[6,8,256,128]{3,2,1,0:T(8,128)(2,1)S(1)} %copy-done.1, ...), custom_call_target="tpu_custom_call" | custom-call | flops 6442450944 | bytes 8388608 | tf_op jit(solution)/shard_map/inner_rows/pallas_call | solution.py:358
  20.1 1.2 %collective-permute-start.3 = (bf16[2,4,32,512]{3,2,1,0:T(8,128)(2,1)S(1)}, bf16[2,4,32,512]{3,2,1,0:T(8,128)(2,1)S(1)}, u32[]{:S(2)}, u32[]{:S(2)}) collective-permute-start(bf16[2,4,32,512]{3,2,1,0:T(8,128)(2,1)S(1)} %get-tuple-element.29), channel_id=1, source_target_pairs={{0,64},{32,96},{64,128},{96,160},{128,192},{160,224},{192,0},{224,... | collective-permute-start | bytes 786440 | tf_op jit(solution)/shard_map/ppermute | solution.py:369
  21.3 2.9 %collective-permute-start.4 = (bf16[2,4,32,512]{3,2,1,0:T(8,128)(2,1)S(1)}, bf16[2,4,32,512]{3,2,1,0:T(8,128)(2,1)S(1)}, u32[]{:S(2)}, u32[]{:S(2)}) collective-permute-start(bf16[2,4,32,512]{3,2,1,0:T(8,128)(2,1)S(1)} %get-tuple-element.30), channel_id=1, source_target_pairs={{0,128},{32,160},{64,192},{96,224},{128,0},{160,32},{192,64},{224,... | collective-permute-start | bytes 786440 | tf_op jit(solution)/shard_map/ppermute | solution.py:369
  24.2 22.8 %collective-permute-done.2.far_sums_ref = bf16[2,2,256,128]{3,2,1,0:T(8,128)(2,1)S(1)} collective-permute-done((bf16[2,2,256,128]{3,2,1,0:T(8,128)(2,1)S(1)}, bf16[2,2,256,128]{3,2,1,0:T(8,128)(2,1)S(1)}, u32[]{:S(2)}, u32[]{:S(2)}) %collective-permute-start.2) | collective-permute-done | bytes 262176 | tf_op jit(solution)/shard_map/ppermute | solution.py:348
  47.0 2.5 %collective-permute-start.5 = (bf16[2,4,32,512]{3,2,1,0:T(8,128)(2,1)S(1)}, bf16[2,4,32,512]{3,2,1,0:T(8,128)(2,1)S(1)}, u32[]{:S(2)}, u32[]{:S(2)}) collective-permute-start(bf16[2,4,32,512]{3,2,1,0:T(8,128)(2,1)S(1)} %get-tuple-element.31), channel_id=1, source_target_pairs={{0,192},{32,224},{64,0},{96,32},{128,64},{160,96},{192,128},{224,1... | collective-permute-start | bytes 786440 | tf_op jit(solution)/shard_map/ppermute | solution.py:369
  49.5 7.3 %near_rows.1 = (f32[512,512]{1,0:T(8,128)S(1)}, bf16[8,2,32,512]{3,2,1,0:T(8,128)(2,1)S(1)}, bf16[2,4,32,512]{3,2,1,0:T(8,128)(2,1)S(1)}, bf16[2,4,32,512]{3,2,1...) custom-call(bf16[6,8,256,128]{3,2,1,0:T(8,128)(2,1)S(1)} %copy-done, ...), custom_call_target="tpu_custom_call" | custom-call | flops 3221225472 | bytes 8388608 | tf_op jit(solution)/shard_map/near_rows/pallas_call | solution.py:371
  56.9 0.1 collective-permute-start.6
  57.0 4.1 %collective-permute-start.7 = (bf16[2,4,32,512]{3,2,1,0:T(8,128)(2,1)S(1)}, bf16[2,4,32,512]{3,2,1,0:T(8,128)(2,1)S(1)}, u32[]{:S(2)}, u32[]{:S(2)}) collective-permute-start(bf16[2,4,32,512]{3,2,1,0:T(8,128)(2,1)S(1)} %get-tuple-element.34), channel_id=1, source_target_pairs={{0,128},{32,160},{64,192},{96,224},{128,0},{160,32},{192,64},{224,... | collective-permute-start | bytes 786440 | tf_op jit(solution)/shard_map/ppermute | solution.py:385
  61.1 0.6 collective-permute-start.8
  61.7 2.9 %collective-permute-done.6.rest_5_ = bf16[2,4,32,512]{3,2,1,0:T(8,128)(2,1)S(1)} collective-permute-done((bf16[2,4,32,512]{3,2,1,0:T(8,128)(2,1)S(1)}, bf16[2,4,32,512]{3,2,1,0:T(8,128)(2,1)S(1)}, u32[]{:S(2)}, u32[]{:S(2)}) %collective-permute-start.6) | collective-permute-done | bytes 262176 | tf_op jit(solution)/shard_map/ppermute | solution.py:385
  64.5 6.0 %collective-permute-done.7.rest_6_ = bf16[2,4,32,512]{3,2,1,0:T(8,128)(2,1)S(1)} collective-permute-done((bf16[2,4,32,512]{3,2,1,0:T(8,128)(2,1)S(1)}, bf16[2,4,32,512]{3,2,1,0:T(8,128)(2,1)S(1)}, u32[]{:S(2)}, u32[]{:S(2)}) %collective-permute-start.7) | collective-permute-done | bytes 262176 | tf_op jit(solution)/shard_map/ppermute | solution.py:385
  70.5 3.3 %collective-permute-done.8.rest_7_ = bf16[2,4,32,512]{3,2,1,0:T(8,128)(2,1)S(1)} collective-permute-done((bf16[2,4,32,512]{3,2,1,0:T(8,128)(2,1)S(1)}, bf16[2,4,32,512]{3,2,1,0:T(8,128)(2,1)S(1)}, u32[]{:S(2)}, u32[]{:S(2)}) %collective-permute-start.8) | collective-permute-done | bytes 262176 | tf_op jit(solution)/shard_map/ppermute | solution.py:385
  73.8 1.4 %between.1 = (f32[512,512]{1,0:T(8,128)S(1)}, bf16[8,32,512]{2,1,0:T(8,128)(2,1)S(1)}, bf16[8,32,512]{2,1,0:T(8,128)(2,1)S(1)}) custom-call(f32[512,512]{1,0:T(8,128)S(1)} %get-tuple-element.27.g_in_ref, bf16[2,4,32,512]{3,2,1,0:T(8,128)(2,1)S(1)} %get-tuple-element.28.rest_0_, bf16[2,4,32,512]{3,2,1,0:T(8,128)(2,1)S(1)} %collective-permute-done.3.rest_1_, ...), custom_call_target="tpu_custom_call" | custom-call | flops 1073741824 | bytes 5242880 | tf_op jit(solution)/shard_map/between/pallas_call | solution.py:388
  75.2 4.6 %collective-permute-start.9 = (bf16[8,32,512]{2,1,0:T(8,128)(2,1)S(1)}, bf16[8,32,512]{2,1,0:T(8,128)(2,1)S(1)}, u32[]{:S(2)}, u32[]{:S(2)}) collective-permute-start(bf16[8,32,512]{2,1,0:T(8,128)(2,1)S(1)} %get-tuple-element.38), channel_id=1, source_target_pairs={{0,32},{32,0},{64,96},{96,64},{128,160},{160,128},{192,224},{224,1... | collective-permute-start | bytes 786440 | tf_op jit(solution)/shard_map/ppermute | solution.py:397
  79.9 4.1 %far_rows.1.g_in_ref = f32[512,512]{1,0:T(8,128)S(1)} custom-call(bf16[6,8,256,128]{3,2,1,0:T(8,128)(2,1)S(1)} %copy-done, bf16[6,8,256,128]{3,2,1,0:T(8,128)(2,1)S(1)} %copy-done.1, bf16[6,8,256,128]{3,2,1,0:T(8,128)(2,1)S(1)} %copy-done.2, bf16[6,8,256,128]{3,2,1,0:T(8,128)(2,1)S(1)} %copy-done.3, ...), custom_call_target="tpu_custom_call" | custom-call | flops 3221225472 | bytes 8388608 | tf_op jit(solution)/shard_map/far_rows/pallas_call | solution.py:399
  84.0 0.2 collective-permute-done.9.theirs_ref
  84.2 0.4 halves.1
  84.6 19.6 %all_to_all.5 = f32[8,64,512]{2,1,0:T(8,128)S(1)} all-to-all(f32[8,64,512]{2,1,0:T(8,128)S(1)} %bitcast.5), channel_id=1, replica_groups=mesh['member'=8,'space'=32] {'member'}, dimensions={0} | all-to-all | bytes 2097152 | tf_op jit(solution)/shard_map/all_to_all | solution.py:420
  104.2 0.7 multiply_bitcast_fusion
  (24 shorter events, 0.1 us)
Async XLA Ops:
  0.0 8.4 %copy-start.1 = (bf16[6,8,256,128]{3,2,1,0:T(8,128)(2,1)S(1)}, bf16[6,8,256,128]{3,2,1,0:T(8,128)(2,1)}, u32[]{:S(2)}) copy-start(bf16[6,8,256,128]{3,2,1,0:T(8,128)(2,1)} %v_hbm.7) | copy-start | bytes 9437188
  0.0 8.4 %copy-start = (bf16[6,8,256,128]{3,2,1,0:T(8,128)(2,1)S(1)}, bf16[6,8,256,128]{3,2,1,0:T(8,128)(2,1)}, u32[]{:S(2)}) copy-start(bf16[6,8,256,128]{3,2,1,0:T(8,128)(2,1)} %u_hbm.7) | copy-start | bytes 9437188
  0.0 8.4 %copy-start.7 = (f32[128]{0:T(128)S(1)}, f32[128]{0:T(128)}, u32[]{:S(2)}) copy-start(f32[128]{0:T(128)} %param.15) | copy-start | bytes 1540
  0.0 8.4 %copy-start.8 = (f32[128]{0:T(128)S(1)}, f32[128]{0:T(128)}, u32[]{:S(2)}) copy-start(f32[128]{0:T(128)} %param.14) | copy-start | bytes 1540
  0.0 8.4 %copy-start.4 = (f32[8,256]{1,0:T(8,128)S(1)}, f32[8,256]{1,0:T(8,128)}, u32[]{:S(2)}) copy-start(f32[8,256]{1,0:T(8,128)} %psi_ref.5) | copy-start | bytes 24580
  2.1 47.5 %collective-permute-start.1 = (bf16[2,6,2,256,128]{4,3,2,1,0:T(8,128)(2,1)S(1)}, bf16[2,6,2,256,128]{4,3,2,1,0:T(8,128)(2,1)S(1)}, u32[]{:S(2)}, u32[]{:S(2)}) collective-permute-start(bf16[2,6,2,256,128]{4,3,2,1,0:T(8,128)(2,1)S(1)} %get-tuple-element.23), channel_id=1, source_target_pairs={{0,1},{2,3},{4,5},{6,7},{8,9},{10,11},{12,13},{14,15},{16,17},{18,... | collective-permute-start | bytes 4718600 | tf_op jit(solution)/shard_map/ppermute | solution.py:350
  2.2 77.7 %collective-permute-start = (bf16[2,6,2,256,128]{4,3,2,1,0:T(8,128)(2,1)S(1)}, bf16[2,6,2,256,128]{4,3,2,1,0:T(8,128)(2,1)S(1)}, u32[]{:S(2)}, u32[]{:S(2)}) collective-permute-start(bf16[2,6,2,256,128]{4,3,2,1,0:T(8,128)(2,1)S(1)} %get-tuple-element.22), channel_id=1, source_target_pairs={{1,2},{3,4},{5,6},{7,8},{9,10},{11,12},{13,14},{15,16},{17,18},{19... | collective-permute-start | bytes 4718600 | tf_op jit(solution)/shard_map/ppermute | solution.py:349
  6.4 40.6 %collective-permute-start.2 = (bf16[2,2,256,128]{3,2,1,0:T(8,128)(2,1)S(1)}, bf16[2,2,256,128]{3,2,1,0:T(8,128)(2,1)S(1)}, u32[]{:S(2)}, u32[]{:S(2)}) collective-permute-start(bf16[2,2,256,128]{3,2,1,0:T(8,128)(2,1)S(1)} %get-tuple-element.24), channel_id=1, source_target_pairs={{1,2},{3,4},{5,6},{7,8},{9,10},{11,12},{13,14},{15,16},{17,18},{19... | collective-permute-start | bytes 786440 | tf_op jit(solution)/shard_map/ppermute | solution.py:348
  8.4 0.7 copy-start.5
  9.1 40.4 %copy-start.2 = (bf16[6,8,256,128]{3,2,1,0:T(8,128)(2,1)S(1)}, bf16[6,8,256,128]{3,2,1,0:T(8,128)(2,1)}, u32[]{:S(2)}) copy-start(bf16[6,8,256,128]{3,2,1,0:T(8,128)(2,1)} %h_hbm.5) | copy-start | bytes 9437188
  9.1 40.4 %copy-start.3 = (bf16[6,8,256,128]{3,2,1,0:T(8,128)(2,1)S(1)}, bf16[6,8,256,128]{3,2,1,0:T(8,128)(2,1)}, u32[]{:S(2)}) copy-start(bf16[6,8,256,128]{3,2,1,0:T(8,128)(2,1)} %q_hbm.5) | copy-start | bytes 9437188
  20.1 36.8 %collective-permute-start.3 = (bf16[2,4,32,512]{3,2,1,0:T(8,128)(2,1)S(1)}, bf16[2,4,32,512]{3,2,1,0:T(8,128)(2,1)S(1)}, u32[]{:S(2)}, u32[]{:S(2)}) collective-permute-start(bf16[2,4,32,512]{3,2,1,0:T(8,128)(2,1)S(1)} %get-tuple-element.29), channel_id=1, source_target_pairs={{0,64},{32,96},{64,128},{96,160},{128,192},{160,224},{192,0},{224,... | collective-permute-start | bytes 786440 | tf_op jit(solution)/shard_map/ppermute | solution.py:369
  21.3 39.7 %collective-permute-start.4 = (bf16[2,4,32,512]{3,2,1,0:T(8,128)(2,1)S(1)}, bf16[2,4,32,512]{3,2,1,0:T(8,128)(2,1)S(1)}, u32[]{:S(2)}, u32[]{:S(2)}) collective-permute-start(bf16[2,4,32,512]{3,2,1,0:T(8,128)(2,1)S(1)} %get-tuple-element.30), channel_id=1, source_target_pairs={{0,128},{32,160},{64,192},{96,224},{128,0},{160,32},{192,64},{224,... | collective-permute-start | bytes 786440 | tf_op jit(solution)/shard_map/ppermute | solution.py:369
  47.0 14.7 %collective-permute-start.5 = (bf16[2,4,32,512]{3,2,1,0:T(8,128)(2,1)S(1)}, bf16[2,4,32,512]{3,2,1,0:T(8,128)(2,1)S(1)}, u32[]{:S(2)}, u32[]{:S(2)}) collective-permute-start(bf16[2,4,32,512]{3,2,1,0:T(8,128)(2,1)S(1)} %get-tuple-element.31), channel_id=1, source_target_pairs={{0,192},{32,224},{64,0},{96,32},{128,64},{160,96},{192,128},{224,1... | collective-permute-start | bytes 786440 | tf_op jit(solution)/shard_map/ppermute | solution.py:369
  56.9 23.0 %copy-start.6 = (f32[8,256]{1,0:T(8,128)S(1)}, f32[8,256]{1,0:T(8,128)}, u32[]{:S(2)}) copy-start(f32[8,256]{1,0:T(8,128)} %bal_ref.5) | copy-start | bytes 24580
  56.9 7.7 %collective-permute-start.6 = (bf16[2,4,32,512]{3,2,1,0:T(8,128)(2,1)S(1)}, bf16[2,4,32,512]{3,2,1,0:T(8,128)(2,1)S(1)}, u32[]{:S(2)}, u32[]{:S(2)}) collective-permute-start(bf16[2,4,32,512]{3,2,1,0:T(8,128)(2,1)S(1)} %get-tuple-element.33), channel_id=1, source_target_pairs={{0,64},{32,96},{64,128},{96,160},{128,192},{160,224},{192,0},{224,... | collective-permute-start | bytes 786440 | tf_op jit(solution)/shard_map/ppermute | solution.py:385
  57.0 13.5 %collective-permute-start.7 = (bf16[2,4,32,512]{3,2,1,0:T(8,128)(2,1)S(1)}, bf16[2,4,32,512]{3,2,1,0:T(8,128)(2,1)S(1)}, u32[]{:S(2)}, u32[]{:S(2)}) collective-permute-start(bf16[2,4,32,512]{3,2,1,0:T(8,128)(2,1)S(1)} %get-tuple-element.34), channel_id=1, source_target_pairs={{0,128},{32,160},{64,192},{96,224},{128,0},{160,32},{192,64},{224,... | collective-permute-start | bytes 786440 | tf_op jit(solution)/shard_map/ppermute | solution.py:385
  61.1 12.8 %collective-permute-start.8 = (bf16[2,4,32,512]{3,2,1,0:T(8,128)(2,1)S(1)}, bf16[2,4,32,512]{3,2,1,0:T(8,128)(2,1)S(1)}, u32[]{:S(2)}, u32[]{:S(2)}) collective-permute-start(bf16[2,4,32,512]{3,2,1,0:T(8,128)(2,1)S(1)} %get-tuple-element.35), channel_id=1, source_target_pairs={{0,192},{32,224},{64,0},{96,32},{128,64},{160,96},{192,128},{224,1... | collective-permute-start | bytes 786440 | tf_op jit(solution)/shard_map/ppermute | solution.py:385
  75.2 9.0 %collective-permute-start.9 = (bf16[8,32,512]{2,1,0:T(8,128)(2,1)S(1)}, bf16[8,32,512]{2,1,0:T(8,128)(2,1)S(1)}, u32[]{:S(2)}, u32[]{:S(2)}) collective-permute-start(bf16[8,32,512]{2,1,0:T(8,128)(2,1)S(1)} %get-tuple-element.38), channel_id=1, source_target_pairs={{0,32},{32,0},{64,96},{96,64},{128,160},{160,128},{192,224},{224,1... | collective-permute-start | bytes 786440 | tf_op jit(solution)/shard_map/ppermute | solution.py:397

commit v4 on v3

--- a/solution.py
+++ b/solution.py
@@ -43,36 +43,54 @@
         copy.wait()
 
 
-def edges_kernel(parallels, u_hbm, v_hbm, far_ref, near_ref, sums_ref, sems):
+def sums_kernel(u_hbm, v_hbm, sums_ref, rows, sems):
+    at = pl.ds((u_hbm.shape[1] - EDGE) * core_index(), EDGE)
+    copies = [pltpu.make_async_copy(x.at[:, at], rows.at[f], sems.at[f]) for f, x in enumerate((u_hbm, v_hbm))]
+    run(copies)
+    for f, copy in enumerate(copies):
+        copy.wait()
+        for r in range(EDGE):
+            total = rows[f, 0, r].astype(jnp.float32)
+            for m in range(1, rows.shape[1]):
+                total = total + rows[f, m, r].astype(jnp.float32)
+            sums_ref[f, r] = total.astype(jnp.bfloat16)
+
+
+def edges_kernel(u_hbm, v_hbm, sums_hbm, far_ref, near_ref, sems):
+    del sums_hbm
     core = core_index()
-    far_at = pl.ds((parallels - EDGE) * core, EDGE)
-    near_at = pl.ds((parallels - EDGE) * (1 - core), EDGE)
-    far = [pltpu.make_async_copy(x.at[:, far_at], far_ref.at[f], sems.at[f]) for f, x in enumerate((u_hbm, v_hbm))]
-    near = [pltpu.make_async_copy(x.at[:, near_at], near_ref.at[f], sems.at[2 + f]) for f, x in enumerate((u_hbm, v_hbm))]
-    run(far + near)
-    for f in range(2):
-        far[f].wait()
-        for r in range(EDGE):
-            total = far_ref[f, 0, r].astype(jnp.float32)
-            for m in range(1, far_ref.shape[1]):
-                total = total + far_ref[f, m, r].astype(jnp.float32)
-            sums_ref[f, r] = total.astype(jnp.bfloat16)
-    finish(near)
+    far_at = pl.ds((u_hbm.shape[1] - EDGE) * core, EDGE)
+    near_at = pl.ds((u_hbm.shape[1] - EDGE) * (1 - core), EDGE)
+    copies = [pltpu.make_async_copy(x.at[:, far_at], far_ref.at[f], sems.at[f]) for f, x in enumerate((u_hbm, v_hbm))]
+    copies += [pltpu.make_async_copy(x.at[:, near_at], near_ref.at[f], sems.at[2 + f]) for f, x in enumerate((u_hbm, v_hbm))]
+    run(copies)
+    finish(copies)
 
 
 def edges_call(u, v):
-    members, parallels, meridians, levels = u.shape
+    members, _, meridians, levels = u.shape
     edge = jax.ShapeDtypeStruct((2, members, EDGE, meridians, levels), u.dtype)
-    return pl.pallas_call(
-        functools.partial(edges_kernel, parallels),
+    sums = pl.pallas_call(
+        sums_kernel,
+        name="edge_sums",
+        out_shape=jax.ShapeDtypeStruct((2, EDGE, meridians, levels), u.dtype),
+        in_specs=[ANY, ANY],
+        out_specs=VMEM,
+        scratch_shapes=[pltpu.VMEM(edge.shape, u.dtype), pltpu.SemaphoreType.DMA((2,))],
+        compiler_params=params(8),
+        cost_estimate=cost(1 << 20, 3 << 20),
+    )(in_hbm(u), in_hbm(v))
+    far, near = pl.pallas_call(
+        edges_kernel,
         name="edges",
-        out_shape=(edge, edge, jax.ShapeDtypeStruct((2, EDGE, meridians, levels), u.dtype)),
-        in_specs=[ANY, ANY],
-        out_specs=(VMEM, VMEM, VMEM),
+        out_shape=(edge, edge),
+        in_specs=[ANY, ANY, ANY],
+        out_specs=(VMEM, VMEM),
         scratch_shapes=[pltpu.SemaphoreType.DMA((4,))],
-        compiler_params=params(50),
+        compiler_params=params(8),
         cost_estimate=cost(1 << 20, 6 << 20),
-    )(u, v)
+    )(in_hbm(u), in_hbm(v), sums)
+    return far, near, sums
 
 
 def spread_over(at, psi_ref, bal_ref, slope_t, levels):
@@ -300,7 +318,7 @@
 
 def row_cost(dims, n):
     members, _, meridians, levels = dims
-    return cost(4 * n * members * meridians * 16 * levels * levels, 8 << 20)
+    return cost(16 * n * members * meridians * 16 * levels * levels, 32 << 20)
 
 
 def between_kernel(members, g_in_ref, *rest):

time: 105 us -> 87.5 us (0.83)
  the two profiles are of different devices: /device:TPU:2 before, /device:TPU:96 now
where the time goes in v4:
time: 87.5 us; the launch traced here: 87.3 us
  Pallas kernels  27.5 us (31%)
  blocking collectives  24.5 us (28%)
  starting transfers between devices  20.4 us (23%)
  waiting for transfers between devices  13.8 us (16%)
    all_to_all x1, blocking collectives, on_device(): lax.all_to_all(g.reshape(peers, width // peers, width), 'member', 0, 0, t...  24.5 us
    pallas_call x1, Pallas kernels, on_device(): pl.pallas_call(functools.partial(inner_kernel, chunk), name='inner_rows',...  11 us
    ppermute x6, waiting for transfers between devices, on_device(): lax.ppermute(x, 'member', along_y(r))  10.8 us
    ppermute x6, starting transfers between devices, on_device(): lax.ppermute(x, 'member', along_y(r))  10.2 us
    pallas_call x1, Pallas kernels, on_device(): pl.pallas_call(functools.partial(near_kernel, chunk), name='near_rows', o...  7.32 us
    pallas_call x1, Pallas kernels, on_device(): pl.pallas_call(functools.partial(far_kernel, chunk), name='far_rows', out...  4.1 us
    ppermute x1, starting transfers between devices, on_device(): far = lax.ppermute(far_edge, 'space', across)  4.08 us
    ppermute x1, starting transfers between devices, on_device(): theirs = lax.ppermute(theirs, 'member', along_x)  3.38 us
  transfers between devices with their start and end apart: 10, of which 3 were waited for; matrix products, arithmetic and copies ran while one was open for 0% of the time, Pallas kernels for 29%

profile of v4, /device:TPU:96, one launch (start us, length us, event | category | flops | bytes accessed | tf_op | source)
XLA Modules:
  0.0 87.3 jit_solution(4221998318246967022)
XLA Ops:
  0.0 1.5 %edge_sums.1.sums_hbm = bf16[2,2,256,128]{3,2,1,0:T(8,128)(2,1)S(1)} custom-call(bf16[6,8,256,128]{3,2,1,0:T(8,128)(2,1)} %u_hbm.9, bf16[6,8,256,128]{3,2,1,0:T(8,128)(2,1)} %v_hbm.9), custom_call_target="tpu_custom_call" | custom-call | flops 1048576 | bytes 3145728 | tf_op jit(solution)/shard_map/edge_sums/pallas_call | solution.py:73
  1.5 0.0 copy-start.6
  1.5 0.0 copy-start.1
  1.6 2.6 %collective-permute-start.2 = (bf16[2,2,256,128]{3,2,1,0:T(8,128)(2,1)S(1)}, bf16[2,2,256,128]{3,2,1,0:T(8,128)(2,1)S(1)}, u32[]{:S(2)}, u32[]{:S(2)}) collective-permute-start(bf16[2,2,256,128]{3,2,1,0:T(8,128)(2,1)S(1)} %edge_sums.1.sums_hbm), channel_id=1, source_target_pairs={{1,2},{3,4},{5,6},{7,8},{9,10},{11,12},{13,14},{15,16},{17,18},{19... | collective-permute-start | bytes 786440 | tf_op jit(solution)/shard_map/ppermute | solution.py:366
  4.2 1.9 %edges.1 = (bf16[2,6,2,256,128]{4,3,2,1,0:T(8,128)(2,1)S(1)}, bf16[2,6,2,256,128]{4,3,2,1,0:T(8,128)(2,1)S(1)}) custom-call(bf16[6,8,256,128]{3,2,1,0:T(8,128)(2,1)} %u_hbm.9, bf16[6,8,256,128]{3,2,1,0:T(8,128)(2,1)} %v_hbm.9, bf16[2,2,256,128]{3,2,1,0:T(8,128)(2,1)S(1)} %edge_sums.1.sums_hbm), custom_call_target="tpu_custom_call" | custom-call | flops 1048576 | bytes 6291456 | tf_op jit(solution)/shard_map/edges/pallas_call | solution.py:83
  6.1 4.1 %collective-permute-start = (bf16[2,6,2,256,128]{4,3,2,1,0:T(8,128)(2,1)S(1)}, bf16[2,6,2,256,128]{4,3,2,1,0:T(8,128)(2,1)S(1)}, u32[]{:S(2)}, u32[]{:S(2)}) collective-permute-start(bf16[2,6,2,256,128]{4,3,2,1,0:T(8,128)(2,1)S(1)} %get-tuple-element.21), channel_id=1, source_target_pairs={{1,2},{3,4},{5,6},{7,8},{9,10},{11,12},{13,14},{15,16},{17,18},{19... | collective-permute-start | bytes 4718600 | tf_op jit(solution)/shard_map/ppermute | solution.py:367
  10.2 0.1 collective-permute-start.1
  10.4 11.0 %inner_rows.1 = (f32[512,512]{1,0:T(8,128)S(1)}, bf16[2,4,32,512]{3,2,1,0:T(8,128)(2,1)S(1)}, bf16[2,4,32,512]{3,2,1,0:T(8,128)(2,1)S(1)}, bf16[2,4,32,512]{3,2,...) custom-call(bf16[6,8,256,128]{3,2,1,0:T(8,128)(2,1)S(1)} %copy-done, bf16[6,8,256,128]{3,2,1,0:T(8,128)(2,1)S(1)} %copy-done.1, ...), custom_call_target="tpu_custom_call" | custom-call | flops 25769803776 | bytes 33554432 | tf_op jit(solution)/shard_map/inner_rows/pallas_call | solution.py:376
  21.4 1.7 %collective-permute-start.3 = (bf16[2,4,32,512]{3,2,1,0:T(8,128)(2,1)S(1)}, bf16[2,4,32,512]{3,2,1,0:T(8,128)(2,1)S(1)}, u32[]{:S(2)}, u32[]{:S(2)}) collective-permute-start(bf16[2,4,32,512]{3,2,1,0:T(8,128)(2,1)S(1)} %get-tuple-element.27), channel_id=1, source_target_pairs={{0,64},{32,96},{64,128},{96,160},{128,192},{160,224},{192,0},{224,... | collective-permute-start | bytes 786440 | tf_op jit(solution)/shard_map/ppermute | solution.py:387
  23.1 2.9 %collective-permute-start.4 = (bf16[2,4,32,512]{3,2,1,0:T(8,128)(2,1)S(1)}, bf16[2,4,32,512]{3,2,1,0:T(8,128)(2,1)S(1)}, u32[]{:S(2)}, u32[]{:S(2)}) collective-permute-start(bf16[2,4,32,512]{3,2,1,0:T(8,128)(2,1)S(1)} %get-tuple-element.28), channel_id=1, source_target_pairs={{0,128},{32,160},{64,192},{96,224},{128,0},{160,32},{192,64},{224,... | collective-permute-start | bytes 786440 | tf_op jit(solution)/shard_map/ppermute | solution.py:387
  26.0 1.3 %collective-permute-start.5 = (bf16[2,4,32,512]{3,2,1,0:T(8,128)(2,1)S(1)}, bf16[2,4,32,512]{3,2,1,0:T(8,128)(2,1)S(1)}, u32[]{:S(2)}, u32[]{:S(2)}) collective-permute-start(bf16[2,4,32,512]{3,2,1,0:T(8,128)(2,1)S(1)} %get-tuple-element.29), channel_id=1, source_target_pairs={{0,192},{32,224},{64,0},{96,32},{128,64},{160,96},{192,128},{224,1... | collective-permute-start | bytes 786440 | tf_op jit(solution)/shard_map/ppermute | solution.py:387
  27.3 7.3 %near_rows.1 = (f32[512,512]{1,0:T(8,128)S(1)}, bf16[8,2,32,512]{3,2,1,0:T(8,128)(2,1)S(1)}, bf16[2,4,32,512]{3,2,1,0:T(8,128)(2,1)S(1)}, bf16[2,4,32,512]{3,2,1...) custom-call(bf16[6,8,256,128]{3,2,1,0:T(8,128)(2,1)S(1)} %copy-done, ...), custom_call_target="tpu_custom_call" | custom-call | flops 12884901888 | bytes 33554432 | tf_op jit(solution)/shard_map/near_rows/pallas_call | solution.py:389
  34.7 0.8 collective-permute-start.6
  35.4 3.6 %collective-permute-start.7 = (bf16[2,4,32,512]{3,2,1,0:T(8,128)(2,1)S(1)}, bf16[2,4,32,512]{3,2,1,0:T(8,128)(2,1)S(1)}, u32[]{:S(2)}, u32[]{:S(2)}) collective-permute-start(bf16[2,4,32,512]{3,2,1,0:T(8,128)(2,1)S(1)} %get-tuple-element.32), channel_id=1, source_target_pairs={{0,128},{32,160},{64,192},{96,224},{128,0},{160,32},{192,64},{224,... | collective-permute-start | bytes 786440 | tf_op jit(solution)/shard_map/ppermute | solution.py:403
  39.0 6.8 %collective-permute-done.6.rest_5_ = bf16[2,4,32,512]{3,2,1,0:T(8,128)(2,1)S(1)} collective-permute-done((bf16[2,4,32,512]{3,2,1,0:T(8,128)(2,1)S(1)}, bf16[2,4,32,512]{3,2,1,0:T(8,128)(2,1)S(1)}, u32[]{:S(2)}, u32[]{:S(2)}) %collective-permute-start.6) | collective-permute-done | bytes 262176 | tf_op jit(solution)/shard_map/ppermute | solution.py:403
  45.8 4.1 %collective-permute-done.8.rest_7_ = bf16[2,4,32,512]{3,2,1,0:T(8,128)(2,1)S(1)} collective-permute-done((bf16[2,4,32,512]{3,2,1,0:T(8,128)(2,1)S(1)}, bf16[2,4,32,512]{3,2,1,0:T(8,128)(2,1)S(1)}, u32[]{:S(2)}, u32[]{:S(2)}) %collective-permute-start.8) | collective-permute-done | bytes 262176 | tf_op jit(solution)/shard_map/ppermute | solution.py:403
  49.9 1.4 %between.1 = (f32[512,512]{1,0:T(8,128)S(1)}, bf16[8,32,512]{2,1,0:T(8,128)(2,1)S(1)}, bf16[8,32,512]{2,1,0:T(8,128)(2,1)S(1)}) custom-call(f32[512,512]{1,0:T(8,128)S(1)} %get-tuple-element.25.g_in_ref, bf16[2,4,32,512]{3,2,1,0:T(8,128)(2,1)S(1)} %get-tuple-element.26.rest_0_, bf16[2,4,32,512]{3,2,1,0:T(8,128)(2,1)S(1)} %collective-permute-done.3.rest_1_, ...), custom_call_target="tpu_custom_call" | custom-call | flops 1073741824 | bytes 5242880 | tf_op jit(solution)/shard_map/between/pallas_call | solution.py:406
  51.3 3.4 %collective-permute-start.9 = (bf16[8,32,512]{2,1,0:T(8,128)(2,1)S(1)}, bf16[8,32,512]{2,1,0:T(8,128)(2,1)S(1)}, u32[]{:S(2)}, u32[]{:S(2)}) collective-permute-start(bf16[8,32,512]{2,1,0:T(8,128)(2,1)S(1)} %get-tuple-element.36), channel_id=1, source_target_pairs={{0,32},{32,0},{64,96},{96,64},{128,160},{160,128},{192,224},{224,1... | collective-permute-start | bytes 786440 | tf_op jit(solution)/shard_map/ppermute | solution.py:415
  54.6 4.1 %far_rows.1.g_in_ref = f32[512,512]{1,0:T(8,128)S(1)} custom-call(bf16[6,8,256,128]{3,2,1,0:T(8,128)(2,1)S(1)} %copy-done, bf16[6,8,256,128]{3,2,1,0:T(8,128)(2,1)S(1)} %copy-done.1, bf16[6,8,256,128]{3,2,1,0:T(8,128)(2,1)S(1)} %copy-done.2, bf16[6,8,256,128]{3,2,1,0:T(8,128)(2,1)S(1)} %copy-done.3, ...), custom_call_target="tpu_custom_call" | custom-call | flops 12884901888 | bytes 33554432 | tf_op jit(solution)/shard_map/far_rows/pallas_call | solution.py:417
  58.7 2.9 %collective-permute-done.9.theirs_ref = bf16[8,32,512]{2,1,0:T(8,128)(2,1)S(1)} collective-permute-done((bf16[8,32,512]{2,1,0:T(8,128)(2,1)S(1)}, bf16[8,32,512]{2,1,0:T(8,128)(2,1)S(1)}, u32[]{:S(2)}, u32[]{:S(2)}) %collective-permute-start.9) | collective-permute-done | bytes 262176 | tf_op jit(solution)/shard_map/ppermute | solution.py:415
  61.6 0.4 halves.1
  62.0 24.5 %all_to_all.5 = f32[8,64,512]{2,1,0:T(8,128)S(1)} all-to-all(f32[8,64,512]{2,1,0:T(8,128)S(1)} %bitcast.5), channel_id=1, replica_groups=mesh['member'=8,'space'=32] {'member'}, dimensions={0} | all-to-all | bytes 2097152 | tf_op jit(solution)/shard_map/all_to_all | solution.py:438
  86.5 0.1 reduce_sum.9
  86.6 0.7 multiply_bitcast_fusion
  (23 shorter events, 0.1 us)
Async XLA Ops:
  1.5 8.8 %copy-start.6 = (f32[128]{0:T(128)S(1)}, f32[128]{0:T(128)}, u32[]{:S(2)}) copy-start(f32[128]{0:T(128)} %param.15) | copy-start | bytes 1540
  1.5 8.8 %copy-start.7 = (f32[128]{0:T(128)S(1)}, f32[128]{0:T(128)}, u32[]{:S(2)}) copy-start(f32[128]{0:T(128)} %param.14) | copy-start | bytes 1540
  1.5 8.8 %copy-start = (bf16[6,8,256,128]{3,2,1,0:T(8,128)(2,1)S(1)}, bf16[6,8,256,128]{3,2,1,0:T(8,128)(2,1)}, u32[]{:S(2)}) copy-start(bf16[6,8,256,128]{3,2,1,0:T(8,128)(2,1)} %u_hbm.9) | copy-start | bytes 9437188
  1.5 8.8 %copy-start.1 = (bf16[6,8,256,128]{3,2,1,0:T(8,128)(2,1)S(1)}, bf16[6,8,256,128]{3,2,1,0:T(8,128)(2,1)}, u32[]{:S(2)}) copy-start(bf16[6,8,256,128]{3,2,1,0:T(8,128)(2,1)} %v_hbm.9) | copy-start | bytes 9437188
  1.5 8.8 %copy-start.4 = (f32[8,256]{1,0:T(8,128)S(1)}, f32[8,256]{1,0:T(8,128)}, u32[]{:S(2)}) copy-start(f32[8,256]{1,0:T(8,128)} %psi_ref.5) | copy-start | bytes 24580
  1.6 8.8 %copy-start.5 = (f32[8,256]{1,0:T(8,128)S(1)}, f32[8,256]{1,0:T(8,128)}, u32[]{:S(2)}) copy-start(f32[8,256]{1,0:T(8,128)} %bal_ref.5) | copy-start | bytes 24580
  1.6 24.4 %collective-permute-start.2 = (bf16[2,2,256,128]{3,2,1,0:T(8,128)(2,1)S(1)}, bf16[2,2,256,128]{3,2,1,0:T(8,128)(2,1)S(1)}, u32[]{:S(2)}, u32[]{:S(2)}) collective-permute-start(bf16[2,2,256,128]{3,2,1,0:T(8,128)(2,1)S(1)} %edge_sums.1.sums_hbm), channel_id=1, source_target_pairs={{1,2},{3,4},{5,6},{7,8},{9,10},{11,12},{13,14},{15,16},{17,18},{19... | collective-permute-start | bytes 786440 | tf_op jit(solution)/shard_map/ppermute | solution.py:366
  6.1 48.5 %collective-permute-start = (bf16[2,6,2,256,128]{4,3,2,1,0:T(8,128)(2,1)S(1)}, bf16[2,6,2,256,128]{4,3,2,1,0:T(8,128)(2,1)S(1)}, u32[]{:S(2)}, u32[]{:S(2)}) collective-permute-start(bf16[2,6,2,256,128]{4,3,2,1,0:T(8,128)(2,1)S(1)} %get-tuple-element.21), channel_id=1, source_target_pairs={{1,2},{3,4},{5,6},{7,8},{9,10},{11,12},{13,14},{15,16},{17,18},{19... | collective-permute-start | bytes 4718600 | tf_op jit(solution)/shard_map/ppermute | solution.py:367
  10.2 17.1 %collective-permute-start.1 = (bf16[2,6,2,256,128]{4,3,2,1,0:T(8,128)(2,1)S(1)}, bf16[2,6,2,256,128]{4,3,2,1,0:T(8,128)(2,1)S(1)}, u32[]{:S(2)}, u32[]{:S(2)}) collective-permute-start(bf16[2,6,2,256,128]{4,3,2,1,0:T(8,128)(2,1)S(1)} %get-tuple-element.22), channel_id=1, source_target_pairs={{0,1},{2,3},{4,5},{6,7},{8,9},{10,11},{12,13},{14,15},{16,17},{18,... | collective-permute-start | bytes 4718600 | tf_op jit(solution)/shard_map/ppermute | solution.py:368
  10.4 17.0 %copy-start.2 = (bf16[6,8,256,128]{3,2,1,0:T(8,128)(2,1)S(1)}, bf16[6,8,256,128]{3,2,1,0:T(8,128)(2,1)}, u32[]{:S(2)}) copy-start(bf16[6,8,256,128]{3,2,1,0:T(8,128)(2,1)} %h_hbm.5) | copy-start | bytes 9437188
  10.4 16.9 %copy-start.3 = (bf16[6,8,256,128]{3,2,1,0:T(8,128)(2,1)S(1)}, bf16[6,8,256,128]{3,2,1,0:T(8,128)(2,1)}, u32[]{:S(2)}) copy-start(bf16[6,8,256,128]{3,2,1,0:T(8,128)(2,1)} %q_hbm.5) | copy-start | bytes 9437188
  21.4 14.0 %collective-permute-start.3 = (bf16[2,4,32,512]{3,2,1,0:T(8,128)(2,1)S(1)}, bf16[2,4,32,512]{3,2,1,0:T(8,128)(2,1)S(1)}, u32[]{:S(2)}, u32[]{:S(2)}) collective-permute-start(bf16[2,4,32,512]{3,2,1,0:T(8,128)(2,1)S(1)} %get-tuple-element.27), channel_id=1, source_target_pairs={{0,64},{32,96},{64,128},{96,160},{128,192},{160,224},{192,0},{224,... | collective-permute-start | bytes 786440 | tf_op jit(solution)/shard_map/ppermute | solution.py:387
  23.1 15.9 %collective-permute-start.4 = (bf16[2,4,32,512]{3,2,1,0:T(8,128)(2,1)S(1)}, bf16[2,4,32,512]{3,2,1,0:T(8,128)(2,1)S(1)}, u32[]{:S(2)}, u32[]{:S(2)}) collective-permute-start(bf16[2,4,32,512]{3,2,1,0:T(8,128)(2,1)S(1)} %get-tuple-element.28), channel_id=1, source_target_pairs={{0,128},{32,160},{64,192},{96,224},{128,0},{160,32},{192,64},{224,... | collective-permute-start | bytes 786440 | tf_op jit(solution)/shard_map/ppermute | solution.py:387
  26.0 13.0 %collective-permute-start.5 = (bf16[2,4,32,512]{3,2,1,0:T(8,128)(2,1)S(1)}, bf16[2,4,32,512]{3,2,1,0:T(8,128)(2,1)S(1)}, u32[]{:S(2)}, u32[]{:S(2)}) collective-permute-start(bf16[2,4,32,512]{3,2,1,0:T(8,128)(2,1)S(1)} %get-tuple-element.29), channel_id=1, source_target_pairs={{0,192},{32,224},{64,0},{96,32},{128,64},{160,96},{192,128},{224,1... | collective-permute-start | bytes 786440 | tf_op jit(solution)/shard_map/ppermute | solution.py:387
  34.7 11.1 %collective-permute-start.6 = (bf16[2,4,32,512]{3,2,1,0:T(8,128)(2,1)S(1)}, bf16[2,4,32,512]{3,2,1,0:T(8,128)(2,1)S(1)}, u32[]{:S(2)}, u32[]{:S(2)}) collective-permute-start(bf16[2,4,32,512]{3,2,1,0:T(8,128)(2,1)S(1)} %get-tuple-element.31), channel_id=1, source_target_pairs={{0,64},{32,96},{64,128},{96,160},{128,192},{160,224},{192,0},{224,... | collective-permute-start | bytes 786440 | tf_op jit(solution)/shard_map/ppermute | solution.py:403
  35.4 10.4 %collective-permute-start.7 = (bf16[2,4,32,512]{3,2,1,0:T(8,128)(2,1)S(1)}, bf16[2,4,32,512]{3,2,1,0:T(8,128)(2,1)S(1)}, u32[]{:S(2)}, u32[]{:S(2)}) collective-permute-start(bf16[2,4,32,512]{3,2,1,0:T(8,128)(2,1)S(1)} %get-tuple-element.32), channel_id=1, source_target_pairs={{0,128},{32,160},{64,192},{96,224},{128,0},{160,32},{192,64},{224,... | collective-permute-start | bytes 786440 | tf_op jit(solution)/shard_map/ppermute | solution.py:403
  39.0 10.9 %collective-permute-start.8 = (bf16[2,4,32,512]{3,2,1,0:T(8,128)(2,1)S(1)}, bf16[2,4,32,512]{3,2,1,0:T(8,128)(2,1)S(1)}, u32[]{:S(2)}, u32[]{:S(2)}) collective-permute-start(bf16[2,4,32,512]{3,2,1,0:T(8,128)(2,1)S(1)} %get-tuple-element.33), channel_id=1, source_target_pairs={{0,192},{32,224},{64,0},{96,32},{128,64},{160,96},{192,128},{224,1... | collective-permute-start | bytes 786440 | tf_op jit(solution)/shard_map/ppermute | solution.py:403
  51.3 10.4 %collective-permute-start.9 = (bf16[8,32,512]{2,1,0:T(8,128)(2,1)S(1)}, bf16[8,32,512]{2,1,0:T(8,128)(2,1)S(1)}, u32[]{:S(2)}, u32[]{:S(2)}) collective-permute-start(bf16[8,32,512]{2,1,0:T(8,128)(2,1)S(1)} %get-tuple-element.36), channel_id=1, source_target_pairs={{0,32},{32,0},{64,96},{96,64},{128,160},{160,128},{192,224},{224,1... | collective-permute-start | bytes 786440 | tf_op jit(solution)/shard_map/ppermute | solution.py:415

commit v5 on v4

--- a/solution.py
+++ b/solution.py
@@ -43,26 +43,23 @@
         copy.wait()
 
 
-def sums_kernel(u_hbm, v_hbm, sums_ref, rows, sems):
+def far_edge_kernel(u_hbm, v_hbm, far_ref, sums_ref, sems):
     at = pl.ds((u_hbm.shape[1] - EDGE) * core_index(), EDGE)
-    copies = [pltpu.make_async_copy(x.at[:, at], rows.at[f], sems.at[f]) for f, x in enumerate((u_hbm, v_hbm))]
+    copies = [pltpu.make_async_copy(x.at[:, at], far_ref.at[f], sems.at[f]) for f, x in enumerate((u_hbm, v_hbm))]
     run(copies)
     for f, copy in enumerate(copies):
         copy.wait()
         for r in range(EDGE):
-            total = rows[f, 0, r].astype(jnp.float32)
-            for m in range(1, rows.shape[1]):
-                total = total + rows[f, m, r].astype(jnp.float32)
+            total = far_ref[f, 0, r].astype(jnp.float32)
+            for m in range(1, far_ref.shape[1]):
+                total = total + far_ref[f, m, r].astype(jnp.float32)
             sums_ref[f, r] = total.astype(jnp.bfloat16)
 
 
-def edges_kernel(u_hbm, v_hbm, sums_hbm, far_ref, near_ref, sems):
+def near_edge_kernel(u_hbm, v_hbm, sums_hbm, near_ref, sems):
     del sums_hbm
-    core = core_index()
-    far_at = pl.ds((u_hbm.shape[1] - EDGE) * core, EDGE)
-    near_at = pl.ds((u_hbm.shape[1] - EDGE) * (1 - core), EDGE)
-    copies = [pltpu.make_async_copy(x.at[:, far_at], far_ref.at[f], sems.at[f]) for f, x in enumerate((u_hbm, v_hbm))]
-    copies += [pltpu.make_async_copy(x.at[:, near_at], near_ref.at[f], sems.at[2 + f]) for f, x in enumerate((u_hbm, v_hbm))]
+    at = pl.ds((u_hbm.shape[1] - EDGE) * (1 - core_index()), EDGE)
+    copies = [pltpu.make_async_copy(x.at[:, at], near_ref.at[f], sems.at[f]) for f, x in enumerate((u_hbm, v_hbm))]
     run(copies)
     finish(copies)
 
@@ -70,25 +67,25 @@
 def edges_call(u, v):
     members, _, meridians, levels = u.shape
     edge = jax.ShapeDtypeStruct((2, members, EDGE, meridians, levels), u.dtype)
-    sums = pl.pallas_call(
-        sums_kernel,
-        name="edge_sums",
-        out_shape=jax.ShapeDtypeStruct((2, EDGE, meridians, levels), u.dtype),
+    far, sums = pl.pallas_call(
+        far_edge_kernel,
+        name="far_edge",
+        out_shape=(edge, jax.ShapeDtypeStruct((2, EDGE, meridians, levels), u.dtype)),
         in_specs=[ANY, ANY],
-        out_specs=VMEM,
-        scratch_shapes=[pltpu.VMEM(edge.shape, u.dtype), pltpu.SemaphoreType.DMA((2,))],
+        out_specs=(VMEM, VMEM),
+        scratch_shapes=[pltpu.SemaphoreType.DMA((2,))],
         compiler_params=params(8),
         cost_estimate=cost(1 << 20, 3 << 20),
     )(in_hbm(u), in_hbm(v))
-    far, near = pl.pallas_call(
-        edges_kernel,
-        name="edges",
-        out_shape=(edge, edge),
+    near = pl.pallas_call(
+        near_edge_kernel,
+        name="near_edge",
+        out_shape=edge,
         in_specs=[ANY, ANY, ANY],
-        out_specs=(VMEM, VMEM),
-        scratch_shapes=[pltpu.SemaphoreType.DMA((4,))],
+        out_specs=VMEM,
+        scratch_shapes=[pltpu.SemaphoreType.DMA((2,))],
         compiler_params=params(8),
-        cost_estimate=cost(1 << 20, 6 << 20),
+        cost_estimate=cost(1 << 20, 3 << 20),
     )(in_hbm(u), in_hbm(v), sums)
     return far, near, sums
 
@@ -295,9 +292,10 @@
     compute_rows(EDGE, row_from, (u_ext, v_ext), (h_buf, q_buf), psi_ref, bal_ref, slopes_ref, work, g_ref, late_ref, True, chunk)
 
 
-def halves_kernel(weight, g_in_ref, mine_ref, theirs_ref, g_ref):
-    apart = (mine_ref[...].astype(jnp.float32) - theirs_ref[...].astype(jnp.float32)).astype(jnp.bfloat16)
-    apart = apart.reshape(-1, apart.shape[2])
+def halves_kernel(weight, g_in_ref, *rest):
+    means, g_ref = rest[:-1], rest[-1]
+    apart = [x[...].astype(jnp.float32) - y[...].astype(jnp.float32) for x, y in zip(means[::2], means[1::2])]
+    apart = jnp.concatenate([x.astype(jnp.bfloat16).reshape(-1, x.shape[2]) for x in apart], axis=0)
     half = g_ref.shape[0] // 2
     top = g_in_ref[0:half] + gram(apart[:, :half], apart) * weight
     g_ref[0:half] = top
@@ -324,22 +322,18 @@
 def between_kernel(members, g_in_ref, *rest):
     parts, (g_ref, mine_ref, theirs_ref) = rest[:-3], rest[-3:]
     side = lax.axis_index("member") % SIDE
-    groups = len(parts) // 2
-    g_ref[...] = g_in_ref[...]
-    first = 0
-    for part in (parts[:groups], parts[groups:]):
-        _, n, chunk, width = part[0].shape
-        overall = sum(p[...].astype(jnp.float32) for p in part) * (1.0 / groups)
-        apart = [(p[...].astype(jnp.float32) - overall).astype(jnp.bfloat16).reshape(-1, width) for p in part]
-        apart = jnp.concatenate(apart, axis=0)
-        half = width // 2
-        g_ref[0:half] += gram(apart[:, :half], apart) * float(members)
-        g_ref[half:, half:] += gram(apart[:, half:], apart[:, half:]) * float(members)
-        overall = overall.astype(jnp.bfloat16)
-        low = side == 0
-        mine_ref[first : first + n] = jnp.where(low, overall[0], overall[1])
-        theirs_ref[first : first + n] = jnp.where(low, overall[1], overall[0])
-        first += n
+    groups = len(parts)
+    _, n, chunk, width = parts[0].shape
+    half = width // 2
+    overall = sum(p[...].astype(jnp.float32) for p in parts) * (1.0 / groups)
+    apart = [(p[...].astype(jnp.float32) - overall).astype(jnp.bfloat16).reshape(-1, width) for p in parts]
+    apart = jnp.concatenate(apart, axis=0)
+    g_ref[0:half] = g_in_ref[0:half] + gram(apart[:, :half], apart) * float(members)
+    g_ref[half:, half:] = g_in_ref[half:, half:] + gram(apart[:, half:], apart[:, half:]) * float(members)
+    overall = overall.astype(jnp.bfloat16)
+    low = side == 0
+    mine_ref[...] = jnp.where(low, overall[0], overall[1])
+    theirs_ref[...] = jnp.where(low, overall[1], overall[0])
 
 
 def on_device(u, v, h, q, psi, bal, slope_t, slope_q):
@@ -402,17 +396,19 @@
     )(u, v, h, q, near, far_sums, psi, bal, slopes, g)
     edge_means = [x if r == 0 else lax.ppermute(x, "member", along_y(r)) for r, x in enumerate(edge_means)]
 
-    half = jax.ShapeDtypeStruct((parallels, chunk, width), jnp.bfloat16)
-    g, mine, theirs = pl.pallas_call(
-        functools.partial(between_kernel, members),
-        name="between",
-        out_shape=(g_shape, half, half),
-        in_specs=[VMEM] * (1 + 2 * groups),
-        out_specs=(VMEM, VMEM, VMEM),
-        compiler_params=params(16),
-        cost_estimate=cost(1 << 30, 5 << 20),
-    )(g, *means, *edge_means)
-    theirs = lax.ppermute(theirs, "member", along_x)
+    halves = []
+    for part in (means, edge_means):
+        half = jax.ShapeDtypeStruct(part[0].shape[1:], jnp.bfloat16)
+        g, mine, theirs = pl.pallas_call(
+            functools.partial(between_kernel, members),
+            name="between",
+            out_shape=(g_shape, half, half),
+            in_specs=[VMEM] * (1 + groups),
+            out_specs=(VMEM, VMEM, VMEM),
+            compiler_params=params(12),
+            cost_estimate=cost(1 << 29, 3 << 20),
+        )(g, *part)
+        halves += [mine, lax.ppermute(theirs, "member", along_x)]
 
     g = pl.pallas_call(
         functools.partial(far_kernel, chunk),
@@ -429,11 +425,11 @@
         functools.partial(halves_kernel, members * groups / 2.0),
         name="halves",
         out_shape=g_shape,
-        in_specs=[VMEM] * 3,
+        in_specs=[VMEM] * (1 + len(halves)),
         out_specs=VMEM,
         compiler_params=params(8),
         cost_estimate=cost(1 << 28, 3 << 20),
-    )(g, mine, theirs)
+    )(g, *halves)
 
     parts = lax.all_to_all(g.reshape(peers, width // peers, width), "member", 0, 0, tiled=True)
     scale = 1.0 / ((members * peers - 1) * parallels * meridians)

time: 87.5 us -> 83.9 us (0.959)
  the two profiles are of different devices: /device:TPU:96 before, /device:TPU:160 now
where the time goes in v5:
time: 83.9 us; the launch traced here: 83.7 us
  Pallas kernels  27.2 us (32%)
  blocking collectives  25.1 us (30%)
  starting transfers between devices  22.6 us (27%)
  waiting for transfers between devices  7.72 us (9%)
    all_to_all x1, blocking collectives, on_device(): lax.all_to_all(g.reshape(peers, width // peers, width), 'member', 0, 0, t...  25.1 us
    pallas_call x1, Pallas kernels, on_device(): pl.pallas_call(functools.partial(inner_kernel, chunk), name='inner_rows',...  11 us
    ppermute x6, starting transfers between devices, on_device(): lax.ppermute(x, 'member', along_y(r))  9.8 us
    ppermute x6, waiting for transfers between devices, on_device(): lax.ppermute(x, 'member', along_y(r))  7.35 us
    pallas_call x1, Pallas kernels, on_device(): pl.pallas_call(functools.partial(near_kernel, chunk), name='near_rows', o...  7.32 us
    ppermute x2, starting transfers between devices, on_device(): halves += [mine, lax.ppermute(theirs, 'member', along_x)]  6.02 us
    pallas_call x1, Pallas kernels, on_device(): pl.pallas_call(functools.partial(far_kernel, chunk), name='far_rows', out...  4.09 us
    ppermute x1, starting transfers between devices, on_device(): far_sums = lax.ppermute(far_sums, 'space', across)  3.55 us
  transfers between devices with their start and end apart: 11, of which 4 were waited for; matrix products, arithmetic and copies ran while one was open for 0% of the time, Pallas kernels for 30%

profile of v5, /device:TPU:160, one launch (start us, length us, event | category | flops | bytes accessed | tf_op | source)
XLA Modules:
  0.0 83.7 jit_solution(12592015717475821180)
XLA Ops:
  0.0 1.5 %far_edge.1 = (bf16[2,6,2,256,128]{4,3,2,1,0:T(8,128)(2,1)S(1)}, bf16[2,2,256,128]{3,2,1,0:T(8,128)(2,1)S(1)}) custom-call(bf16[6,8,256,128]{3,2,1,0:T(8,128)(2,1)} %u_hbm.9, bf16[6,8,256,128]{3,2,1,0:T(8,128)(2,1)} %v_hbm.9), custom_call_target="tpu_custom_call" | custom-call | flops 1048576 | bytes 3145728 | tf_op jit(solution)/shard_map/far_edge/pallas_call | solution.py:70
  1.6 3.5 %collective-permute-start.2 = (bf16[2,2,256,128]{3,2,1,0:T(8,128)(2,1)S(1)}, bf16[2,2,256,128]{3,2,1,0:T(8,128)(2,1)S(1)}, u32[]{:S(2)}, u32[]{:S(2)}) collective-permute-start(bf16[2,2,256,128]{3,2,1,0:T(8,128)(2,1)S(1)} %get-tuple-element.25.sums_hbm), channel_id=1, source_target_pairs={{1,2},{3,4},{5,6},{7,8},{9,10},{11,12},{13,14},{15,16},{17,18},{19... | collective-permute-start | bytes 786440 | tf_op jit(solution)/shard_map/ppermute | solution.py:360
  5.1 1.4 %near_edge.1 = bf16[2,6,2,256,128]{4,3,2,1,0:T(8,128)(2,1)S(1)} custom-call(bf16[6,8,256,128]{3,2,1,0:T(8,128)(2,1)} %u_hbm.9, bf16[6,8,256,128]{3,2,1,0:T(8,128)(2,1)} %v_hbm.9, bf16[2,2,256,128]{3,2,1,0:T(8,128)(2,1)S(1)} %get-tuple-element.25.sums_hbm), custom_call_target="tpu_custom_call" | custom-call | flops 1048576 | bytes 3145728 | tf_op jit(solution)/shard_map/near_edge/pallas_call | solution.py:80
  6.5 0.3 collective-permute-start.1
  6.8 3.0 %collective-permute-start = (bf16[2,6,2,256,128]{4,3,2,1,0:T(8,128)(2,1)S(1)}, bf16[2,6,2,256,128]{4,3,2,1,0:T(8,128)(2,1)S(1)}, u32[]{:S(2)}, u32[]{:S(2)}) collective-permute-start(bf16[2,6,2,256,128]{4,3,2,1,0:T(8,128)(2,1)S(1)} %get-tuple-element.24), channel_id=1, source_target_pairs={{1,2},{3,4},{5,6},{7,8},{9,10},{11,12},{13,14},{15,16},{17,18},{19... | collective-permute-start | bytes 4718600 | tf_op jit(solution)/shard_map/ppermute | solution.py:361
  9.9 11.0 %inner_rows.1 = (f32[512,512]{1,0:T(8,128)S(1)}, bf16[2,4,32,512]{3,2,1,0:T(8,128)(2,1)S(1)}, bf16[2,4,32,512]{3,2,1,0:T(8,128)(2,1)S(1)}, bf16[2,4,32,512]{3,2,...) custom-call(bf16[6,8,256,128]{3,2,1,0:T(8,128)(2,1)S(1)} %copy-done, bf16[6,8,256,128]{3,2,1,0:T(8,128)(2,1)S(1)} %copy-done.1, ...), custom_call_target="tpu_custom_call" | custom-call | flops 25769803776 | bytes 33554432 | tf_op jit(solution)/shard_map/inner_rows/pallas_call | solution.py:370
  20.9 1.7 %collective-permute-start.3 = (bf16[2,4,32,512]{3,2,1,0:T(8,128)(2,1)S(1)}, bf16[2,4,32,512]{3,2,1,0:T(8,128)(2,1)S(1)}, u32[]{:S(2)}, u32[]{:S(2)}) collective-permute-start(bf16[2,4,32,512]{3,2,1,0:T(8,128)(2,1)S(1)} %get-tuple-element.30), channel_id=1, source_target_pairs={{0,64},{32,96},{64,128},{96,160},{128,192},{160,224},{192,0},{224,... | collective-permute-start | bytes 786440 | tf_op jit(solution)/shard_map/ppermute | solution.py:381
  22.6 2.9 %collective-permute-start.4 = (bf16[2,4,32,512]{3,2,1,0:T(8,128)(2,1)S(1)}, bf16[2,4,32,512]{3,2,1,0:T(8,128)(2,1)S(1)}, u32[]{:S(2)}, u32[]{:S(2)}) collective-permute-start(bf16[2,4,32,512]{3,2,1,0:T(8,128)(2,1)S(1)} %get-tuple-element.31), channel_id=1, source_target_pairs={{0,128},{32,160},{64,192},{96,224},{128,0},{160,32},{192,64},{224,... | collective-permute-start | bytes 786440 | tf_op jit(solution)/shard_map/ppermute | solution.py:381
  25.5 1.3 %collective-permute-start.5 = (bf16[2,4,32,512]{3,2,1,0:T(8,128)(2,1)S(1)}, bf16[2,4,32,512]{3,2,1,0:T(8,128)(2,1)S(1)}, u32[]{:S(2)}, u32[]{:S(2)}) collective-permute-start(bf16[2,4,32,512]{3,2,1,0:T(8,128)(2,1)S(1)} %get-tuple-element.32), channel_id=1, source_target_pairs={{0,192},{32,224},{64,0},{96,32},{128,64},{160,96},{192,128},{224,1... | collective-permute-start | bytes 786440 | tf_op jit(solution)/shard_map/ppermute | solution.py:381
  26.9 7.3 %near_rows.1 = (f32[512,512]{1,0:T(8,128)S(1)}, bf16[8,2,32,512]{3,2,1,0:T(8,128)(2,1)S(1)}, bf16[2,4,32,512]{3,2,1,0:T(8,128)(2,1)S(1)}, bf16[2,4,32,512]{3,2,1...) custom-call(bf16[6,8,256,128]{3,2,1,0:T(8,128)(2,1)S(1)} %copy-done, ...), custom_call_target="tpu_custom_call" | custom-call | flops 12884901888 | bytes 33554432 | tf_op jit(solution)/shard_map/near_rows/pallas_call | solution.py:383
  34.2 0.8 collective-permute-start.6
  34.9 3.1 %collective-permute-start.7 = (bf16[2,4,32,512]{3,2,1,0:T(8,128)(2,1)S(1)}, bf16[2,4,32,512]{3,2,1,0:T(8,128)(2,1)S(1)}, u32[]{:S(2)}, u32[]{:S(2)}) collective-permute-start(bf16[2,4,32,512]{3,2,1,0:T(8,128)(2,1)S(1)} %get-tuple-element.36), channel_id=1, source_target_pairs={{0,128},{32,160},{64,192},{96,224},{128,0},{160,32},{192,64},{224,... | collective-permute-start | bytes 786440 | tf_op jit(solution)/shard_map/ppermute | solution.py:397
  38.1 0.2 collective-permute-done.4.rest_2_
  38.3 0.8 between.2
  39.1 2.9 %collective-permute-start.9 = (bf16[4,32,512]{2,1,0:T(8,128)(2,1)S(1)}, bf16[4,32,512]{2,1,0:T(8,128)(2,1)S(1)}, u32[]{:S(2)}, u32[]{:S(2)}) collective-permute-start(bf16[4,32,512]{2,1,0:T(8,128)(2,1)S(1)} %get-tuple-element.40), channel_id=1, source_target_pairs={{0,32},{32,0},{64,96},{96,64},{128,160},{160,128},{192,224},{224,1... | collective-permute-start | bytes 393224 | tf_op jit(solution)/shard_map/ppermute | solution.py:411
  42.0 7.0 %collective-permute-done.6.rest_1_ = bf16[2,4,32,512]{3,2,1,0:T(8,128)(2,1)S(1)} collective-permute-done((bf16[2,4,32,512]{3,2,1,0:T(8,128)(2,1)S(1)}, bf16[2,4,32,512]{3,2,1,0:T(8,128)(2,1)S(1)}, u32[]{:S(2)}, u32[]{:S(2)}) %collective-permute-start.6) | collective-permute-done | bytes 262176 | tf_op jit(solution)/shard_map/ppermute | solution.py:397
  49.0 0.2 collective-permute-done.8.rest_3_
  49.2 0.8 between.3
  50.0 3.1 %collective-permute-start.10 = (bf16[4,32,512]{2,1,0:T(8,128)(2,1)S(1)}, bf16[4,32,512]{2,1,0:T(8,128)(2,1)S(1)}, u32[]{:S(2)}, u32[]{:S(2)}) collective-permute-start(bf16[4,32,512]{2,1,0:T(8,128)(2,1)S(1)} %get-tuple-element.42), channel_id=1, source_target_pairs={{0,32},{32,0},{64,96},{96,64},{128,160},{160,128},{192,224},{224,1... | collective-permute-start | bytes 393224 | tf_op jit(solution)/shard_map/ppermute | solution.py:411
  53.1 4.1 %far_rows.1.g_in_ref = f32[512,512]{1,0:T(8,128)S(1)} custom-call(bf16[6,8,256,128]{3,2,1,0:T(8,128)(2,1)S(1)} %copy-done, bf16[6,8,256,128]{3,2,1,0:T(8,128)(2,1)S(1)} %copy-done.1, bf16[6,8,256,128]{3,2,1,0:T(8,128)(2,1)S(1)} %copy-done.2, bf16[6,8,256,128]{3,2,1,0:T(8,128)(2,1)S(1)} %copy-done.3, ...), custom_call_target="tpu_custom_call" | custom-call | flops 12884901888 | bytes 33554432 | tf_op jit(solution)/shard_map/far_rows/pallas_call | solution.py:413
  57.2 0.4 collective-permute-done.10.rest_3_
  57.5 0.4 halves.1
  57.9 25.1 %all_to_all.5 = f32[8,64,512]{2,1,0:T(8,128)S(1)} all-to-all(f32[8,64,512]{2,1,0:T(8,128)S(1)} %bitcast.5), channel_id=1, replica_groups=mesh['member'=8,'space'=32] {'member'}, dimensions={0} | all-to-all | bytes 2097152 | tf_op jit(solution)/shard_map/all_to_all | solution.py:434
  83.0 0.7 multiply_bitcast_fusion
  (26 shorter events, 0.2 us)
Async XLA Ops:
  1.5 8.3 %copy-start.6 = (f32[128]{0:T(128)S(1)}, f32[128]{0:T(128)}, u32[]{:S(2)}) copy-start(f32[128]{0:T(128)} %param.15) | copy-start | bytes 1540
  1.5 8.3 %copy-start.7 = (f32[128]{0:T(128)S(1)}, f32[128]{0:T(128)}, u32[]{:S(2)}) copy-start(f32[128]{0:T(128)} %param.14) | copy-start | bytes 1540
  1.5 8.3 %copy-start = (bf16[6,8,256,128]{3,2,1,0:T(8,128)(2,1)S(1)}, bf16[6,8,256,128]{3,2,1,0:T(8,128)(2,1)}, u32[]{:S(2)}) copy-start(bf16[6,8,256,128]{3,2,1,0:T(8,128)(2,1)} %u_hbm.9) | copy-start | bytes 9437188
  1.5 8.3 %copy-start.1 = (bf16[6,8,256,128]{3,2,1,0:T(8,128)(2,1)S(1)}, bf16[6,8,256,128]{3,2,1,0:T(8,128)(2,1)}, u32[]{:S(2)}) copy-start(bf16[6,8,256,128]{3,2,1,0:T(8,128)(2,1)} %v_hbm.9) | copy-start | bytes 9437188
  1.5 8.3 %copy-start.4 = (f32[8,256]{1,0:T(8,128)S(1)}, f32[8,256]{1,0:T(8,128)}, u32[]{:S(2)}) copy-start(f32[8,256]{1,0:T(8,128)} %psi_ref.5) | copy-start | bytes 24580
  1.6 8.3 %copy-start.5 = (f32[8,256]{1,0:T(8,128)S(1)}, f32[8,256]{1,0:T(8,128)}, u32[]{:S(2)}) copy-start(f32[8,256]{1,0:T(8,128)} %bal_ref.5) | copy-start | bytes 24580
  1.6 23.9 %collective-permute-start.2 = (bf16[2,2,256,128]{3,2,1,0:T(8,128)(2,1)S(1)}, bf16[2,2,256,128]{3,2,1,0:T(8,128)(2,1)S(1)}, u32[]{:S(2)}, u32[]{:S(2)}) collective-permute-start(bf16[2,2,256,128]{3,2,1,0:T(8,128)(2,1)S(1)} %get-tuple-element.25.sums_hbm), channel_id=1, source_target_pairs={{1,2},{3,4},{5,6},{7,8},{9,10},{11,12},{13,14},{15,16},{17,18},{19... | collective-permute-start | bytes 786440 | tf_op jit(solution)/shard_map/ppermute | solution.py:360
  6.5 20.3 %collective-permute-start.1 = (bf16[2,6,2,256,128]{4,3,2,1,0:T(8,128)(2,1)S(1)}, bf16[2,6,2,256,128]{4,3,2,1,0:T(8,128)(2,1)S(1)}, u32[]{:S(2)}, u32[]{:S(2)}) collective-permute-start(bf16[2,6,2,256,128]{4,3,2,1,0:T(8,128)(2,1)S(1)} %near_edge.1), channel_id=1, source_target_pairs={{0,1},{2,3},{4,5},{6,7},{8,9},{10,11},{12,13},{14,15},{16,17},{18,... | collective-permute-start | bytes 4718600 | tf_op jit(solution)/shard_map/ppermute | solution.py:362
  6.8 46.2 %collective-permute-start = (bf16[2,6,2,256,128]{4,3,2,1,0:T(8,128)(2,1)S(1)}, bf16[2,6,2,256,128]{4,3,2,1,0:T(8,128)(2,1)S(1)}, u32[]{:S(2)}, u32[]{:S(2)}) collective-permute-start(bf16[2,6,2,256,128]{4,3,2,1,0:T(8,128)(2,1)S(1)} %get-tuple-element.24), channel_id=1, source_target_pairs={{1,2},{3,4},{5,6},{7,8},{9,10},{11,12},{13,14},{15,16},{17,18},{19... | collective-permute-start | bytes 4718600 | tf_op jit(solution)/shard_map/ppermute | solution.py:361
  9.9 17.0 %copy-start.2 = (bf16[6,8,256,128]{3,2,1,0:T(8,128)(2,1)S(1)}, bf16[6,8,256,128]{3,2,1,0:T(8,128)(2,1)}, u32[]{:S(2)}) copy-start(bf16[6,8,256,128]{3,2,1,0:T(8,128)(2,1)} %h_hbm.5) | copy-start | bytes 9437188
  9.9 16.9 %copy-start.3 = (bf16[6,8,256,128]{3,2,1,0:T(8,128)(2,1)S(1)}, bf16[6,8,256,128]{3,2,1,0:T(8,128)(2,1)}, u32[]{:S(2)}) copy-start(bf16[6,8,256,128]{3,2,1,0:T(8,128)(2,1)} %q_hbm.5) | copy-start | bytes 9437188
  20.9 14.0 %collective-permute-start.3 = (bf16[2,4,32,512]{3,2,1,0:T(8,128)(2,1)S(1)}, bf16[2,4,32,512]{3,2,1,0:T(8,128)(2,1)S(1)}, u32[]{:S(2)}, u32[]{:S(2)}) collective-permute-start(bf16[2,4,32,512]{3,2,1,0:T(8,128)(2,1)S(1)} %get-tuple-element.30), channel_id=1, source_target_pairs={{0,64},{32,96},{64,128},{96,160},{128,192},{160,224},{192,0},{224,... | collective-permute-start | bytes 786440 | tf_op jit(solution)/shard_map/ppermute | solution.py:381
  22.6 15.7 %collective-permute-start.4 = (bf16[2,4,32,512]{3,2,1,0:T(8,128)(2,1)S(1)}, bf16[2,4,32,512]{3,2,1,0:T(8,128)(2,1)S(1)}, u32[]{:S(2)}, u32[]{:S(2)}) collective-permute-start(bf16[2,4,32,512]{3,2,1,0:T(8,128)(2,1)S(1)} %get-tuple-element.31), channel_id=1, source_target_pairs={{0,128},{32,160},{64,192},{96,224},{128,0},{160,32},{192,64},{224,... | collective-permute-start | bytes 786440 | tf_op jit(solution)/shard_map/ppermute | solution.py:381
  25.5 12.8 %collective-permute-start.5 = (bf16[2,4,32,512]{3,2,1,0:T(8,128)(2,1)S(1)}, bf16[2,4,32,512]{3,2,1,0:T(8,128)(2,1)S(1)}, u32[]{:S(2)}, u32[]{:S(2)}) collective-permute-start(bf16[2,4,32,512]{3,2,1,0:T(8,128)(2,1)S(1)} %get-tuple-element.32), channel_id=1, source_target_pairs={{0,192},{32,224},{64,0},{96,32},{128,64},{160,96},{192,128},{224,1... | collective-permute-start | bytes 786440 | tf_op jit(solution)/shard_map/ppermute | solution.py:381
  34.2 14.8 %collective-permute-start.6 = (bf16[2,4,32,512]{3,2,1,0:T(8,128)(2,1)S(1)}, bf16[2,4,32,512]{3,2,1,0:T(8,128)(2,1)S(1)}, u32[]{:S(2)}, u32[]{:S(2)}) collective-permute-start(bf16[2,4,32,512]{3,2,1,0:T(8,128)(2,1)S(1)} %get-tuple-element.35), channel_id=1, source_target_pairs={{0,64},{32,96},{64,128},{96,160},{128,192},{160,224},{192,0},{224,... | collective-permute-start | bytes 786440 | tf_op jit(solution)/shard_map/ppermute | solution.py:397
  34.9 14.1 %collective-permute-start.7 = (bf16[2,4,32,512]{3,2,1,0:T(8,128)(2,1)S(1)}, bf16[2,4,32,512]{3,2,1,0:T(8,128)(2,1)S(1)}, u32[]{:S(2)}, u32[]{:S(2)}) collective-permute-start(bf16[2,4,32,512]{3,2,1,0:T(8,128)(2,1)S(1)} %get-tuple-element.36), channel_id=1, source_target_pairs={{0,128},{32,160},{64,192},{96,224},{128,0},{160,32},{192,64},{224,... | collective-permute-start | bytes 786440 | tf_op jit(solution)/shard_map/ppermute | solution.py:397
  38.3 10.9 %collective-permute-start.8 = (bf16[2,4,32,512]{3,2,1,0:T(8,128)(2,1)S(1)}, bf16[2,4,32,512]{3,2,1,0:T(8,128)(2,1)S(1)}, u32[]{:S(2)}, u32[]{:S(2)}) collective-permute-start(bf16[2,4,32,512]{3,2,1,0:T(8,128)(2,1)S(1)} %get-tuple-element.37), channel_id=1, source_target_pairs={{0,192},{32,224},{64,0},{96,32},{128,64},{160,96},{192,128},{224,1... | collective-permute-start | bytes 786440 | tf_op jit(solution)/shard_map/ppermute | solution.py:397
  39.1 18.1 %collective-permute-start.9 = (bf16[4,32,512]{2,1,0:T(8,128)(2,1)S(1)}, bf16[4,32,512]{2,1,0:T(8,128)(2,1)S(1)}, u32[]{:S(2)}, u32[]{:S(2)}) collective-permute-start(bf16[4,32,512]{2,1,0:T(8,128)(2,1)S(1)} %get-tuple-element.40), channel_id=1, source_target_pairs={{0,32},{32,0},{64,96},{96,64},{128,160},{160,128},{192,224},{224,1... | collective-permute-start | bytes 393224 | tf_op jit(solution)/shard_map/ppermute | solution.py:411
  50.0 7.6 %collective-permute-start.10 = (bf16[4,32,512]{2,1,0:T(8,128)(2,1)S(1)}, bf16[4,32,512]{2,1,0:T(8,128)(2,1)S(1)}, u32[]{:S(2)}, u32[]{:S(2)}) collective-permute-start(bf16[4,32,512]{2,1,0:T(8,128)(2,1)S(1)} %get-tuple-element.42), channel_id=1, source_target_pairs={{0,32},{32,0},{64,96},{96,64},{128,160},{160,128},{192,224},{224,1... | collective-permute-start | bytes 393224 | tf_op jit(solution)/shard_map/ppermute | solution.py:411

commit v6 on v5

--- a/solution.py
+++ b/solution.py
@@ -227,25 +227,33 @@
     return copies
 
 
-def near_kernel(chunk, u_hbm, v_hbm, h_hbm, q_hbm, near_hbm, far_sums_ref, psi_ref, bal_ref, slopes_ref, g_in_ref, g_ref, late_ref, *rest):
-    outs, scratch = rest[:-22], rest[-22:]
+def near_kernel(chunk, u_hbm, v_hbm, h_hbm, q_hbm, near_hbm, psi_ref, bal_ref, slopes_ref, g_in_ref, g_ref, *rest):
+    outs, scratch = rest[:-15], rest[-15:]
     u_ext, v_ext, h_buf, q_buf = scratch[:4]
     work = scratch[4:12]
-    m_scr, u_sum, v_sum, sems, out_sems, late_sems = scratch[12:18]
-    members, parallels, meridians, levels = u_hbm.shape
+    m_scr, sems, out_sems = scratch[12:]
     side = 1 - core_index()
     copies = edge_copies(side, u_hbm, v_hbm, h_hbm, q_hbm, near_hbm, u_ext, v_ext, h_buf, q_buf, sems)
     run(copies)
-    copies_far = edge_copies(1 - side, u_hbm, v_hbm, h_hbm, q_hbm, None, *scratch[18:22], late_sems)
-    run(copies_far)
     g_ref[...] = g_in_ref[...]
     finish(copies)
-    compute_rows(EDGE, (parallels - EDGE) * side, (u_ext, v_ext), (h_buf, q_buf), psi_ref, bal_ref, slopes_ref, work, g_ref, m_scr, False, chunk)
+    row_from = (u_hbm.shape[1] - EDGE) * side
+    compute_rows(EDGE, row_from, (u_ext, v_ext), (h_buf, q_buf), psi_ref, bal_ref, slopes_ref, work, g_ref, m_scr, False, chunk)
     sends = scatter_means(m_scr, outs, 0, out_sems, len(outs))
     run(sends)
-
-    finish(copies_far)
-    u_ext, v_ext, h_buf, q_buf = scratch[18:22]
+    finish(sends)
+
+
+def far_means_kernel(chunk, u_hbm, v_hbm, h_hbm, q_hbm, after_hbm, far_sums_ref, psi_ref, bal_ref, slopes_ref, late_ref, *rest):
+    del after_hbm
+    outs, scratch = rest[:-14], rest[-14:]
+    u_ext, v_ext, h_buf, q_buf = scratch[:4]
+    work = scratch[4:10]
+    u_sum, v_sum, sems, out_sems = scratch[10:]
+    members, parallels, meridians, levels = u_hbm.shape
+    copies = edge_copies(core_index(), u_hbm, v_hbm, h_hbm, q_hbm, None, u_ext, v_ext, h_buf, q_buf, sems)
+    run(copies)
+    finish(copies)
     core = core_index()
     own = 2 * EDGE
     row_from = (parallels - EDGE) * core
@@ -274,9 +282,9 @@
             moist = sum(q_buf[m, k, at].astype(jnp.float32) for m in range(members)) - slopes_ref[1:2, :] * heat
             for f, x in enumerate((curl, spread, heat, moist)):
                 late_ref[c, k, :, f * levels : (f + 1) * levels] = (x * (1.0 / members)).astype(jnp.bfloat16)
-    late_sends = scatter_means(late_ref, outs, EDGE, late_sems, len(outs))
-    run(late_sends)
-    finish(sends + late_sends)
+    sends = scatter_means(late_ref, outs, 0, out_sems, len(outs))
+    run(sends)
+    finish(sends)
 
 
 def far_kernel(chunk, u_hbm, v_hbm, h_hbm, q_hbm, far_hbm, late_ref, psi_ref, bal_ref, slopes_ref, g_in_ref, g_ref, *scratch):
@@ -322,18 +330,24 @@
 def between_kernel(members, g_in_ref, *rest):
     parts, (g_ref, mine_ref, theirs_ref) = rest[:-3], rest[-3:]
     side = lax.axis_index("member") % SIDE
-    groups = len(parts)
-    _, n, chunk, width = parts[0].shape
+    groups = lax.axis_size("member") // SIDE
+    width = parts[0].shape[3]
     half = width // 2
-    overall = sum(p[...].astype(jnp.float32) for p in parts) * (1.0 / groups)
-    apart = [(p[...].astype(jnp.float32) - overall).astype(jnp.bfloat16).reshape(-1, width) for p in parts]
+    low = side == 0
+    apart = []
+    first = 0
+    for at in range(0, len(parts), groups):
+        part = parts[at : at + groups]
+        n = part[0].shape[1]
+        overall = sum(p[...].astype(jnp.float32) for p in part) * (1.0 / groups)
+        apart += [(p[...].astype(jnp.float32) - overall).astype(jnp.bfloat16).reshape(-1, width) for p in part]
+        overall = overall.astype(jnp.bfloat16)
+        mine_ref[first : first + n] = jnp.where(low, overall[0], overall[1])
+        theirs_ref[first : first + n] = jnp.where(low, overall[1], overall[0])
+        first += n
     apart = jnp.concatenate(apart, axis=0)
     g_ref[0:half] = g_in_ref[0:half] + gram(apart[:, :half], apart) * float(members)
     g_ref[half:, half:] = g_in_ref[half:, half:] + gram(apart[:, half:], apart[:, half:]) * float(members)
-    overall = overall.astype(jnp.bfloat16)
-    low = side == 0
-    mine_ref[...] = jnp.where(low, overall[0], overall[1])
-    theirs_ref[...] = jnp.where(low, overall[1], overall[0])
 
 
 def on_device(u, v, h, q, psi, bal, slope_t, slope_q):
@@ -380,30 +394,43 @@
     )(u, v, in_hbm(h), in_hbm(q), psi, bal, slopes)
     means = [x if r == 0 else lax.ppermute(x, "member", along_y(r)) for r, x in enumerate(means)]
 
-    g, late, *edge_means = pl.pallas_call(
+    g, *near_means = pl.pallas_call(
         functools.partial(near_kernel, chunk),
         name="near_rows",
-        out_shape=(g_shape, late_shape) + handed(2 * EDGE),
-        in_specs=[ANY] * 5 + [VMEM] * 5,
-        out_specs=(VMEM, VMEM) + (ANY,) * groups,
+        out_shape=(g_shape,) + handed(EDGE),
+        in_specs=[ANY] * 5 + [VMEM] * 4,
+        out_specs=(VMEM,) + (ANY,) * groups,
         scratch_shapes=row_scratch(dims, EDGE, 3 * EDGE)
-        + [pltpu.VMEM((peers, EDGE, chunk, width), jnp.bfloat16)]
+        + [pltpu.VMEM((peers, EDGE, chunk, width), jnp.bfloat16), dma((6,)), dma((groups,))],
+        compiler_params=params(16),
+        cost_estimate=row_cost(dims, EDGE),
+    )(u, v, h, q, near, psi, bal, slopes, g)
+    after = near_means[0]
+    near_means = [x if r == 0 else lax.ppermute(x, "member", along_y(r)) for r, x in enumerate(near_means)]
+
+    late, *far_means = pl.pallas_call(
+        functools.partial(far_means_kernel, chunk),
+        name="far_means",
+        out_shape=(late_shape,) + handed(EDGE),
+        in_specs=[ANY] * 5 + [VMEM] * 4,
+        out_specs=(VMEM,) + (ANY,) * groups,
+        scratch_shapes=row_scratch(dims, EDGE, 3 * EDGE)[:10]
         + [pltpu.VMEM(sum_shape, jnp.float32)] * 2
-        + [dma((6,)), dma((groups,)), dma((4,))]
-        + row_scratch(dims, EDGE, 3 * EDGE)[:4],
-        compiler_params=params(24),
+        + [dma((4,)), dma((groups,))],
+        compiler_params=params(14),
         cost_estimate=row_cost(dims, EDGE),
-    )(u, v, h, q, near, far_sums, psi, bal, slopes, g)
-    edge_means = [x if r == 0 else lax.ppermute(x, "member", along_y(r)) for r, x in enumerate(edge_means)]
+    )(u, v, h, q, after, far_sums, psi, bal, slopes)
+    far_means = [x if r == 0 else lax.ppermute(x, "member", along_y(r)) for r, x in enumerate(far_means)]
 
     halves = []
-    for part in (means, edge_means):
-        half = jax.ShapeDtypeStruct(part[0].shape[1:], jnp.bfloat16)
+    for part in (means + near_means, far_means):
+        rows = sum(x.shape[1] for x in part[::groups])
+        half = jax.ShapeDtypeStruct((rows, chunk, width), jnp.bfloat16)
         g, mine, theirs = pl.pallas_call(
             functools.partial(between_kernel, members),
             name="between",
             out_shape=(g_shape, half, half),
-            in_specs=[VMEM] * (1 + groups),
+            in_specs=[VMEM] * (1 + len(part)),
             out_specs=(VMEM, VMEM, VMEM),
             compiler_params=params(12),
             cost_estimate=cost(1 << 29, 3 << 20),

time: 83.9 us -> 81.6 us (0.973)
  the two profiles are of different devices: /device:TPU:160 before, /device:TPU:2 now
where the time goes in v6:
time: 81.6 us; the launch traced here: 80.2 us
  Pallas kernels  27.7 us (34%)
  starting transfers between devices  23.4 us (29%)
  blocking collectives  21.5 us (26%)
  waiting for transfers between devices  6.55 us (8%)
    all_to_all x1, blocking collectives, on_device(): lax.all_to_all(g.reshape(peers, width // peers, width), 'member', 0, 0, t...  21.5 us
    ppermute x9, starting transfers between devices, on_device(): lax.ppermute(x, 'member', along_y(r))  11.8 us
    pallas_call x1, Pallas kernels, on_device(): pl.pallas_call(functools.partial(inner_kernel, chunk), name='inner_rows',...  11 us
    ppermute x9, waiting for transfers between devices, on_device(): lax.ppermute(x, 'member', along_y(r))  6.53 us
    pallas_call x1, Pallas kernels, on_device(): pl.pallas_call(functools.partial(near_kernel, chunk), name='near_rows', o...  5.68 us
    ppermute x2, starting transfers between devices, on_device(): halves += [mine, lax.ppermute(theirs, 'member', along_x)]  5.39 us
    pallas_call x1, Pallas kernels, on_device(): pl.pallas_call(functools.partial(far_kernel, chunk), name='far_rows', out...  4.1 us
    ppermute x1, starting transfers between devices, on_device(): far_sums = lax.ppermute(far_sums, 'space', across)  2.32 us
  transfers between devices with their start and end apart: 14, of which 4 were waited for; matrix products, arithmetic and copies ran while one was open for 0% of the time, Pallas kernels for 32%

profile of v6, /device:TPU:2, one launch (start us, length us, event | category | flops | bytes accessed | tf_op | source)
XLA Modules:
  0.0 80.2 jit_solution(18202409357240104374)
XLA Ops:
  0.0 1.5 %far_edge.1 = (bf16[2,6,2,256,128]{4,3,2,1,0:T(8,128)(2,1)S(1)}, bf16[2,2,256,128]{3,2,1,0:T(8,128)(2,1)S(1)}) custom-call(bf16[6,8,256,128]{3,2,1,0:T(8,128)(2,1)} %u_hbm.11, bf16[6,8,256,128]{3,2,1,0:T(8,128)(2,1)} %v_hbm.11), custom_call_target="tpu_custom_call" | custom-call | flops 1048576 | bytes 3145728 | tf_op jit(solution)/shard_map/far_edge/pallas_call | solution.py:70
  1.6 2.3 %collective-permute-start.2 = (bf16[2,2,256,128]{3,2,1,0:T(8,128)(2,1)S(1)}, bf16[2,2,256,128]{3,2,1,0:T(8,128)(2,1)S(1)}, u32[]{:S(2)}, u32[]{:S(2)}) collective-permute-start(bf16[2,2,256,128]{3,2,1,0:T(8,128)(2,1)S(1)} %get-tuple-element.29.sums_hbm), channel_id=1, source_target_pairs={{1,2},{3,4},{5,6},{7,8},{9,10},{11,12},{13,14},{15,16},{17,18},{19... | collective-permute-start | bytes 786440 | tf_op jit(solution)/shard_map/ppermute | solution.py:374
  3.9 1.4 %near_edge.1 = bf16[2,6,2,256,128]{4,3,2,1,0:T(8,128)(2,1)S(1)} custom-call(bf16[6,8,256,128]{3,2,1,0:T(8,128)(2,1)} %u_hbm.11, bf16[6,8,256,128]{3,2,1,0:T(8,128)(2,1)} %v_hbm.11, bf16[2,2,256,128]{3,2,1,0:T(8,128)(2,1)S(1)} %get-tuple-element.29.sums_hbm), custom_call_target="tpu_custom_call" | custom-call | flops 1048576 | bytes 3145728 | tf_op jit(solution)/shard_map/near_edge/pallas_call | solution.py:80
  5.3 1.9 %collective-permute-start.1 = (bf16[2,6,2,256,128]{4,3,2,1,0:T(8,128)(2,1)S(1)}, bf16[2,6,2,256,128]{4,3,2,1,0:T(8,128)(2,1)S(1)}, u32[]{:S(2)}, u32[]{:S(2)}) collective-permute-start(bf16[2,6,2,256,128]{4,3,2,1,0:T(8,128)(2,1)S(1)} %near_edge.1), channel_id=1, source_target_pairs={{0,1},{2,3},{4,5},{6,7},{8,9},{10,11},{12,13},{14,15},{16,17},{18,... | collective-permute-start | bytes 4718600 | tf_op jit(solution)/shard_map/ppermute | solution.py:376
  7.2 1.9 %collective-permute-start = (bf16[2,6,2,256,128]{4,3,2,1,0:T(8,128)(2,1)S(1)}, bf16[2,6,2,256,128]{4,3,2,1,0:T(8,128)(2,1)S(1)}, u32[]{:S(2)}, u32[]{:S(2)}) collective-permute-start(bf16[2,6,2,256,128]{4,3,2,1,0:T(8,128)(2,1)S(1)} %get-tuple-element.28), channel_id=1, source_target_pairs={{1,2},{3,4},{5,6},{7,8},{9,10},{11,12},{13,14},{15,16},{17,18},{19... | collective-permute-start | bytes 4718600 | tf_op jit(solution)/shard_map/ppermute | solution.py:375
  9.3 11.0 %inner_rows.1 = (f32[512,512]{1,0:T(8,128)S(1)}, bf16[2,4,32,512]{3,2,1,0:T(8,128)(2,1)S(1)}, bf16[2,4,32,512]{3,2,1,0:T(8,128)(2,1)S(1)}, bf16[2,4,32,512]{3,2,...) custom-call(bf16[6,8,256,128]{3,2,1,0:T(8,128)(2,1)S(1)} %copy-done, bf16[6,8,256,128]{3,2,1,0:T(8,128)(2,1)S(1)} %copy-done.1, ...), custom_call_target="tpu_custom_call" | custom-call | flops 25769803776 | bytes 33554432 | tf_op jit(solution)/shard_map/inner_rows/pallas_call | solution.py:384
  20.3 1.7 %collective-permute-start.3 = (bf16[2,4,32,512]{3,2,1,0:T(8,128)(2,1)S(1)}, bf16[2,4,32,512]{3,2,1,0:T(8,128)(2,1)S(1)}, u32[]{:S(2)}, u32[]{:S(2)}) collective-permute-start(bf16[2,4,32,512]{3,2,1,0:T(8,128)(2,1)S(1)} %get-tuple-element.35), channel_id=1, source_target_pairs={{0,64},{32,96},{64,128},{96,160},{128,192},{160,224},{192,0},{224,... | collective-permute-start | bytes 786440 | tf_op jit(solution)/shard_map/ppermute | solution.py:395
  21.9 2.9 %collective-permute-start.4 = (bf16[2,4,32,512]{3,2,1,0:T(8,128)(2,1)S(1)}, bf16[2,4,32,512]{3,2,1,0:T(8,128)(2,1)S(1)}, u32[]{:S(2)}, u32[]{:S(2)}) collective-permute-start(bf16[2,4,32,512]{3,2,1,0:T(8,128)(2,1)S(1)} %get-tuple-element.36), channel_id=1, source_target_pairs={{0,128},{32,160},{64,192},{96,224},{128,0},{160,32},{192,64},{224,... | collective-permute-start | bytes 786440 | tf_op jit(solution)/shard_map/ppermute | solution.py:395
  24.8 1.3 %collective-permute-start.5 = (bf16[2,4,32,512]{3,2,1,0:T(8,128)(2,1)S(1)}, bf16[2,4,32,512]{3,2,1,0:T(8,128)(2,1)S(1)}, u32[]{:S(2)}, u32[]{:S(2)}) collective-permute-start(bf16[2,4,32,512]{3,2,1,0:T(8,128)(2,1)S(1)} %get-tuple-element.37), channel_id=1, source_target_pairs={{0,192},{32,224},{64,0},{96,32},{128,64},{160,96},{192,128},{224,1... | collective-permute-start | bytes 786440 | tf_op jit(solution)/shard_map/ppermute | solution.py:395
  26.2 5.7 %near_rows.1 = (f32[512,512]{1,0:T(8,128)S(1)}, bf16[2,2,32,512]{3,2,1,0:T(8,128)(2,1)S(1)}, bf16[2,2,32,512]{3,2,1,0:T(8,128)(2,1)S(1)}, bf16[2,2,32,512]{3,2,1,0:T(8,128)(2,1)S(1)}, bf16[2,2,32,512]{3,2,1,0:T(8,128)(2,1)S(1)}) custom-call(bf16[6,8,256,128]{3,2,1,0:T(8,128)(2,1)S(1)} %copy-done, bf16[6,8,256,128]{3,2,1,0:T(8,128)(2,1)S(1)} %copy-done.1, ...), custom_call_target="tpu_custom_call" | custom-call | flops 12884901888 | bytes 33554432 | tf_op jit(solution)/shard_map/near_rows/pallas_call | solution.py:397
  31.9 0.8 collective-permute-start.6
  32.7 0.8 %collective-permute-start.7 = (bf16[2,2,32,512]{3,2,1,0:T(8,128)(2,1)S(1)}, bf16[2,2,32,512]{3,2,1,0:T(8,128)(2,1)S(1)}, u32[]{:S(2)}, u32[]{:S(2)}) collective-permute-start(bf16[2,2,32,512]{3,2,1,0:T(8,128)(2,1)S(1)} %get-tuple-element.39), channel_id=1, source_target_pairs={{0,128},{32,160},{64,192},{96,224},{128,0},{160,32},{192,64},{224,... | collective-permute-start | bytes 393224 | tf_op jit(solution)/shard_map/ppermute | solution.py:409
  33.5 3.6 %collective-permute-done.4.rest_2_ = bf16[2,4,32,512]{3,2,1,0:T(8,128)(2,1)S(1)} collective-permute-done((bf16[2,4,32,512]{3,2,1,0:T(8,128)(2,1)S(1)}, bf16[2,4,32,512]{3,2,1,0:T(8,128)(2,1)S(1)}, u32[]{:S(2)}, u32[]{:S(2)}) %collective-permute-start.4) | collective-permute-done | bytes 262176 | tf_op jit(solution)/shard_map/ppermute | solution.py:395
  37.1 2.2 %far_means.1 = (bf16[8,2,32,512]{3,2,1,0:T(8,128)(2,1)S(1)}, bf16[2,2,32,512]{3,2,1,0:T(8,128)(2,1)S(1)}, bf16[2,2,32,512]{3,2,1,0:T(8,128)(2,1)S(1)}, bf16[2,2,...) custom-call(bf16[6,8,256,128]{3,2,1,0:T(8,128)(2,1)S(1)} %copy-done, bf16[6,8,256,128]{3,2,1,0:T(8,128)(2,1)S(1)} %copy-done.1, ...), custom_call_target="tpu_custom_call" | custom-call | flops 12884901888 | bytes 33554432 | tf_op jit(solution)/shard_map/far_means/pallas_call | solution.py:411
  39.3 2.1 %collective-permute-start.9 = (bf16[2,2,32,512]{3,2,1,0:T(8,128)(2,1)S(1)}, bf16[2,2,32,512]{3,2,1,0:T(8,128)(2,1)S(1)}, u32[]{:S(2)}, u32[]{:S(2)}) collective-permute-start(bf16[2,2,32,512]{3,2,1,0:T(8,128)(2,1)S(1)} %get-tuple-element.43), channel_id=1, source_target_pairs={{0,64},{32,96},{64,128},{96,160},{128,192},{160,224},{192,0},{224,... | collective-permute-start | bytes 393224 | tf_op jit(solution)/shard_map/ppermute | solution.py:423
  41.4 0.7 collective-permute-start.10
  42.7 1.6 %collective-permute-start.11 = (bf16[2,2,32,512]{3,2,1,0:T(8,128)(2,1)S(1)}, bf16[2,2,32,512]{3,2,1,0:T(8,128)(2,1)S(1)}, u32[]{:S(2)}, u32[]{:S(2)}) collective-permute-start(bf16[2,2,32,512]{3,2,1,0:T(8,128)(2,1)S(1)} %get-tuple-element.45), channel_id=1, source_target_pairs={{0,192},{32,224},{64,0},{96,32},{128,64},{160,96},{192,128},{224,1... | collective-permute-start | bytes 393224 | tf_op jit(solution)/shard_map/ppermute | solution.py:423
  44.2 1.0 %between.2 = (f32[512,512]{1,0:T(8,128)S(1)}, bf16[6,32,512]{2,1,0:T(8,128)(2,1)S(1)}, bf16[6,32,512]{2,1,0:T(8,128)(2,1)S(1)}) custom-call(f32[512,512]{1,0:T(8,128)S(1)} %get-tuple-element.33.g_in_ref, bf16[2,4,32,512]{3,2,1,0:T(8,128)(2,1)S(1)} %get-tuple-element.34.rest_0_, bf16[2,4,32,512]{3,2,1,0:T(8,128)(2,1)S(1)} %collective-permute-done.3.rest_1_, ...), custom_call_target="tpu_custom_call" | custom-call | flops 536870912 | bytes 3145728 | tf_op jit(solution)/shard_map/between/pallas_call | solution.py:429
  45.3 2.8 %collective-permute-start.12 = (bf16[6,32,512]{2,1,0:T(8,128)(2,1)S(1)}, bf16[6,32,512]{2,1,0:T(8,128)(2,1)S(1)}, u32[]{:S(2)}, u32[]{:S(2)}) collective-permute-start(bf16[6,32,512]{2,1,0:T(8,128)(2,1)S(1)} %get-tuple-element.48), channel_id=1, source_target_pairs={{0,32},{32,0},{64,96},{96,64},{128,160},{160,128},{192,224},{224,1... | collective-permute-start | bytes 589832 | tf_op jit(solution)/shard_map/ppermute | solution.py:438
  48.0 1.7 %collective-permute-done.9.rest_1_ = bf16[2,2,32,512]{3,2,1,0:T(8,128)(2,1)S(1)} collective-permute-done((bf16[2,2,32,512]{3,2,1,0:T(8,128)(2,1)S(1)}, bf16[2,2,32,512]{3,2,1,0:T(8,128)(2,1)S(1)}, u32[]{:S(2)}, u32[]{:S(2)}) %collective-permute-start.9) | collective-permute-done | bytes 131104 | tf_op jit(solution)/shard_map/ppermute | solution.py:423
  50.8 2.6 %collective-permute-start.13 = (bf16[2,32,512]{2,1,0:T(8,128)(2,1)S(1)}, bf16[2,32,512]{2,1,0:T(8,128)(2,1)S(1)}, u32[]{:S(2)}, u32[]{:S(2)}) collective-permute-start(bf16[2,32,512]{2,1,0:T(8,128)(2,1)S(1)} %get-tuple-element.50), channel_id=1, source_target_pairs={{0,32},{32,0},{64,96},{96,64},{128,160},{160,128},{192,224},{224,1... | collective-permute-start | bytes 196616 | tf_op jit(solution)/shard_map/ppermute | solution.py:438
  53.5 4.1 %far_rows.1.g_in_ref = f32[512,512]{1,0:T(8,128)S(1)} custom-call(bf16[6,8,256,128]{3,2,1,0:T(8,128)(2,1)S(1)} %copy-done, bf16[6,8,256,128]{3,2,1,0:T(8,128)(2,1)S(1)} %copy-done.1, bf16[6,8,256,128]{3,2,1,0:T(8,128)(2,1)S(1)} %copy-done.2, bf16[6,8,256,128]{3,2,1,0:T(8,128)(2,1)S(1)} %copy-done.3, ...), custom_call_target="tpu_custom_call" | custom-call | flops 12884901888 | bytes 33554432 | tf_op jit(solution)/shard_map/far_rows/pallas_call | solution.py:440
  58.0 21.5 %all_to_all.5 = f32[8,64,512]{2,1,0:T(8,128)S(1)} all-to-all(f32[8,64,512]{2,1,0:T(8,128)S(1)} %bitcast.5), channel_id=1, replica_groups=mesh['member'=8,'space'=32] {'member'}, dimensions={0} | all-to-all | bytes 2097152 | tf_op jit(solution)/shard_map/all_to_all | solution.py:461
  79.6 0.7 multiply_bitcast_fusion
  (33 shorter events, 2.2 us)
Async XLA Ops:
  1.5 7.7 %copy-start.6 = (f32[128]{0:T(128)S(1)}, f32[128]{0:T(128)}, u32[]{:S(2)}) copy-start(f32[128]{0:T(128)} %param.15) | copy-start | bytes 1540
  1.5 7.7 %copy-start.7 = (f32[128]{0:T(128)S(1)}, f32[128]{0:T(128)}, u32[]{:S(2)}) copy-start(f32[128]{0:T(128)} %param.14) | copy-start | bytes 1540
  1.5 7.7 %copy-start = (bf16[6,8,256,128]{3,2,1,0:T(8,128)(2,1)S(1)}, bf16[6,8,256,128]{3,2,1,0:T(8,128)(2,1)}, u32[]{:S(2)}) copy-start(bf16[6,8,256,128]{3,2,1,0:T(8,128)(2,1)} %u_hbm.11) | copy-start | bytes 9437188
  1.5 7.7 %copy-start.1 = (bf16[6,8,256,128]{3,2,1,0:T(8,128)(2,1)S(1)}, bf16[6,8,256,128]{3,2,1,0:T(8,128)(2,1)}, u32[]{:S(2)}) copy-start(bf16[6,8,256,128]{3,2,1,0:T(8,128)(2,1)} %v_hbm.11) | copy-start | bytes 9437188
  1.5 7.7 %copy-start.4 = (f32[8,256]{1,0:T(8,128)S(1)}, f32[8,256]{1,0:T(8,128)}, u32[]{:S(2)}) copy-start(f32[8,256]{1,0:T(8,128)} %psi_ref.7) | copy-start | bytes 24580
  1.6 7.7 %copy-start.5 = (f32[8,256]{1,0:T(8,128)S(1)}, f32[8,256]{1,0:T(8,128)}, u32[]{:S(2)}) copy-start(f32[8,256]{1,0:T(8,128)} %bal_ref.7) | copy-start | bytes 24580
  1.6 30.3 %collective-permute-start.2 = (bf16[2,2,256,128]{3,2,1,0:T(8,128)(2,1)S(1)}, bf16[2,2,256,128]{3,2,1,0:T(8,128)(2,1)S(1)}, u32[]{:S(2)}, u32[]{:S(2)}) collective-permute-start(bf16[2,2,256,128]{3,2,1,0:T(8,128)(2,1)S(1)} %get-tuple-element.29.sums_hbm), channel_id=1, source_target_pairs={{1,2},{3,4},{5,6},{7,8},{9,10},{11,12},{13,14},{15,16},{17,18},{19... | collective-permute-start | bytes 786440 | tf_op jit(solution)/shard_map/ppermute | solution.py:374
  5.3 19.5 %collective-permute-start.1 = (bf16[2,6,2,256,128]{4,3,2,1,0:T(8,128)(2,1)S(1)}, bf16[2,6,2,256,128]{4,3,2,1,0:T(8,128)(2,1)S(1)}, u32[]{:S(2)}, u32[]{:S(2)}) collective-permute-start(bf16[2,6,2,256,128]{4,3,2,1,0:T(8,128)(2,1)S(1)} %near_edge.1), channel_id=1, source_target_pairs={{0,1},{2,3},{4,5},{6,7},{8,9},{10,11},{12,13},{14,15},{16,17},{18,... | collective-permute-start | bytes 4718600 | tf_op jit(solution)/shard_map/ppermute | solution.py:376
  7.2 46.2 %collective-permute-start = (bf16[2,6,2,256,128]{4,3,2,1,0:T(8,128)(2,1)S(1)}, bf16[2,6,2,256,128]{4,3,2,1,0:T(8,128)(2,1)S(1)}, u32[]{:S(2)}, u32[]{:S(2)}) collective-permute-start(bf16[2,6,2,256,128]{4,3,2,1,0:T(8,128)(2,1)S(1)} %get-tuple-element.28), channel_id=1, source_target_pairs={{1,2},{3,4},{5,6},{7,8},{9,10},{11,12},{13,14},{15,16},{17,18},{19... | collective-permute-start | bytes 4718600 | tf_op jit(solution)/shard_map/ppermute | solution.py:375
  9.2 17.0 %copy-start.2 = (bf16[6,8,256,128]{3,2,1,0:T(8,128)(2,1)S(1)}, bf16[6,8,256,128]{3,2,1,0:T(8,128)(2,1)}, u32[]{:S(2)}) copy-start(bf16[6,8,256,128]{3,2,1,0:T(8,128)(2,1)} %h_hbm.7) | copy-start | bytes 9437188
  9.3 16.9 %copy-start.3 = (bf16[6,8,256,128]{3,2,1,0:T(8,128)(2,1)S(1)}, bf16[6,8,256,128]{3,2,1,0:T(8,128)(2,1)}, u32[]{:S(2)}) copy-start(bf16[6,8,256,128]{3,2,1,0:T(8,128)(2,1)} %q_hbm.7) | copy-start | bytes 9437188
  20.3 12.4 %collective-permute-start.3 = (bf16[2,4,32,512]{3,2,1,0:T(8,128)(2,1)S(1)}, bf16[2,4,32,512]{3,2,1,0:T(8,128)(2,1)S(1)}, u32[]{:S(2)}, u32[]{:S(2)}) collective-permute-start(bf16[2,4,32,512]{3,2,1,0:T(8,128)(2,1)S(1)} %get-tuple-element.35), channel_id=1, source_target_pairs={{0,64},{32,96},{64,128},{96,160},{128,192},{160,224},{192,0},{224,... | collective-permute-start | bytes 786440 | tf_op jit(solution)/shard_map/ppermute | solution.py:395
  21.9 15.2 %collective-permute-start.4 = (bf16[2,4,32,512]{3,2,1,0:T(8,128)(2,1)S(1)}, bf16[2,4,32,512]{3,2,1,0:T(8,128)(2,1)S(1)}, u32[]{:S(2)}, u32[]{:S(2)}) collective-permute-start(bf16[2,4,32,512]{3,2,1,0:T(8,128)(2,1)S(1)} %get-tuple-element.36), channel_id=1, source_target_pairs={{0,128},{32,160},{64,192},{96,224},{128,0},{160,32},{192,64},{224,... | collective-permute-start | bytes 786440 | tf_op jit(solution)/shard_map/ppermute | solution.py:395
  24.8 14.4 %collective-permute-start.5 = (bf16[2,4,32,512]{3,2,1,0:T(8,128)(2,1)S(1)}, bf16[2,4,32,512]{3,2,1,0:T(8,128)(2,1)S(1)}, u32[]{:S(2)}, u32[]{:S(2)}) collective-permute-start(bf16[2,4,32,512]{3,2,1,0:T(8,128)(2,1)S(1)} %get-tuple-element.37), channel_id=1, source_target_pairs={{0,192},{32,224},{64,0},{96,32},{128,64},{160,96},{192,128},{224,1... | collective-permute-start | bytes 786440 | tf_op jit(solution)/shard_map/ppermute | solution.py:395
  31.9 9.5 %collective-permute-start.6 = (bf16[2,2,32,512]{3,2,1,0:T(8,128)(2,1)S(1)}, bf16[2,2,32,512]{3,2,1,0:T(8,128)(2,1)S(1)}, u32[]{:S(2)}, u32[]{:S(2)}) collective-permute-start(bf16[2,2,32,512]{3,2,1,0:T(8,128)(2,1)S(1)} %get-tuple-element.38), channel_id=1, source_target_pairs={{0,64},{32,96},{64,128},{96,160},{128,192},{160,224},{192,0},{224,... | collective-permute-start | bytes 393224 | tf_op jit(solution)/shard_map/ppermute | solution.py:409
  32.7 10.0 %collective-permute-start.7 = (bf16[2,2,32,512]{3,2,1,0:T(8,128)(2,1)S(1)}, bf16[2,2,32,512]{3,2,1,0:T(8,128)(2,1)S(1)}, u32[]{:S(2)}, u32[]{:S(2)}) collective-permute-start(bf16[2,2,32,512]{3,2,1,0:T(8,128)(2,1)S(1)} %get-tuple-element.39), channel_id=1, source_target_pairs={{0,128},{32,160},{64,192},{96,224},{128,0},{160,32},{192,64},{224,... | collective-permute-start | bytes 393224 | tf_op jit(solution)/shard_map/ppermute | solution.py:409
  37.1 7.1 %collective-permute-start.8 = (bf16[2,2,32,512]{3,2,1,0:T(8,128)(2,1)S(1)}, bf16[2,2,32,512]{3,2,1,0:T(8,128)(2,1)S(1)}, u32[]{:S(2)}, u32[]{:S(2)}) collective-permute-start(bf16[2,2,32,512]{3,2,1,0:T(8,128)(2,1)S(1)} %get-tuple-element.40), channel_id=1, source_target_pairs={{0,192},{32,224},{64,0},{96,32},{128,64},{160,96},{192,128},{224,1... | collective-permute-start | bytes 393224 | tf_op jit(solution)/shard_map/ppermute | solution.py:409
  39.3 10.4 %collective-permute-start.9 = (bf16[2,2,32,512]{3,2,1,0:T(8,128)(2,1)S(1)}, bf16[2,2,32,512]{3,2,1,0:T(8,128)(2,1)S(1)}, u32[]{:S(2)}, u32[]{:S(2)}) collective-permute-start(bf16[2,2,32,512]{3,2,1,0:T(8,128)(2,1)S(1)} %get-tuple-element.43), channel_id=1, source_target_pairs={{0,64},{32,96},{64,128},{96,160},{128,192},{160,224},{192,0},{224,... | collective-permute-start | bytes 393224 | tf_op jit(solution)/shard_map/ppermute | solution.py:423
  41.4 8.3 %collective-permute-start.10 = (bf16[2,2,32,512]{3,2,1,0:T(8,128)(2,1)S(1)}, bf16[2,2,32,512]{3,2,1,0:T(8,128)(2,1)S(1)}, u32[]{:S(2)}, u32[]{:S(2)}) collective-permute-start(bf16[2,2,32,512]{3,2,1,0:T(8,128)(2,1)S(1)} %get-tuple-element.44), channel_id=1, source_target_pairs={{0,128},{32,160},{64,192},{96,224},{128,0},{160,32},{192,64},{224,... | collective-permute-start | bytes 393224 | tf_op jit(solution)/shard_map/ppermute | solution.py:423
  42.7 7.7 %collective-permute-start.11 = (bf16[2,2,32,512]{3,2,1,0:T(8,128)(2,1)S(1)}, bf16[2,2,32,512]{3,2,1,0:T(8,128)(2,1)S(1)}, u32[]{:S(2)}, u32[]{:S(2)}) collective-permute-start(bf16[2,2,32,512]{3,2,1,0:T(8,128)(2,1)S(1)} %get-tuple-element.45), channel_id=1, source_target_pairs={{0,192},{32,224},{64,0},{96,32},{128,64},{160,96},{192,128},{224,1... | collective-permute-start | bytes 393224 | tf_op jit(solution)/shard_map/ppermute | solution.py:423
  45.3 12.3 %collective-permute-start.12 = (bf16[6,32,512]{2,1,0:T(8,128)(2,1)S(1)}, bf16[6,32,512]{2,1,0:T(8,128)(2,1)S(1)}, u32[]{:S(2)}, u32[]{:S(2)}) collective-permute-start(bf16[6,32,512]{2,1,0:T(8,128)(2,1)S(1)} %get-tuple-element.48), channel_id=1, source_target_pairs={{0,32},{32,0},{64,96},{96,64},{128,160},{160,128},{192,224},{224,1... | collective-permute-start | bytes 589832 | tf_op jit(solution)/shard_map/ppermute | solution.py:438
  50.8 6.7 %collective-permute-start.13 = (bf16[2,32,512]{2,1,0:T(8,128)(2,1)S(1)}, bf16[2,32,512]{2,1,0:T(8,128)(2,1)S(1)}, u32[]{:S(2)}, u32[]{:S(2)}) collective-permute-start(bf16[2,32,512]{2,1,0:T(8,128)(2,1)S(1)} %get-tuple-element.50), channel_id=1, source_target_pairs={{0,32},{32,0},{64,96},{96,64},{128,160},{160,128},{192,224},{224,1... | collective-permute-start | bytes 196616 | tf_op jit(solution)/shard_map/ppermute | solution.py:438

commit v7 on v6

--- a/solution.py
+++ b/solution.py
@@ -43,51 +43,38 @@
         copy.wait()
 
 
-def far_edge_kernel(u_hbm, v_hbm, far_ref, sums_ref, sems):
-    at = pl.ds((u_hbm.shape[1] - EDGE) * core_index(), EDGE)
-    copies = [pltpu.make_async_copy(x.at[:, at], far_ref.at[f], sems.at[f]) for f, x in enumerate((u_hbm, v_hbm))]
-    run(copies)
-    for f, copy in enumerate(copies):
+def edges_kernel(u_hbm, v_hbm, far_ref, near_ref, sums_ref, sems):
+    parallels = u_hbm.shape[1]
+    core = core_index()
+    winds = tuple(enumerate((u_hbm, v_hbm)))
+    far_at = pl.ds((parallels - EDGE) * core, EDGE)
+    near_at = pl.ds((parallels - EDGE) * (1 - core), EDGE)
+    far = [pltpu.make_async_copy(x.at[:, far_at], far_ref.at[f], sems.at[f]) for f, x in winds]
+    near = [pltpu.make_async_copy(x.at[:, near_at], near_ref.at[f], sems.at[2 + f]) for f, x in winds]
+    run(far + near)
+    for f, copy in enumerate(far):
         copy.wait()
         for r in range(EDGE):
             total = far_ref[f, 0, r].astype(jnp.float32)
             for m in range(1, far_ref.shape[1]):
                 total = total + far_ref[f, m, r].astype(jnp.float32)
             sums_ref[f, r] = total.astype(jnp.bfloat16)
-
-
-def near_edge_kernel(u_hbm, v_hbm, sums_hbm, near_ref, sems):
-    del sums_hbm
-    at = pl.ds((u_hbm.shape[1] - EDGE) * (1 - core_index()), EDGE)
-    copies = [pltpu.make_async_copy(x.at[:, at], near_ref.at[f], sems.at[f]) for f, x in enumerate((u_hbm, v_hbm))]
-    run(copies)
-    finish(copies)
+    finish(near)
 
 
 def edges_call(u, v):
     members, _, meridians, levels = u.shape
     edge = jax.ShapeDtypeStruct((2, members, EDGE, meridians, levels), u.dtype)
-    far, sums = pl.pallas_call(
-        far_edge_kernel,
-        name="far_edge",
-        out_shape=(edge, jax.ShapeDtypeStruct((2, EDGE, meridians, levels), u.dtype)),
+    return pl.pallas_call(
+        edges_kernel,
+        name="edges",
+        out_shape=(edge, edge, jax.ShapeDtypeStruct((2, EDGE, meridians, levels), u.dtype)),
         in_specs=[ANY, ANY],
-        out_specs=(VMEM, VMEM),
-        scratch_shapes=[pltpu.SemaphoreType.DMA((2,))],
+        out_specs=(VMEM, VMEM, VMEM),
+        scratch_shapes=[pltpu.SemaphoreType.DMA((4,))],
         compiler_params=params(8),
-        cost_estimate=cost(1 << 20, 3 << 20),
+        cost_estimate=cost(1 << 20, 6 << 20),
     )(in_hbm(u), in_hbm(v))
-    near = pl.pallas_call(
-        near_edge_kernel,
-        name="near_edge",
-        out_shape=edge,
-        in_specs=[ANY, ANY, ANY],
-        out_specs=VMEM,
-        scratch_shapes=[pltpu.SemaphoreType.DMA((2,))],
-        compiler_params=params(8),
-        cost_estimate=cost(1 << 20, 3 << 20),
-    )(in_hbm(u), in_hbm(v), sums)
-    return far, near, sums
 
 
 def spread_over(at, psi_ref, bal_ref, slope_t, levels):
@@ -190,19 +177,27 @@
     ]
 
 
-def inner_kernel(chunk, u_hbm, v_hbm, h_hbm, q_hbm, psi_ref, bal_ref, slopes_ref, g_ref, *rest):
+def early_kernel(chunk, u_hbm, v_hbm, h_hbm, q_hbm, near_hbm, psi_ref, bal_ref, slopes_ref, g_ref, *rest):
     outs, scratch = rest[:-15], rest[-15:]
     u_ext, v_ext, h_buf, q_buf = scratch[:4]
     work = scratch[4:12]
     m_scr, sems, out_sems = scratch[12:]
+    parallels = u_hbm.shape[1]
     n = m_scr.shape[1]
-    inner = pl.ds(EDGE, n)
-    pairs = ((u_hbm, u_ext), (v_hbm, v_ext), (h_hbm.at[:, inner], h_buf), (q_hbm.at[:, inner], q_buf))
+    core = core_index()
+    own_to = pl.ds(EDGE * core, parallels)
+    near_to = pl.ds(parallels * (1 - core), EDGE)
+    row_from = EDGE * (1 - core)
+    rows = pl.ds(row_from, n)
+    pairs = [(u_hbm, u_ext.at[:, own_to]), (v_hbm, v_ext.at[:, own_to])]
+    pairs += [(near_hbm.at[0], u_ext.at[:, near_to]), (near_hbm.at[1], v_ext.at[:, near_to])]
+    pairs += [(h_hbm.at[:, rows], h_buf), (q_hbm.at[:, rows], q_buf)]
     copies = [pltpu.make_async_copy(x, y, sems.at[i]) for i, (x, y) in enumerate(pairs)]
     run(copies)
     g_ref[...] = jnp.zeros_like(g_ref)
-    finish(copies[:2])
-    compute_rows(n, EDGE, (u_ext, v_ext), (h_buf, q_buf), psi_ref, bal_ref, slopes_ref, work, g_ref, m_scr, False, chunk, lambda: finish(copies[2:]))
+    finish(copies[:4])
+    ready = lambda: finish(copies[4:])
+    compute_rows(n, row_from, (u_ext, v_ext), (h_buf, q_buf), psi_ref, bal_ref, slopes_ref, work, g_ref, m_scr, False, chunk, ready)
     sends = scatter_means(m_scr, outs, 0, out_sems, len(outs))
     run(sends)
     finish(sends)
@@ -225,23 +220,6 @@
         copies.append(pltpu.make_async_copy(halo.at[0], u_ext.at[:, halo_to], sems.at[4]))
         copies.append(pltpu.make_async_copy(halo.at[1], v_ext.at[:, halo_to], sems.at[5]))
     return copies
-
-
-def near_kernel(chunk, u_hbm, v_hbm, h_hbm, q_hbm, near_hbm, psi_ref, bal_ref, slopes_ref, g_in_ref, g_ref, *rest):
-    outs, scratch = rest[:-15], rest[-15:]
-    u_ext, v_ext, h_buf, q_buf = scratch[:4]
-    work = scratch[4:12]
-    m_scr, sems, out_sems = scratch[12:]
-    side = 1 - core_index()
-    copies = edge_copies(side, u_hbm, v_hbm, h_hbm, q_hbm, near_hbm, u_ext, v_ext, h_buf, q_buf, sems)
-    run(copies)
-    g_ref[...] = g_in_ref[...]
-    finish(copies)
-    row_from = (u_hbm.shape[1] - EDGE) * side
-    compute_rows(EDGE, row_from, (u_ext, v_ext), (h_buf, q_buf), psi_ref, bal_ref, slopes_ref, work, g_ref, m_scr, False, chunk)
-    sends = scatter_means(m_scr, outs, 0, out_sems, len(outs))
-    run(sends)
-    finish(sends)
 
 
 def far_means_kernel(chunk, u_hbm, v_hbm, h_hbm, q_hbm, after_hbm, far_sums_ref, psi_ref, bal_ref, slopes_ref, late_ref, *rest):
@@ -357,7 +335,6 @@
     peers = lax.axis_size("member")
     groups = peers // SIDE
     chunk = meridians // peers
-    inner = parallels - 2 * EDGE
     slopes = jnp.stack([slope_t, slope_q])
 
     across = [(i, i + 1) for i in range(1, count - 1, 2)]
@@ -382,31 +359,18 @@
     sum_shape = (3 * EDGE, meridians, levels)
     late_shape = jax.ShapeDtypeStruct((peers, EDGE, chunk, width), jnp.bfloat16)
     g, *means = pl.pallas_call(
-        functools.partial(inner_kernel, chunk),
-        name="inner_rows",
-        out_shape=(g_shape,) + handed(inner),
-        in_specs=[ANY] * 4 + [VMEM] * 3,
+        functools.partial(early_kernel, chunk),
+        name="early_rows",
+        out_shape=(g_shape,) + handed(parallels - EDGE),
+        in_specs=[ANY] * 5 + [VMEM] * 3,
         out_specs=(VMEM,) + (ANY,) * groups,
-        scratch_shapes=row_scratch(dims, inner, parallels)
-        + [pltpu.VMEM((peers, inner, chunk, width), jnp.bfloat16), dma((4,)), dma((groups,))],
-        compiler_params=params(22),
-        cost_estimate=row_cost(dims, inner),
-    )(u, v, in_hbm(h), in_hbm(q), psi, bal, slopes)
+        scratch_shapes=row_scratch(dims, parallels - EDGE, parallels + EDGE)
+        + [pltpu.VMEM((peers, parallels - EDGE, chunk, width), jnp.bfloat16), dma((6,)), dma((groups,))],
+        compiler_params=params(26),
+        cost_estimate=row_cost(dims, parallels - EDGE),
+    )(u, v, in_hbm(h), in_hbm(q), near, psi, bal, slopes)
+    after = means[0]
     means = [x if r == 0 else lax.ppermute(x, "member", along_y(r)) for r, x in enumerate(means)]
-
-    g, *near_means = pl.pallas_call(
-        functools.partial(near_kernel, chunk),
-        name="near_rows",
-        out_shape=(g_shape,) + handed(EDGE),
-        in_specs=[ANY] * 5 + [VMEM] * 4,
-        out_specs=(VMEM,) + (ANY,) * groups,
-        scratch_shapes=row_scratch(dims, EDGE, 3 * EDGE)
-        + [pltpu.VMEM((peers, EDGE, chunk, width), jnp.bfloat16), dma((6,)), dma((groups,))],
-        compiler_params=params(16),
-        cost_estimate=row_cost(dims, EDGE),
-    )(u, v, h, q, near, psi, bal, slopes, g)
-    after = near_means[0]
-    near_means = [x if r == 0 else lax.ppermute(x, "member", along_y(r)) for r, x in enumerate(near_means)]
 
     late, *far_means = pl.pallas_call(
         functools.partial(far_means_kernel, chunk),
@@ -423,7 +387,7 @@
     far_means = [x if r == 0 else lax.ppermute(x, "member", along_y(r)) for r, x in enumerate(far_means)]
 
     halves = []
-    for part in (means + near_means, far_means):
+    for part in (means, far_means):
         rows = sum(x.shape[1] for x in part[::groups])
         half = jax.ShapeDtypeStruct((rows, chunk, width), jnp.bfloat16)
         g, mine, theirs = pl.pallas_call(

time: 81.6 us -> 84.4 us (1.034); the launches traced: 80.2 us -> 84.1 us
  waiting for transfers between devices: 6.55 us -> 15.8 us
  starting transfers between devices: 23.4 us -> 18 us
    ppermute x9 -> x6, waiting for transfers between devices: 6.53 us -> 15.8 us  [on_device(): lax.ppermute(x, 'member', along_y(r))]
    ppermute x9 -> x6, starting transfers between devices: 11.8 us -> 7.65 us  [on_device(): lax.ppermute(x, 'member', along_y(r))]
    ppermute x1, starting transfers between devices: 2.32 us -> 4.25 us  [on_device(): far_sums = lax.ppermute(far_sums, 'space', across)]
    ppermute x1, starting transfers between devices: 1.95 us -> 0.09 us  [on_device(): near = lax.ppermute(near_edge, 'space', within)]
    ppermute x2, starting transfers between devices: 5.39 us -> 4.05 us  [on_device(): halves += [mine, lax.ppermute(theirs, 'member', along_x)]]
    pallas_call x4 -> x2, Pallas kernels: 19.6 us -> 18.7 us  [the longest x1 16.7 us: on_device(): pl.pallas_call(functools.partial(early_kernel, chunk), name='early_rows',...]
  transfers between devices with their start and end apart: 14 -> 11, of which waited for: 4 -> 5; matrix products, arithmetic and copies ran while one was open for 0% -> 0% of each run, Pallas kernels for 32% -> 29%
where the time goes in v7:
time: 84.4 us; the launch traced here: 84.1 us
  Pallas kernels  26.9 us (32%)
  blocking collectives  21.5 us (25%)
  starting transfers between devices  18 us (21%)
  waiting for transfers between devices  15.8 us (19%)
  local copies, waits for them, and re-layouts  0.87 us (1%)
    all_to_all x1, blocking collectives, on_device(): lax.all_to_all(g.reshape(peers, width // peers, width), 'member', 0, 0, t...  21.5 us
    pallas_call x1, Pallas kernels, on_device(): pl.pallas_call(functools.partial(early_kernel, chunk), name='early_rows',...  16.7 us
    ppermute x6, waiting for transfers between devices, on_device(): lax.ppermute(x, 'member', along_y(r))  15.8 us
    ppermute x6, starting transfers between devices, on_device(): lax.ppermute(x, 'member', along_y(r))  7.65 us
    ppermute x1, starting transfers between devices, on_device(): far_sums = lax.ppermute(far_sums, 'space', across)  4.25 us
    pallas_call x1, Pallas kernels, on_device(): pl.pallas_call(functools.partial(far_kernel, chunk), name='far_rows', out...  4.09 us
    ppermute x2, starting transfers between devices, on_device(): halves += [mine, lax.ppermute(theirs, 'member', along_x)]  4.05 us
    pallas_call x1, Pallas kernels, on_device(): pl.pallas_call(functools.partial(far_means_kernel, chunk), name='far_mean...  2.2 us
  transfers between devices with their start and end apart: 11, of which 5 were waited for; matrix products, arithmetic and copies ran while one was open for 0% of the time, Pallas kernels for 29%

profile of v7, /device:TPU:2, one launch (start us, length us, event | category | flops | bytes accessed | tf_op | source)
XLA Modules:
  0.0 84.1 jit_solution(17207842530349044985)
XLA Ops:
  0.0 2.0 %edges.1 = (bf16[2,6,2,256,128]{4,3,2,1,0:T(8,128)(2,1)S(1)}, bf16[2,6,2,256,128]{4,3,2,1,0:T(8,128)(2,1)S(1)}, bf16[2,2,256,128]{3,2,1,0:T(8,128)(2,1)S(1)}) custom-call(bf16[6,8,256,128]{3,2,1,0:T(8,128)(2,1)} %u_hbm.7, bf16[6,8,256,128]{3,2,1,0:T(8,128)(2,1)} %v_hbm.7), custom_call_target="tpu_custom_call" | custom-call | flops 1048576 | bytes 6291456 | tf_op jit(solution)/shard_map/edges/pallas_call | solution.py:68
  2.2 4.3 %collective-permute-start.2 = (bf16[2,2,256,128]{3,2,1,0:T(8,128)(2,1)S(1)}, bf16[2,2,256,128]{3,2,1,0:T(8,128)(2,1)S(1)}, u32[]{:S(2)}, u32[]{:S(2)}) collective-permute-start(bf16[2,2,256,128]{3,2,1,0:T(8,128)(2,1)S(1)} %get-tuple-element.27), channel_id=1, source_target_pairs={{1,2},{3,4},{5,6},{7,8},{9,10},{11,12},{13,14},{15,16},{17,18},{19... | collective-permute-start | bytes 786440 | tf_op jit(solution)/shard_map/ppermute | solution.py:351
  6.4 1.9 %collective-permute-start = (bf16[2,6,2,256,128]{4,3,2,1,0:T(8,128)(2,1)S(1)}, bf16[2,6,2,256,128]{4,3,2,1,0:T(8,128)(2,1)S(1)}, u32[]{:S(2)}, u32[]{:S(2)}) collective-permute-start(bf16[2,6,2,256,128]{4,3,2,1,0:T(8,128)(2,1)S(1)} %get-tuple-element.24), channel_id=1, source_target_pairs={{1,2},{3,4},{5,6},{7,8},{9,10},{11,12},{13,14},{15,16},{17,18},{19... | collective-permute-start | bytes 4718600 | tf_op jit(solution)/shard_map/ppermute | solution.py:352
  8.5 0.8 copy-done.5
  9.3 16.7 %early_rows.1 = (f32[512,512]{1,0:T(8,128)S(1)}, bf16[2,6,32,512]{3,2,1,0:T(8,128)(2,1)S(1)}, bf16[2,6,32,512]{3,2,1,0:T(8,128)(2,1)S(1)}, bf16[2,6,32,512]{3,2,...) custom-call(bf16[6,8,256,128]{3,2,1,0:T(8,128)(2,1)S(1)} %copy-done, bf16[6,8,256,128]{3,2,1,0:T(8,128)(2,1)S(1)} %copy-done.1, ...), custom_call_target="tpu_custom_call" | custom-call | flops 38654705664 | bytes 33554432 | tf_op jit(solution)/shard_map/early_rows/pallas_call | solution.py:361
  26.0 1.4 %collective-permute-start.3 = (bf16[2,6,32,512]{3,2,1,0:T(8,128)(2,1)S(1)}, bf16[2,6,32,512]{3,2,1,0:T(8,128)(2,1)S(1)}, u32[]{:S(2)}, u32[]{:S(2)}) collective-permute-start(bf16[2,6,32,512]{3,2,1,0:T(8,128)(2,1)S(1)} %get-tuple-element.30), channel_id=1, source_target_pairs={{0,64},{32,96},{64,128},{96,160},{128,192},{160,224},{192,0},{224,... | collective-permute-start | bytes 1179656 | tf_op jit(solution)/shard_map/ppermute | solution.py:373
  27.4 2.9 %collective-permute-start.4 = (bf16[2,6,32,512]{3,2,1,0:T(8,128)(2,1)S(1)}, bf16[2,6,32,512]{3,2,1,0:T(8,128)(2,1)S(1)}, u32[]{:S(2)}, u32[]{:S(2)}) collective-permute-start(bf16[2,6,32,512]{3,2,1,0:T(8,128)(2,1)S(1)} %get-tuple-element.31), channel_id=1, source_target_pairs={{0,128},{32,160},{64,192},{96,224},{128,0},{160,32},{192,64},{224,... | collective-permute-start | bytes 1179656 | tf_op jit(solution)/shard_map/ppermute | solution.py:373
  30.3 1.3 %collective-permute-start.5 = (bf16[2,6,32,512]{3,2,1,0:T(8,128)(2,1)S(1)}, bf16[2,6,32,512]{3,2,1,0:T(8,128)(2,1)S(1)}, u32[]{:S(2)}, u32[]{:S(2)}) collective-permute-start(bf16[2,6,32,512]{3,2,1,0:T(8,128)(2,1)S(1)} %get-tuple-element.32), channel_id=1, source_target_pairs={{0,192},{32,224},{64,0},{96,32},{128,64},{160,96},{192,128},{224,1... | collective-permute-start | bytes 1179656 | tf_op jit(solution)/shard_map/ppermute | solution.py:373
  31.6 2.2 %far_means.1 = (bf16[8,2,32,512]{3,2,1,0:T(8,128)(2,1)S(1)}, bf16[2,2,32,512]{3,2,1,0:T(8,128)(2,1)S(1)}, bf16[2,2,32,512]{3,2,1,0:T(8,128)(2,1)S(1)}, bf16[2,2,...) custom-call(bf16[6,8,256,128]{3,2,1,0:T(8,128)(2,1)S(1)} %copy-done, bf16[6,8,256,128]{3,2,1,0:T(8,128)(2,1)S(1)} %copy-done.1, ...), custom_call_target="tpu_custom_call" | custom-call | flops 12884901888 | bytes 33554432 | tf_op jit(solution)/shard_map/far_means/pallas_call | solution.py:375
  33.8 0.8 collective-permute-start.6
  34.6 4.9 %collective-permute-done.3.rest_1_ = bf16[2,6,32,512]{3,2,1,0:T(8,128)(2,1)S(1)} collective-permute-done((bf16[2,6,32,512]{3,2,1,0:T(8,128)(2,1)S(1)}, bf16[2,6,32,512]{3,2,1,0:T(8,128)(2,1)S(1)}, u32[]{:S(2)}, u32[]{:S(2)}) %collective-permute-start.3) | collective-permute-done | bytes 393248 | tf_op jit(solution)/shard_map/ppermute | solution.py:373
  39.5 1.3 %collective-permute-start.7 = (bf16[2,2,32,512]{3,2,1,0:T(8,128)(2,1)S(1)}, bf16[2,2,32,512]{3,2,1,0:T(8,128)(2,1)S(1)}, u32[]{:S(2)}, u32[]{:S(2)}) collective-permute-start(bf16[2,2,32,512]{3,2,1,0:T(8,128)(2,1)S(1)} %get-tuple-element.36), channel_id=1, source_target_pairs={{0,128},{32,160},{64,192},{96,224},{128,0},{160,32},{192,64},{224,... | collective-permute-start | bytes 393224 | tf_op jit(solution)/shard_map/ppermute | solution.py:387
  40.8 7.7 %collective-permute-done.4.rest_2_ = bf16[2,6,32,512]{3,2,1,0:T(8,128)(2,1)S(1)} collective-permute-done((bf16[2,6,32,512]{3,2,1,0:T(8,128)(2,1)S(1)}, bf16[2,6,32,512]{3,2,1,0:T(8,128)(2,1)S(1)}, u32[]{:S(2)}, u32[]{:S(2)}) %collective-permute-start.4) | collective-permute-done | bytes 393248 | tf_op jit(solution)/shard_map/ppermute | solution.py:373
  48.4 0.4 collective-permute-done.5.rest_3_
  48.8 1.1 %between.2 = (f32[512,512]{1,0:T(8,128)S(1)}, bf16[6,32,512]{2,1,0:T(8,128)(2,1)S(1)}, bf16[6,32,512]{2,1,0:T(8,128)(2,1)S(1)}) custom-call(f32[512,512]{1,0:T(8,128)S(1)} %get-tuple-element.29.g_in_ref, bf16[2,6,32,512]{3,2,1,0:T(8,128)(2,1)S(1)} %get-tuple-element.26.after_hbm.rest_0_, bf16[2,6,32,512]{3,2,1,0:T(8,128)(2,1)S(1)} %collective-permute-done.3.rest_1_, ...), custom_call_target="tpu_custom_call" | custom-call | flops 536870912 | bytes 3145728 | tf_op jit(solution)/shard_map/between/pallas_call | solution.py:393
  49.9 1.9 %collective-permute-start.9 = (bf16[6,32,512]{2,1,0:T(8,128)(2,1)S(1)}, bf16[6,32,512]{2,1,0:T(8,128)(2,1)S(1)}, u32[]{:S(2)}, u32[]{:S(2)}) collective-permute-start(bf16[6,32,512]{2,1,0:T(8,128)(2,1)S(1)} %get-tuple-element.40), channel_id=1, source_target_pairs={{0,32},{32,0},{64,96},{96,64},{128,160},{160,128},{192,224},{224,1... | collective-permute-start | bytes 589832 | tf_op jit(solution)/shard_map/ppermute | solution.py:402
  51.7 2.2 %collective-permute-done.7.rest_2_ = bf16[2,2,32,512]{3,2,1,0:T(8,128)(2,1)S(1)} collective-permute-done((bf16[2,2,32,512]{3,2,1,0:T(8,128)(2,1)S(1)}, bf16[2,2,32,512]{3,2,1,0:T(8,128)(2,1)S(1)}, u32[]{:S(2)}, u32[]{:S(2)}) %collective-permute-start.7) | collective-permute-done | bytes 131104 | tf_op jit(solution)/shard_map/ppermute | solution.py:387
  54.0 0.7 collective-permute-done.8.rest_3_
  54.7 0.5 between.3
  55.1 2.2 %collective-permute-start.10 = (bf16[2,32,512]{2,1,0:T(8,128)(2,1)S(1)}, bf16[2,32,512]{2,1,0:T(8,128)(2,1)S(1)}, u32[]{:S(2)}, u32[]{:S(2)}) collective-permute-start(bf16[2,32,512]{2,1,0:T(8,128)(2,1)S(1)} %get-tuple-element.42), channel_id=1, source_target_pairs={{0,32},{32,0},{64,96},{96,64},{128,160},{160,128},{192,224},{224,1... | collective-permute-start | bytes 196616 | tf_op jit(solution)/shard_map/ppermute | solution.py:402
  57.4 4.1 %far_rows.1.g_in_ref = f32[512,512]{1,0:T(8,128)S(1)} custom-call(bf16[6,8,256,128]{3,2,1,0:T(8,128)(2,1)S(1)} %copy-done, bf16[6,8,256,128]{3,2,1,0:T(8,128)(2,1)S(1)} %copy-done.1, bf16[6,8,256,128]{3,2,1,0:T(8,128)(2,1)S(1)} %copy-done.2, bf16[6,8,256,128]{3,2,1,0:T(8,128)(2,1)S(1)} %copy-done.3, ...), custom_call_target="tpu_custom_call" | custom-call | flops 12884901888 | bytes 33554432 | tf_op jit(solution)/shard_map/far_rows/pallas_call | solution.py:404
  61.5 0.4 halves.1
  61.8 21.5 %all_to_all.5 = f32[8,64,512]{2,1,0:T(8,128)S(1)} all-to-all(f32[8,64,512]{2,1,0:T(8,128)S(1)} %bitcast.5), channel_id=1, replica_groups=mesh['member'=8,'space'=32] {'member'}, dimensions={0} | all-to-all | bytes 2097152 | tf_op jit(solution)/shard_map/all_to_all | solution.py:425
  83.4 0.7 multiply_bitcast_fusion
  (25 shorter events, 0.2 us)
Async XLA Ops:
  0.0 8.4 %copy-start.1 = (bf16[6,8,256,128]{3,2,1,0:T(8,128)(2,1)S(1)}, bf16[6,8,256,128]{3,2,1,0:T(8,128)(2,1)}, u32[]{:S(2)}) copy-start(bf16[6,8,256,128]{3,2,1,0:T(8,128)(2,1)} %v_hbm.7) | copy-start | bytes 9437188
  0.0 8.4 %copy-start = (bf16[6,8,256,128]{3,2,1,0:T(8,128)(2,1)S(1)}, bf16[6,8,256,128]{3,2,1,0:T(8,128)(2,1)}, u32[]{:S(2)}) copy-start(bf16[6,8,256,128]{3,2,1,0:T(8,128)(2,1)} %u_hbm.7) | copy-start | bytes 9437188
  0.0 8.4 %copy-start.6 = (f32[128]{0:T(128)S(1)}, f32[128]{0:T(128)}, u32[]{:S(2)}) copy-start(f32[128]{0:T(128)} %param.15) | copy-start | bytes 1540
  0.0 8.4 %copy-start.7 = (f32[128]{0:T(128)S(1)}, f32[128]{0:T(128)}, u32[]{:S(2)}) copy-start(f32[128]{0:T(128)} %param.14) | copy-start | bytes 1540
  0.0 8.4 %copy-start.4 = (f32[8,256]{1,0:T(8,128)S(1)}, f32[8,256]{1,0:T(8,128)}, u32[]{:S(2)}) copy-start(f32[8,256]{1,0:T(8,128)} %psi_ref.5) | copy-start | bytes 24580
  2.1 6.4 %collective-permute-start.1 = (bf16[2,6,2,256,128]{4,3,2,1,0:T(8,128)(2,1)S(1)}, bf16[2,6,2,256,128]{4,3,2,1,0:T(8,128)(2,1)S(1)}, u32[]{:S(2)}, u32[]{:S(2)}) collective-permute-start(bf16[2,6,2,256,128]{4,3,2,1,0:T(8,128)(2,1)S(1)} %get-tuple-element.25), channel_id=1, source_target_pairs={{0,1},{2,3},{4,5},{6,7},{8,9},{10,11},{12,13},{14,15},{16,17},{18,... | collective-permute-start | bytes 4718600 | tf_op jit(solution)/shard_map/ppermute | solution.py:353
  2.2 29.4 %collective-permute-start.2 = (bf16[2,2,256,128]{3,2,1,0:T(8,128)(2,1)S(1)}, bf16[2,2,256,128]{3,2,1,0:T(8,128)(2,1)S(1)}, u32[]{:S(2)}, u32[]{:S(2)}) collective-permute-start(bf16[2,2,256,128]{3,2,1,0:T(8,128)(2,1)S(1)} %get-tuple-element.27), channel_id=1, source_target_pairs={{1,2},{3,4},{5,6},{7,8},{9,10},{11,12},{13,14},{15,16},{17,18},{19... | collective-permute-start | bytes 786440 | tf_op jit(solution)/shard_map/ppermute | solution.py:351
  6.4 50.9 %collective-permute-start = (bf16[2,6,2,256,128]{4,3,2,1,0:T(8,128)(2,1)S(1)}, bf16[2,6,2,256,128]{4,3,2,1,0:T(8,128)(2,1)S(1)}, u32[]{:S(2)}, u32[]{:S(2)}) collective-permute-start(bf16[2,6,2,256,128]{4,3,2,1,0:T(8,128)(2,1)S(1)} %get-tuple-element.24), channel_id=1, source_target_pairs={{1,2},{3,4},{5,6},{7,8},{9,10},{11,12},{13,14},{15,16},{17,18},{19... | collective-permute-start | bytes 4718600 | tf_op jit(solution)/shard_map/ppermute | solution.py:352
  8.4 23.2 %copy-start.2 = (bf16[6,8,256,128]{3,2,1,0:T(8,128)(2,1)S(1)}, bf16[6,8,256,128]{3,2,1,0:T(8,128)(2,1)}, u32[]{:S(2)}) copy-start(bf16[6,8,256,128]{3,2,1,0:T(8,128)(2,1)} %h_hbm.5) | copy-start | bytes 9437188
  8.4 23.2 %copy-start.3 = (bf16[6,8,256,128]{3,2,1,0:T(8,128)(2,1)S(1)}, bf16[6,8,256,128]{3,2,1,0:T(8,128)(2,1)}, u32[]{:S(2)}) copy-start(bf16[6,8,256,128]{3,2,1,0:T(8,128)(2,1)} %q_hbm.5) | copy-start | bytes 9437188
  8.5 0.8 %copy-start.5 = (f32[8,256]{1,0:T(8,128)S(1)}, f32[8,256]{1,0:T(8,128)}, u32[]{:S(2)}) copy-start(f32[8,256]{1,0:T(8,128)} %bal_ref.5) | copy-start | bytes 24580
  26.0 13.5 %collective-permute-start.3 = (bf16[2,6,32,512]{3,2,1,0:T(8,128)(2,1)S(1)}, bf16[2,6,32,512]{3,2,1,0:T(8,128)(2,1)S(1)}, u32[]{:S(2)}, u32[]{:S(2)}) collective-permute-start(bf16[2,6,32,512]{3,2,1,0:T(8,128)(2,1)S(1)} %get-tuple-element.30), channel_id=1, source_target_pairs={{0,64},{32,96},{64,128},{96,160},{128,192},{160,224},{192,0},{224,... | collective-permute-start | bytes 1179656 | tf_op jit(solution)/shard_map/ppermute | solution.py:373
  27.4 21.1 %collective-permute-start.4 = (bf16[2,6,32,512]{3,2,1,0:T(8,128)(2,1)S(1)}, bf16[2,6,32,512]{3,2,1,0:T(8,128)(2,1)S(1)}, u32[]{:S(2)}, u32[]{:S(2)}) collective-permute-start(bf16[2,6,32,512]{3,2,1,0:T(8,128)(2,1)S(1)} %get-tuple-element.31), channel_id=1, source_target_pairs={{0,128},{32,160},{64,192},{96,224},{128,0},{160,32},{192,64},{224,... | collective-permute-start | bytes 1179656 | tf_op jit(solution)/shard_map/ppermute | solution.py:373
  30.3 18.5 %collective-permute-start.5 = (bf16[2,6,32,512]{3,2,1,0:T(8,128)(2,1)S(1)}, bf16[2,6,32,512]{3,2,1,0:T(8,128)(2,1)S(1)}, u32[]{:S(2)}, u32[]{:S(2)}) collective-permute-start(bf16[2,6,32,512]{3,2,1,0:T(8,128)(2,1)S(1)} %get-tuple-element.32), channel_id=1, source_target_pairs={{0,192},{32,224},{64,0},{96,32},{128,64},{160,96},{192,128},{224,1... | collective-permute-start | bytes 1179656 | tf_op jit(solution)/shard_map/ppermute | solution.py:373
  33.8 17.9 %collective-permute-start.6 = (bf16[2,2,32,512]{3,2,1,0:T(8,128)(2,1)S(1)}, bf16[2,2,32,512]{3,2,1,0:T(8,128)(2,1)S(1)}, u32[]{:S(2)}, u32[]{:S(2)}) collective-permute-start(bf16[2,2,32,512]{3,2,1,0:T(8,128)(2,1)S(1)} %get-tuple-element.35), channel_id=1, source_target_pairs={{0,64},{32,96},{64,128},{96,160},{128,192},{160,224},{192,0},{224,... | collective-permute-start | bytes 393224 | tf_op jit(solution)/shard_map/ppermute | solution.py:387
  39.5 14.5 %collective-permute-start.7 = (bf16[2,2,32,512]{3,2,1,0:T(8,128)(2,1)S(1)}, bf16[2,2,32,512]{3,2,1,0:T(8,128)(2,1)S(1)}, u32[]{:S(2)}, u32[]{:S(2)}) collective-permute-start(bf16[2,2,32,512]{3,2,1,0:T(8,128)(2,1)S(1)} %get-tuple-element.36), channel_id=1, source_target_pairs={{0,128},{32,160},{64,192},{96,224},{128,0},{160,32},{192,64},{224,... | collective-permute-start | bytes 393224 | tf_op jit(solution)/shard_map/ppermute | solution.py:387
  48.4 6.2 %collective-permute-start.8 = (bf16[2,2,32,512]{3,2,1,0:T(8,128)(2,1)S(1)}, bf16[2,2,32,512]{3,2,1,0:T(8,128)(2,1)S(1)}, u32[]{:S(2)}, u32[]{:S(2)}) collective-permute-start(bf16[2,2,32,512]{3,2,1,0:T(8,128)(2,1)S(1)} %get-tuple-element.37), channel_id=1, source_target_pairs={{0,192},{32,224},{64,0},{96,32},{128,64},{160,96},{192,128},{224,1... | collective-permute-start | bytes 393224 | tf_op jit(solution)/shard_map/ppermute | solution.py:387
  49.9 11.6 %collective-permute-start.9 = (bf16[6,32,512]{2,1,0:T(8,128)(2,1)S(1)}, bf16[6,32,512]{2,1,0:T(8,128)(2,1)S(1)}, u32[]{:S(2)}, u32[]{:S(2)}) collective-permute-start(bf16[6,32,512]{2,1,0:T(8,128)(2,1)S(1)} %get-tuple-element.40), channel_id=1, source_target_pairs={{0,32},{32,0},{64,96},{96,64},{128,160},{160,128},{192,224},{224,1... | collective-permute-start | bytes 589832 | tf_op jit(solution)/shard_map/ppermute | solution.py:402
  55.1 6.3 %collective-permute-start.10 = (bf16[2,32,512]{2,1,0:T(8,128)(2,1)S(1)}, bf16[2,32,512]{2,1,0:T(8,128)(2,1)S(1)}, u32[]{:S(2)}, u32[]{:S(2)}) collective-permute-start(bf16[2,32,512]{2,1,0:T(8,128)(2,1)S(1)} %get-tuple-element.42), channel_id=1, source_target_pairs={{0,32},{32,0},{64,96},{96,64},{128,160},{160,128},{192,224},{224,1... | collective-permute-start | bytes 196616 | tf_op jit(solution)/shard_map/ppermute | solution.py:402

commit v8 on v6

--- a/solution.py
+++ b/solution.py
@@ -43,51 +43,38 @@
         copy.wait()
 
 
-def far_edge_kernel(u_hbm, v_hbm, far_ref, sums_ref, sems):
-    at = pl.ds((u_hbm.shape[1] - EDGE) * core_index(), EDGE)
-    copies = [pltpu.make_async_copy(x.at[:, at], far_ref.at[f], sems.at[f]) for f, x in enumerate((u_hbm, v_hbm))]
-    run(copies)
-    for f, copy in enumerate(copies):
+def edges_kernel(u_hbm, v_hbm, far_ref, near_ref, sums_ref, sems):
+    parallels = u_hbm.shape[1]
+    core = core_index()
+    winds = tuple(enumerate((u_hbm, v_hbm)))
+    far_at = pl.ds((parallels - EDGE) * core, EDGE)
+    near_at = pl.ds((parallels - EDGE) * (1 - core), EDGE)
+    far = [pltpu.make_async_copy(x.at[:, far_at], far_ref.at[f], sems.at[f]) for f, x in winds]
+    near = [pltpu.make_async_copy(x.at[:, near_at], near_ref.at[f], sems.at[2 + f]) for f, x in winds]
+    run(far + near)
+    for f, copy in enumerate(far):
         copy.wait()
         for r in range(EDGE):
             total = far_ref[f, 0, r].astype(jnp.float32)
             for m in range(1, far_ref.shape[1]):
                 total = total + far_ref[f, m, r].astype(jnp.float32)
             sums_ref[f, r] = total.astype(jnp.bfloat16)
-
-
-def near_edge_kernel(u_hbm, v_hbm, sums_hbm, near_ref, sems):
-    del sums_hbm
-    at = pl.ds((u_hbm.shape[1] - EDGE) * (1 - core_index()), EDGE)
-    copies = [pltpu.make_async_copy(x.at[:, at], near_ref.at[f], sems.at[f]) for f, x in enumerate((u_hbm, v_hbm))]
-    run(copies)
-    finish(copies)
+    finish(near)
 
 
 def edges_call(u, v):
     members, _, meridians, levels = u.shape
     edge = jax.ShapeDtypeStruct((2, members, EDGE, meridians, levels), u.dtype)
-    far, sums = pl.pallas_call(
-        far_edge_kernel,
-        name="far_edge",
-        out_shape=(edge, jax.ShapeDtypeStruct((2, EDGE, meridians, levels), u.dtype)),
+    return pl.pallas_call(
+        edges_kernel,
+        name="edges",
+        out_shape=(edge, edge, jax.ShapeDtypeStruct((2, EDGE, meridians, levels), u.dtype)),
         in_specs=[ANY, ANY],
-        out_specs=(VMEM, VMEM),
-        scratch_shapes=[pltpu.SemaphoreType.DMA((2,))],
+        out_specs=(VMEM, VMEM, VMEM),
+        scratch_shapes=[pltpu.SemaphoreType.DMA((4,))],
         compiler_params=params(8),
-        cost_estimate=cost(1 << 20, 3 << 20),
+        cost_estimate=cost(1 << 20, 6 << 20),
     )(in_hbm(u), in_hbm(v))
-    near = pl.pallas_call(
-        near_edge_kernel,
-        name="near_edge",
-        out_shape=edge,
-        in_specs=[ANY, ANY, ANY],
-        out_specs=VMEM,
-        scratch_shapes=[pltpu.SemaphoreType.DMA((2,))],
-        compiler_params=params(8),
-        cost_estimate=cost(1 << 20, 3 << 20),
-    )(in_hbm(u), in_hbm(v), sums)
-    return far, near, sums
 
 
 def spread_over(at, psi_ref, bal_ref, slope_t, levels):

time: 81.6 us -> 95.2 us (1.17); the launches traced: 80.2 us -> 95 us
  waiting for transfers between devices: 6.55 us -> 19 us
  starting transfers between devices: 23.4 us -> 31.3 us
  blocking collectives: 21.5 us -> 16.1 us
    ppermute x1, waiting for transfers between devices: 0.01 us -> 14.9 us  [on_device(): far_sums = lax.ppermute(far_sums, 'space', across)]
    all_to_all x1, blocking collectives: 21.5 us -> 16.1 us  [on_device(): lax.all_to_all(g.reshape(peers, width // peers, width), 'member', 0, 0, t...]
    ppermute x9, starting transfers between devices: 11.8 us -> 15.9 us  [on_device(): lax.ppermute(x, 'member', along_y(r))]
    ppermute x2, starting transfers between devices: 5.39 us -> 9.31 us  [on_device(): halves += [mine, lax.ppermute(theirs, 'member', along_x)]]
    ppermute x9, waiting for transfers between devices: 6.53 us -> 4.11 us  [on_device(): lax.ppermute(x, 'member', along_y(r))]
    pallas_call x2 -> x1, Pallas kernels: 2.89 us -> 2.04 us  [edges_call(): pl.pallas_call(edges_kernel, name='edges', out_shape=(edge, edge, jax.Sha...]
  transfers between devices with their start and end apart: 14 -> 14, of which waited for: 4 -> 2; matrix products, arithmetic and copies ran while one was open for 0% -> 0% of each run, Pallas kernels for 32% -> 26%
where the time goes in v8:
time: 95.2 us; the launch traced here: 95 us
  starting transfers between devices  31.3 us (33%)
  Pallas kernels  26.9 us (28%)
  waiting for transfers between devices  19 us (20%)
  blocking collectives  16.1 us (17%)
    all_to_all x1, blocking collectives, on_device(): lax.all_to_all(g.reshape(peers, width // peers, width), 'member', 0, 0, t...  16.1 us
    ppermute x9, starting transfers between devices, on_device(): lax.ppermute(x, 'member', along_y(r))  15.9 us
    ppermute x1, waiting for transfers between devices, on_device(): far_sums = lax.ppermute(far_sums, 'space', across)  14.9 us
    pallas_call x1, Pallas kernels, on_device(): pl.pallas_call(functools.partial(inner_kernel, chunk), name='inner_rows',...  11 us
    ppermute x2, starting transfers between devices, on_device(): halves += [mine, lax.ppermute(theirs, 'member', along_x)]  9.31 us
    pallas_call x1, Pallas kernels, on_device(): pl.pallas_call(functools.partial(near_kernel, chunk), name='near_rows', o...  5.68 us
    ppermute x9, waiting for transfers between devices, on_device(): lax.ppermute(x, 'member', along_y(r))  4.11 us
    pallas_call x1, Pallas kernels, on_device(): pl.pallas_call(functools.partial(far_kernel, chunk), name='far_rows', out...  4.1 us
  transfers between devices with their start and end apart: 14, of which 2 were waited for; matrix products, arithmetic and copies ran while one was open for 0% of the time, Pallas kernels for 26%

profile of v8, /device:TPU:2, one launch (start us, length us, event | category | flops | bytes accessed | tf_op | source)
XLA Modules:
  0.0 95.0 jit_solution(5827709602873085722)
XLA Ops:
  0.0 2.0 %edges.1 = (bf16[2,6,2,256,128]{4,3,2,1,0:T(8,128)(2,1)S(1)}, bf16[2,6,2,256,128]{4,3,2,1,0:T(8,128)(2,1)S(1)}, bf16[2,2,256,128]{3,2,1,0:T(8,128)(2,1)S(1)}) custom-call(bf16[6,8,256,128]{3,2,1,0:T(8,128)(2,1)} %u_hbm.9, bf16[6,8,256,128]{3,2,1,0:T(8,128)(2,1)} %v_hbm.9), custom_call_target="tpu_custom_call" | custom-call | flops 1048576 | bytes 6291456 | tf_op jit(solution)/shard_map/edges/pallas_call | solution.py:68
  2.1 2.1 %collective-permute-start = (bf16[2,6,2,256,128]{4,3,2,1,0:T(8,128)(2,1)S(1)}, bf16[2,6,2,256,128]{4,3,2,1,0:T(8,128)(2,1)S(1)}, u32[]{:S(2)}, u32[]{:S(2)}) collective-permute-start(bf16[2,6,2,256,128]{4,3,2,1,0:T(8,128)(2,1)S(1)} %get-tuple-element.29), channel_id=1, source_target_pairs={{1,2},{3,4},{5,6},{7,8},{9,10},{11,12},{13,14},{15,16},{17,18},{19... | collective-permute-start | bytes 4718600 | tf_op jit(solution)/shard_map/ppermute | solution.py:362
  4.1 2.1 %collective-permute-start.1 = (bf16[2,6,2,256,128]{4,3,2,1,0:T(8,128)(2,1)S(1)}, bf16[2,6,2,256,128]{4,3,2,1,0:T(8,128)(2,1)S(1)}, u32[]{:S(2)}, u32[]{:S(2)}) collective-permute-start(bf16[2,6,2,256,128]{4,3,2,1,0:T(8,128)(2,1)S(1)} %get-tuple-element.30), channel_id=1, source_target_pairs={{0,1},{2,3},{4,5},{6,7},{8,9},{10,11},{12,13},{14,15},{16,17},{18,... | collective-permute-start | bytes 4718600 | tf_op jit(solution)/shard_map/ppermute | solution.py:363
  6.2 1.9 %collective-permute-start.2 = (bf16[2,2,256,128]{3,2,1,0:T(8,128)(2,1)S(1)}, bf16[2,2,256,128]{3,2,1,0:T(8,128)(2,1)S(1)}, u32[]{:S(2)}, u32[]{:S(2)}) collective-permute-start(bf16[2,2,256,128]{3,2,1,0:T(8,128)(2,1)S(1)} %get-tuple-element.33), channel_id=1, source_target_pairs={{1,2},{3,4},{5,6},{7,8},{9,10},{11,12},{13,14},{15,16},{17,18},{19... | collective-permute-start | bytes 786440 | tf_op jit(solution)/shard_map/ppermute | solution.py:361
  8.2 0.7 copy-done.5
  8.9 11.0 %inner_rows.1 = (f32[512,512]{1,0:T(8,128)S(1)}, bf16[2,4,32,512]{3,2,1,0:T(8,128)(2,1)S(1)}, bf16[2,4,32,512]{3,2,1,0:T(8,128)(2,1)S(1)}, bf16[2,4,32,512]{3,2,...) custom-call(bf16[6,8,256,128]{3,2,1,0:T(8,128)(2,1)S(1)} %copy-done, bf16[6,8,256,128]{3,2,1,0:T(8,128)(2,1)S(1)} %copy-done.1, ...), custom_call_target="tpu_custom_call" | custom-call | flops 25769803776 | bytes 33554432 | tf_op jit(solution)/shard_map/inner_rows/pallas_call | solution.py:371
  19.9 1.7 %collective-permute-start.3 = (bf16[2,4,32,512]{3,2,1,0:T(8,128)(2,1)S(1)}, bf16[2,4,32,512]{3,2,1,0:T(8,128)(2,1)S(1)}, u32[]{:S(2)}, u32[]{:S(2)}) collective-permute-start(bf16[2,4,32,512]{3,2,1,0:T(8,128)(2,1)S(1)} %get-tuple-element.37), channel_id=1, source_target_pairs={{0,64},{32,96},{64,128},{96,160},{128,192},{160,224},{192,0},{224,... | collective-permute-start | bytes 786440 | tf_op jit(solution)/shard_map/ppermute | solution.py:382
  21.6 2.9 %collective-permute-start.4 = (bf16[2,4,32,512]{3,2,1,0:T(8,128)(2,1)S(1)}, bf16[2,4,32,512]{3,2,1,0:T(8,128)(2,1)S(1)}, u32[]{:S(2)}, u32[]{:S(2)}) collective-permute-start(bf16[2,4,32,512]{3,2,1,0:T(8,128)(2,1)S(1)} %get-tuple-element.38), channel_id=1, source_target_pairs={{0,128},{32,160},{64,192},{96,224},{128,0},{160,32},{192,64},{224,... | collective-permute-start | bytes 786440 | tf_op jit(solution)/shard_map/ppermute | solution.py:382
  24.5 1.3 %collective-permute-start.5 = (bf16[2,4,32,512]{3,2,1,0:T(8,128)(2,1)S(1)}, bf16[2,4,32,512]{3,2,1,0:T(8,128)(2,1)S(1)}, u32[]{:S(2)}, u32[]{:S(2)}) collective-permute-start(bf16[2,4,32,512]{3,2,1,0:T(8,128)(2,1)S(1)} %get-tuple-element.39), channel_id=1, source_target_pairs={{0,192},{32,224},{64,0},{96,32},{128,64},{160,96},{192,128},{224,1... | collective-permute-start | bytes 786440 | tf_op jit(solution)/shard_map/ppermute | solution.py:382
  25.8 5.7 %near_rows.1 = (f32[512,512]{1,0:T(8,128)S(1)}, bf16[2,2,32,512]{3,2,1,0:T(8,128)(2,1)S(1)}, bf16[2,2,32,512]{3,2,1,0:T(8,128)(2,1)S(1)}, bf16[2,2,32,512]{3,2,1,0:T(8,128)(2,1)S(1)}, bf16[2,2,32,512]{3,2,1,0:T(8,128)(2,1)S(1)}) custom-call(bf16[6,8,256,128]{3,2,1,0:T(8,128)(2,1)S(1)} %copy-done, bf16[6,8,256,128]{3,2,1,0:T(8,128)(2,1)S(1)} %copy-done.1, ...), custom_call_target="tpu_custom_call" | custom-call | flops 12884901888 | bytes 33554432 | tf_op jit(solution)/shard_map/near_rows/pallas_call | solution.py:384
  31.5 14.9 %collective-permute-done.2.far_sums_ref = bf16[2,2,256,128]{3,2,1,0:T(8,128)(2,1)S(1)} collective-permute-done((bf16[2,2,256,128]{3,2,1,0:T(8,128)(2,1)S(1)}, bf16[2,2,256,128]{3,2,1,0:T(8,128)(2,1)S(1)}, u32[]{:S(2)}, u32[]{:S(2)}) %collective-permute-start.2) | collective-permute-done | bytes 262176 | tf_op jit(solution)/shard_map/ppermute | solution.py:361
  46.4 2.3 %collective-permute-start.6 = (bf16[2,2,32,512]{3,2,1,0:T(8,128)(2,1)S(1)}, bf16[2,2,32,512]{3,2,1,0:T(8,128)(2,1)S(1)}, u32[]{:S(2)}, u32[]{:S(2)}) collective-permute-start(bf16[2,2,32,512]{3,2,1,0:T(8,128)(2,1)S(1)} %get-tuple-element.40), channel_id=1, source_target_pairs={{0,64},{32,96},{64,128},{96,160},{128,192},{160,224},{192,0},{224,... | collective-permute-start | bytes 393224 | tf_op jit(solution)/shard_map/ppermute | solution.py:396
  48.7 2.3 %collective-permute-start.7 = (bf16[2,2,32,512]{3,2,1,0:T(8,128)(2,1)S(1)}, bf16[2,2,32,512]{3,2,1,0:T(8,128)(2,1)S(1)}, u32[]{:S(2)}, u32[]{:S(2)}) collective-permute-start(bf16[2,2,32,512]{3,2,1,0:T(8,128)(2,1)S(1)} %get-tuple-element.41), channel_id=1, source_target_pairs={{0,128},{32,160},{64,192},{96,224},{128,0},{160,32},{192,64},{224,... | collective-permute-start | bytes 393224 | tf_op jit(solution)/shard_map/ppermute | solution.py:396
  51.0 2.1 %collective-permute-start.8 = (bf16[2,2,32,512]{3,2,1,0:T(8,128)(2,1)S(1)}, bf16[2,2,32,512]{3,2,1,0:T(8,128)(2,1)S(1)}, u32[]{:S(2)}, u32[]{:S(2)}) collective-permute-start(bf16[2,2,32,512]{3,2,1,0:T(8,128)(2,1)S(1)} %get-tuple-element.42), channel_id=1, source_target_pairs={{0,192},{32,224},{64,0},{96,32},{128,64},{160,96},{192,128},{224,1... | collective-permute-start | bytes 393224 | tf_op jit(solution)/shard_map/ppermute | solution.py:396
  53.1 2.2 %far_means.1 = (bf16[8,2,32,512]{3,2,1,0:T(8,128)(2,1)S(1)}, bf16[2,2,32,512]{3,2,1,0:T(8,128)(2,1)S(1)}, bf16[2,2,32,512]{3,2,1,0:T(8,128)(2,1)S(1)}, bf16[2,2,...) custom-call(bf16[6,8,256,128]{3,2,1,0:T(8,128)(2,1)S(1)} %copy-done, bf16[6,8,256,128]{3,2,1,0:T(8,128)(2,1)S(1)} %copy-done.1, ...), custom_call_target="tpu_custom_call" | custom-call | flops 12884901888 | bytes 33554432 | tf_op jit(solution)/shard_map/far_means/pallas_call | solution.py:398
  55.4 1.4 %collective-permute-start.10 = (bf16[2,2,32,512]{3,2,1,0:T(8,128)(2,1)S(1)}, bf16[2,2,32,512]{3,2,1,0:T(8,128)(2,1)S(1)}, u32[]{:S(2)}, u32[]{:S(2)}) collective-permute-start(bf16[2,2,32,512]{3,2,1,0:T(8,128)(2,1)S(1)} %get-tuple-element.46), channel_id=1, source_target_pairs={{0,128},{32,160},{64,192},{96,224},{128,0},{160,32},{192,64},{224,... | collective-permute-start | bytes 393224 | tf_op jit(solution)/shard_map/ppermute | solution.py:410
  56.8 1.9 %collective-permute-start.11 = (bf16[2,2,32,512]{3,2,1,0:T(8,128)(2,1)S(1)}, bf16[2,2,32,512]{3,2,1,0:T(8,128)(2,1)S(1)}, u32[]{:S(2)}, u32[]{:S(2)}) collective-permute-start(bf16[2,2,32,512]{3,2,1,0:T(8,128)(2,1)S(1)} %get-tuple-element.47), channel_id=1, source_target_pairs={{0,192},{32,224},{64,0},{96,32},{128,64},{160,96},{192,128},{224,1... | collective-permute-start | bytes 393224 | tf_op jit(solution)/shard_map/ppermute | solution.py:410
  58.7 1.0 %between.2 = (f32[512,512]{1,0:T(8,128)S(1)}, bf16[6,32,512]{2,1,0:T(8,128)(2,1)S(1)}, bf16[6,32,512]{2,1,0:T(8,128)(2,1)S(1)}) custom-call(f32[512,512]{1,0:T(8,128)S(1)} %get-tuple-element.35.g_in_ref, bf16[2,4,32,512]{3,2,1,0:T(8,128)(2,1)S(1)} %get-tuple-element.36.rest_0_, bf16[2,4,32,512]{3,2,1,0:T(8,128)(2,1)S(1)} %collective-permute-done.3.rest_1_, ...), custom_call_target="tpu_custom_call" | custom-call | flops 536870912 | bytes 3145728 | tf_op jit(solution)/shard_map/between/pallas_call | solution.py:416
  59.7 3.8 %collective-permute-start.12 = (bf16[6,32,512]{2,1,0:T(8,128)(2,1)S(1)}, bf16[6,32,512]{2,1,0:T(8,128)(2,1)S(1)}, u32[]{:S(2)}, u32[]{:S(2)}) collective-permute-start(bf16[6,32,512]{2,1,0:T(8,128)(2,1)S(1)} %get-tuple-element.50), channel_id=1, source_target_pairs={{0,32},{32,0},{64,96},{96,64},{128,160},{160,128},{192,224},{224,1... | collective-permute-start | bytes 589832 | tf_op jit(solution)/shard_map/ppermute | solution.py:425
  63.6 4.1 %collective-permute-done.11.rest_3_ = bf16[2,2,32,512]{3,2,1,0:T(8,128)(2,1)S(1)} collective-permute-done((bf16[2,2,32,512]{3,2,1,0:T(8,128)(2,1)S(1)}, bf16[2,2,32,512]{3,2,1,0:T(8,128)(2,1)S(1)}, u32[]{:S(2)}, u32[]{:S(2)}) %collective-permute-start.11) | collective-permute-done | bytes 131104 | tf_op jit(solution)/shard_map/ppermute | solution.py:410
  68.2 5.5 %collective-permute-start.13 = (bf16[2,32,512]{2,1,0:T(8,128)(2,1)S(1)}, bf16[2,32,512]{2,1,0:T(8,128)(2,1)S(1)}, u32[]{:S(2)}, u32[]{:S(2)}) collective-permute-start(bf16[2,32,512]{2,1,0:T(8,128)(2,1)S(1)} %get-tuple-element.52), channel_id=1, source_target_pairs={{0,32},{32,0},{64,96},{96,64},{128,160},{160,128},{192,224},{224,1... | collective-permute-start | bytes 196616 | tf_op jit(solution)/shard_map/ppermute | solution.py:425
  73.6 4.1 %far_rows.1.g_in_ref = f32[512,512]{1,0:T(8,128)S(1)} custom-call(bf16[6,8,256,128]{3,2,1,0:T(8,128)(2,1)S(1)} %copy-done, bf16[6,8,256,128]{3,2,1,0:T(8,128)(2,1)S(1)} %copy-done.1, bf16[6,8,256,128]{3,2,1,0:T(8,128)(2,1)S(1)} %copy-done.2, bf16[6,8,256,128]{3,2,1,0:T(8,128)(2,1)S(1)} %copy-done.3, ...), custom_call_target="tpu_custom_call" | custom-call | flops 12884901888 | bytes 33554432 | tf_op jit(solution)/shard_map/far_rows/pallas_call | solution.py:427
  78.1 16.1 %all_to_all.5 = f32[8,64,512]{2,1,0:T(8,128)S(1)} all-to-all(f32[8,64,512]{2,1,0:T(8,128)S(1)} %bitcast.5), channel_id=1, replica_groups=mesh['member'=8,'space'=32] {'member'}, dimensions={0} | all-to-all | bytes 2097152 | tf_op jit(solution)/shard_map/all_to_all | solution.py:448
  94.3 0.7 multiply_bitcast_fusion
  (32 shorter events, 1.1 us)
Async XLA Ops:
  0.0 8.2 %copy-start = (bf16[6,8,256,128]{3,2,1,0:T(8,128)(2,1)S(1)}, bf16[6,8,256,128]{3,2,1,0:T(8,128)(2,1)}, u32[]{:S(2)}) copy-start(bf16[6,8,256,128]{3,2,1,0:T(8,128)(2,1)} %u_hbm.9) | copy-start | bytes 9437188
  0.0 8.2 %copy-start.1 = (bf16[6,8,256,128]{3,2,1,0:T(8,128)(2,1)S(1)}, bf16[6,8,256,128]{3,2,1,0:T(8,128)(2,1)}, u32[]{:S(2)}) copy-start(bf16[6,8,256,128]{3,2,1,0:T(8,128)(2,1)} %v_hbm.9) | copy-start | bytes 9437188
  0.0 8.1 %copy-start.6 = (f32[128]{0:T(128)S(1)}, f32[128]{0:T(128)}, u32[]{:S(2)}) copy-start(f32[128]{0:T(128)} %param.15) | copy-start | bytes 1540
  0.0 8.1 %copy-start.7 = (f32[128]{0:T(128)S(1)}, f32[128]{0:T(128)}, u32[]{:S(2)}) copy-start(f32[128]{0:T(128)} %param.14) | copy-start | bytes 1540
  0.0 8.2 %copy-start.4 = (f32[8,256]{1,0:T(8,128)S(1)}, f32[8,256]{1,0:T(8,128)}, u32[]{:S(2)}) copy-start(f32[8,256]{1,0:T(8,128)} %psi_ref.7) | copy-start | bytes 24580
  2.1 71.6 %collective-permute-start = (bf16[2,6,2,256,128]{4,3,2,1,0:T(8,128)(2,1)S(1)}, bf16[2,6,2,256,128]{4,3,2,1,0:T(8,128)(2,1)S(1)}, u32[]{:S(2)}, u32[]{:S(2)}) collective-permute-start(bf16[2,6,2,256,128]{4,3,2,1,0:T(8,128)(2,1)S(1)} %get-tuple-element.29), channel_id=1, source_target_pairs={{1,2},{3,4},{5,6},{7,8},{9,10},{11,12},{13,14},{15,16},{17,18},{19... | collective-permute-start | bytes 4718600 | tf_op jit(solution)/shard_map/ppermute | solution.py:362
  4.1 20.3 %collective-permute-start.1 = (bf16[2,6,2,256,128]{4,3,2,1,0:T(8,128)(2,1)S(1)}, bf16[2,6,2,256,128]{4,3,2,1,0:T(8,128)(2,1)S(1)}, u32[]{:S(2)}, u32[]{:S(2)}) collective-permute-start(bf16[2,6,2,256,128]{4,3,2,1,0:T(8,128)(2,1)S(1)} %get-tuple-element.30), channel_id=1, source_target_pairs={{0,1},{2,3},{4,5},{6,7},{8,9},{10,11},{12,13},{14,15},{16,17},{18,... | collective-permute-start | bytes 4718600 | tf_op jit(solution)/shard_map/ppermute | solution.py:363
  6.2 40.2 %collective-permute-start.2 = (bf16[2,2,256,128]{3,2,1,0:T(8,128)(2,1)S(1)}, bf16[2,2,256,128]{3,2,1,0:T(8,128)(2,1)S(1)}, u32[]{:S(2)}, u32[]{:S(2)}) collective-permute-start(bf16[2,2,256,128]{3,2,1,0:T(8,128)(2,1)S(1)} %get-tuple-element.33), channel_id=1, source_target_pairs={{1,2},{3,4},{5,6},{7,8},{9,10},{11,12},{13,14},{15,16},{17,18},{19... | collective-permute-start | bytes 786440 | tf_op jit(solution)/shard_map/ppermute | solution.py:361
  8.2 0.7 copy-start.5
  8.9 16.9 %copy-start.2 = (bf16[6,8,256,128]{3,2,1,0:T(8,128)(2,1)S(1)}, bf16[6,8,256,128]{3,2,1,0:T(8,128)(2,1)}, u32[]{:S(2)}) copy-start(bf16[6,8,256,128]{3,2,1,0:T(8,128)(2,1)} %h_hbm.7) | copy-start | bytes 9437188
  8.9 16.9 %copy-start.3 = (bf16[6,8,256,128]{3,2,1,0:T(8,128)(2,1)S(1)}, bf16[6,8,256,128]{3,2,1,0:T(8,128)(2,1)}, u32[]{:S(2)}) copy-start(bf16[6,8,256,128]{3,2,1,0:T(8,128)(2,1)} %q_hbm.7) | copy-start | bytes 9437188
  19.9 28.8 %collective-permute-start.3 = (bf16[2,4,32,512]{3,2,1,0:T(8,128)(2,1)S(1)}, bf16[2,4,32,512]{3,2,1,0:T(8,128)(2,1)S(1)}, u32[]{:S(2)}, u32[]{:S(2)}) collective-permute-start(bf16[2,4,32,512]{3,2,1,0:T(8,128)(2,1)S(1)} %get-tuple-element.37), channel_id=1, source_target_pairs={{0,64},{32,96},{64,128},{96,160},{128,192},{160,224},{192,0},{224,... | collective-permute-start | bytes 786440 | tf_op jit(solution)/shard_map/ppermute | solution.py:382
  21.6 29.4 %collective-permute-start.4 = (bf16[2,4,32,512]{3,2,1,0:T(8,128)(2,1)S(1)}, bf16[2,4,32,512]{3,2,1,0:T(8,128)(2,1)S(1)}, u32[]{:S(2)}, u32[]{:S(2)}) collective-permute-start(bf16[2,4,32,512]{3,2,1,0:T(8,128)(2,1)S(1)} %get-tuple-element.38), channel_id=1, source_target_pairs={{0,128},{32,160},{64,192},{96,224},{128,0},{160,32},{192,64},{224,... | collective-permute-start | bytes 786440 | tf_op jit(solution)/shard_map/ppermute | solution.py:382
  24.5 30.8 %collective-permute-start.5 = (bf16[2,4,32,512]{3,2,1,0:T(8,128)(2,1)S(1)}, bf16[2,4,32,512]{3,2,1,0:T(8,128)(2,1)S(1)}, u32[]{:S(2)}, u32[]{:S(2)}) collective-permute-start(bf16[2,4,32,512]{3,2,1,0:T(8,128)(2,1)S(1)} %get-tuple-element.39), channel_id=1, source_target_pairs={{0,192},{32,224},{64,0},{96,32},{128,64},{160,96},{192,128},{224,1... | collective-permute-start | bytes 786440 | tf_op jit(solution)/shard_map/ppermute | solution.py:382
  46.4 8.9 %collective-permute-start.6 = (bf16[2,2,32,512]{3,2,1,0:T(8,128)(2,1)S(1)}, bf16[2,2,32,512]{3,2,1,0:T(8,128)(2,1)S(1)}, u32[]{:S(2)}, u32[]{:S(2)}) collective-permute-start(bf16[2,2,32,512]{3,2,1,0:T(8,128)(2,1)S(1)} %get-tuple-element.40), channel_id=1, source_target_pairs={{0,64},{32,96},{64,128},{96,160},{128,192},{160,224},{192,0},{224,... | collective-permute-start | bytes 393224 | tf_op jit(solution)/shard_map/ppermute | solution.py:396
  48.7 8.1 %collective-permute-start.7 = (bf16[2,2,32,512]{3,2,1,0:T(8,128)(2,1)S(1)}, bf16[2,2,32,512]{3,2,1,0:T(8,128)(2,1)S(1)}, u32[]{:S(2)}, u32[]{:S(2)}) collective-permute-start(bf16[2,2,32,512]{3,2,1,0:T(8,128)(2,1)S(1)} %get-tuple-element.41), channel_id=1, source_target_pairs={{0,128},{32,160},{64,192},{96,224},{128,0},{160,32},{192,64},{224,... | collective-permute-start | bytes 393224 | tf_op jit(solution)/shard_map/ppermute | solution.py:396
  51.0 7.7 %collective-permute-start.8 = (bf16[2,2,32,512]{3,2,1,0:T(8,128)(2,1)S(1)}, bf16[2,2,32,512]{3,2,1,0:T(8,128)(2,1)S(1)}, u32[]{:S(2)}, u32[]{:S(2)}) collective-permute-start(bf16[2,2,32,512]{3,2,1,0:T(8,128)(2,1)S(1)} %get-tuple-element.42), channel_id=1, source_target_pairs={{0,192},{32,224},{64,0},{96,32},{128,64},{160,96},{192,128},{224,1... | collective-permute-start | bytes 393224 | tf_op jit(solution)/shard_map/ppermute | solution.py:396
  55.3 8.3 %collective-permute-start.9 = (bf16[2,2,32,512]{3,2,1,0:T(8,128)(2,1)S(1)}, bf16[2,2,32,512]{3,2,1,0:T(8,128)(2,1)S(1)}, u32[]{:S(2)}, u32[]{:S(2)}) collective-permute-start(bf16[2,2,32,512]{3,2,1,0:T(8,128)(2,1)S(1)} %get-tuple-element.45), channel_id=1, source_target_pairs={{0,64},{32,96},{64,128},{96,160},{128,192},{160,224},{192,0},{224,... | collective-permute-start | bytes 393224 | tf_op jit(solution)/shard_map/ppermute | solution.py:410
  55.4 8.2 %collective-permute-start.10 = (bf16[2,2,32,512]{3,2,1,0:T(8,128)(2,1)S(1)}, bf16[2,2,32,512]{3,2,1,0:T(8,128)(2,1)S(1)}, u32[]{:S(2)}, u32[]{:S(2)}) collective-permute-start(bf16[2,2,32,512]{3,2,1,0:T(8,128)(2,1)S(1)} %get-tuple-element.46), channel_id=1, source_target_pairs={{0,128},{32,160},{64,192},{96,224},{128,0},{160,32},{192,64},{224,... | collective-permute-start | bytes 393224 | tf_op jit(solution)/shard_map/ppermute | solution.py:410
  56.8 10.8 %collective-permute-start.11 = (bf16[2,2,32,512]{3,2,1,0:T(8,128)(2,1)S(1)}, bf16[2,2,32,512]{3,2,1,0:T(8,128)(2,1)S(1)}, u32[]{:S(2)}, u32[]{:S(2)}) collective-permute-start(bf16[2,2,32,512]{3,2,1,0:T(8,128)(2,1)S(1)} %get-tuple-element.47), channel_id=1, source_target_pairs={{0,192},{32,224},{64,0},{96,32},{128,64},{160,96},{192,128},{224,1... | collective-permute-start | bytes 393224 | tf_op jit(solution)/shard_map/ppermute | solution.py:410
  59.7 18.0 %collective-permute-start.12 = (bf16[6,32,512]{2,1,0:T(8,128)(2,1)S(1)}, bf16[6,32,512]{2,1,0:T(8,128)(2,1)S(1)}, u32[]{:S(2)}, u32[]{:S(2)}) collective-permute-start(bf16[6,32,512]{2,1,0:T(8,128)(2,1)S(1)} %get-tuple-element.50), channel_id=1, source_target_pairs={{0,32},{32,0},{64,96},{96,64},{128,160},{160,128},{192,224},{224,1... | collective-permute-start | bytes 589832 | tf_op jit(solution)/shard_map/ppermute | solution.py:425
  68.2 9.6 %collective-permute-start.13 = (bf16[2,32,512]{2,1,0:T(8,128)(2,1)S(1)}, bf16[2,32,512]{2,1,0:T(8,128)(2,1)S(1)}, u32[]{:S(2)}, u32[]{:S(2)}) collective-permute-start(bf16[2,32,512]{2,1,0:T(8,128)(2,1)S(1)} %get-tuple-element.52), channel_id=1, source_target_pairs={{0,32},{32,0},{64,96},{96,64},{128,160},{160,128},{192,224},{224,1... | collective-permute-start | bytes 196616 | tf_op jit(solution)/shard_map/ppermute | solution.py:425
